TPU v7x, 32 devices: a whole 2x2x4 slice. The times are simulated.
32 devices in a mesh: dp: 8 (over y, x, core), mp: 4 (over z).
Axes of the slice: x: 2, y: 2, z: 4, core: 2. Of those that a mesh axis runs over, the one named last changes fastest.
Arguments:
- block_in: float32 [9216, 1024], P(('dp', 'mp')), may hold values from -6 to 6
- out_grad: float32 [9216, 1024], P(('dp', 'mp')), may hold values from -6 to 6
- segment_ids: int32 [9216], P('dp'), may hold values from 0 to 31, never falling along the last dimension, each value on 1 to 576 neighbouring positions
- w_qkv: bfloat16 [3, 1024, 1024], P(None, 'dp', 'mp')
- w_out: bfloat16 [1024, 1024], P('mp', 'dp'), may hold values from -0.75 to 0.75
- w_up: bfloat16 [1024, 4096], P('dp', 'mp'), may hold values from -0.1875 to 0.1875
- w_down: bfloat16 [4096, 1024], P('mp', 'dp'), may hold values from -0.25 to 0.25
- ln1_gain: float32 [1024], P(('dp', 'mp')), may hold values from 0.5 to 1.5
- ln1_bias: float32 [1024], P(('dp', 'mp')), may hold values from -3 to 3
- bias_qv: float32 [2, 1024], P(None, ('dp', 'mp')), may hold values from -3 to 3
- bias_out: float32 [1024], P(('dp', 'mp')), may hold values from -3 to 3
- ln2_gain: float32 [1024], P(('dp', 'mp')), may hold values from 0.5 to 1.5
- ln2_bias: float32 [1024], P(('dp', 'mp')), may hold values from -3 to 3
- bias_up: float32 [4096], P(('dp', 'mp')), may hold values from -3 to 3
- bias_down: float32 [1024], P(('dp', 'mp')), may hold values from -3 to 3
Outputs:
- block_out: float32 [9216, 1024], P(('dp', 'mp'))
- in_grad: float32 [9216, 1024], P(('dp', 'mp'))
- grad_w_qkv: float32 [3, 1024, 1024], P(None, 'dp', 'mp')
- grad_w_out: float32 [1024, 1024], P('mp', 'dp')
- grad_w_up: float32 [1024, 4096], P('dp', 'mp')
- grad_w_down: float32 [4096, 1024], P('mp', 'dp')
- grad_ln1_gain: float32 [1024], P(('dp', 'mp'))
- grad_ln1_bias: float32 [1024], P(('dp', 'mp'))
- grad_bias_qv: float32 [2, 1024], P(None, ('dp', 'mp'))
- grad_bias_out: float32 [1024], P(('dp', 'mp'))
- grad_ln2_gain: float32 [1024], P(('dp', 'mp'))
- grad_ln2_bias: float32 [1024], P(('dp', 'mp'))
- grad_bias_up: float32 [4096], P(('dp', 'mp'))
- grad_bias_down: float32 [1024], P(('dp', 'mp'))
Inputs may be any that keep to these rules, and one draw needn't show every extreme that they name: `segment_ids`: segment numbers never fall along the tokens; a segment spans 1 to 576 tokens.
All inputs are finite; a program needn't handle non-finite values.
Results may differ from a plain program's by a relative error of at most 0.011.
Values may be sent and summed in bfloat16 or wider, within the bound.
No kernel may reach another device: no remote copies, remote signals or barrier semaphores. Data moves between devices by JAX's collectives and lax.ppermute only.
A program may use at most 128 MiB of HBM per device.

v0:
```python
import jax
import jax.numpy as jnp
from jax import lax
from jax.sharding import PartitionSpec as P

H = 16
HD = 64
L = 1152
QB = 576


NORM_EPS = 1e-05
GELU_SCALE = 0.7978845608028654
GELU_CUBE = 0.044715


def gelu_value(pre_act):
    inner = jnp.tanh(GELU_SCALE * (pre_act + GELU_CUBE * pre_act * pre_act * pre_act))
    return 0.5 * pre_act * (1.0 + inner)


def gelu_slope(pre_act):
    inner = jnp.tanh(GELU_SCALE * (pre_act + GELU_CUBE * pre_act * pre_act * pre_act))
    return 0.5 * (1.0 + inner) + 0.5 * pre_act * (1.0 - inner * inner) * GELU_SCALE * (
        1.0 + 3.0 * GELU_CUBE * pre_act * pre_act
    )


def norm_rows(inputs):
    center = inputs - jnp.mean(inputs, axis=-1, keepdims=True)
    scale_inv = lax.rsqrt(jnp.mean(center * center, axis=-1, keepdims=True) + NORM_EPS)
    return (center * scale_inv, scale_inv)


def norm_back(norm_grad, x_hat, scale_inv, gain):
    scaled = norm_grad * gain
    return scale_inv * (
        scaled
        - jnp.mean(scaled, axis=-1, keepdims=True)
        - x_hat * jnp.mean(scaled * x_hat, axis=-1, keepdims=True)
    )


def cross_dot(left, right):
    return lax.dot_general(
        left, right, (((0,), (0,)), ((), ())), preferred_element_type=jnp.float32
    )


def trans_dot(left, right):
    return lax.dot_general(
        left, right, (((1,), (1,)), ((), ())), preferred_element_type=jnp.float32
    )


def to_heads(flat, n_heads):
    return flat.reshape(flat.shape[0], n_heads, HD).transpose(1, 0, 2)


def from_heads(stacked):
    return stacked.transpose(1, 0, 2).reshape(stacked.shape[1], -1)


def head_scores(query_blk, key_rows, head_slope, row_start, seg_rows, seg_all):
    raw_scores = trans_dot(query_blk, key_rows) * HD ** (-0.5)
    row_pos = row_start + jnp.arange(query_blk.shape[0], dtype=jnp.int32)
    col_pos = jnp.arange(key_rows.shape[0], dtype=jnp.int32)
    distance = (row_pos[:, None] - col_pos[None, :]).astype(jnp.float32)
    allowed = (col_pos[None, :] <= row_pos[:, None]) & (seg_rows[:, None] == seg_all[None, :])
    return jnp.where(allowed, raw_scores - head_slope * distance, -1e30)


def head_forward(query_rows, key_rows, value_rows, head_slope, seg_all):

    def one_block(block_id):
        row_start = block_id * QB
        query_blk = lax.dynamic_slice_in_dim(query_rows, row_start, QB, 0)
        seg_rows = lax.dynamic_slice_in_dim(seg_all, row_start, QB, 0)
        scores = head_scores(query_blk, key_rows, head_slope, row_start, seg_rows, seg_all)
        top_score = jnp.max(scores, axis=1, keepdims=True)
        log_total = top_score + jnp.log(jnp.sum(jnp.exp(scores - top_score), axis=1, keepdims=True))
        prob_rows = jnp.exp(scores - log_total).astype(jnp.bfloat16)
        attended = jnp.dot(prob_rows, value_rows, preferred_element_type=jnp.float32).astype(
            jnp.bfloat16
        )
        return (attended, log_total[:, 0])

    attended, log_total = lax.map(one_block, jnp.arange(L // QB, dtype=jnp.int32))
    return (attended.reshape(L, HD), log_total.reshape(L))


def head_backward(
    query_rows, key_rows, value_rows, attended, attended_grad, log_total, head_slope, seg_all
):
    delta_all = jnp.sum(attended.astype(jnp.float32) * attended_grad.astype(jnp.float32), axis=1)
    score_scale = HD ** (-0.5)

    def one_block(running, block_id):
        key_grad, value_grad = running
        row_start = block_id * QB
        query_blk = lax.dynamic_slice_in_dim(query_rows, row_start, QB, 0)
        grad_blk = lax.dynamic_slice_in_dim(attended_grad, row_start, QB, 0)
        total_blk = lax.dynamic_slice_in_dim(log_total, row_start, QB, 0)
        delta_blk = lax.dynamic_slice_in_dim(delta_all, row_start, QB, 0)
        seg_rows = lax.dynamic_slice_in_dim(seg_all, row_start, QB, 0)
        scores = head_scores(query_blk, key_rows, head_slope, row_start, seg_rows, seg_all)
        prob_full = jnp.exp(scores - total_blk[:, None])
        prob_rows = prob_full.astype(jnp.bfloat16)
        value_grad = value_grad + cross_dot(prob_rows, grad_blk)
        prob_grad = trans_dot(grad_blk, value_rows)
        score_grad = (prob_full * (prob_grad - delta_blk[:, None])).astype(jnp.bfloat16)
        query_grad = jnp.dot(score_grad, key_rows, preferred_element_type=jnp.float32) * score_scale
        key_grad = key_grad + cross_dot(score_grad, query_blk) * score_scale
        return ((key_grad, value_grad), query_grad)

    empty = jnp.zeros(key_rows.shape, jnp.float32)
    (key_grad, value_grad), query_grad = lax.scan(
        one_block, (empty, empty), jnp.arange(L // QB, dtype=jnp.int32)
    )
    return (query_grad.reshape(L, HD), key_grad, value_grad)


def local(
    block_in,
    out_grad,
    segment_ids,
    w_qkv,
    w_out,
    w_up,
    w_down,
    ln1_gain,
    ln1_bias,
    bias_qv,
    bias_out,
    ln2_gain,
    ln2_bias,
    bias_up,
    bias_down,
):
    model_index = lax.axis_index("mp")
    vectors = (
        lax.all_gather(ln1_gain, ("dp", "mp"), axis=0, tiled=True),
        lax.all_gather(ln1_bias, ("dp", "mp"), axis=0, tiled=True),
        lax.all_gather(bias_qv, ("dp", "mp"), axis=1, tiled=True),
        lax.all_gather(bias_out, ("dp", "mp"), axis=0, tiled=True),
        lax.all_gather(ln2_gain, ("dp", "mp"), axis=0, tiled=True),
        lax.all_gather(ln2_bias, ("dp", "mp"), axis=0, tiled=True),
        lax.all_gather(bias_up, ("dp", "mp"), axis=0, tiled=True),
        lax.all_gather(bias_down, ("dp", "mp"), axis=0, tiled=True),
    )
    gain_one, shift_one, qv_all, out_shift, gain_two, shift_two, up_all, down_shift = vectors
    weights = (
        lax.all_gather(w_qkv, "dp", axis=1, tiled=True),
        lax.all_gather(w_out, "dp", axis=1, tiled=True),
        lax.all_gather(w_up, "dp", axis=0, tiled=True),
        lax.all_gather(w_down, "dp", axis=1, tiled=True),
    )
    qkv_full, out_full, up_full, down_full = weights
    head_cols = qkv_full.shape[2]
    hid_cols = up_full.shape[1]
    n_heads = head_cols // HD
    qv_shift = lax.dynamic_slice_in_dim(qv_all, model_index * head_cols, head_cols, 1)
    up_shift = lax.dynamic_slice_in_dim(up_all, model_index * hid_cols, hid_cols, 0)
    head_number = model_index * n_heads + jnp.arange(n_heads, dtype=jnp.int32)
    slopes = jnp.exp2(-8.0 * (head_number + 1).astype(jnp.float32) / H)
    hat_one, inv_one = norm_rows(block_in)
    normed_one = (hat_one * gain_one + shift_one).astype(jnp.bfloat16)
    rows_one = lax.all_gather(normed_one, "mp", axis=0, tiled=True)
    query_heads = to_heads(
        (jnp.dot(rows_one, qkv_full[0], preferred_element_type=jnp.float32) + qv_shift[0]).astype(
            jnp.bfloat16
        ),
        n_heads,
    )
    key_heads = to_heads(
        jnp.dot(rows_one, qkv_full[1], preferred_element_type=jnp.float32).astype(jnp.bfloat16),
        n_heads,
    )
    value_heads = to_heads(
        (jnp.dot(rows_one, qkv_full[2], preferred_element_type=jnp.float32) + qv_shift[1]).astype(
            jnp.bfloat16
        ),
        n_heads,
    )

    def one_head(packed):
        return head_forward(packed[0], packed[1], packed[2], packed[3], segment_ids)

    attended_heads, total_heads = lax.map(one_head, (query_heads, key_heads, value_heads, slopes))
    attended = from_heads(attended_heads)
    attn_sum = lax.psum_scatter(
        jnp.dot(attended, out_full, preferred_element_type=jnp.float32),
        "mp",
        scatter_dimension=0,
        tiled=True,
    )
    resid = block_in + attn_sum + out_shift
    hat_two, inv_two = norm_rows(resid)
    normed_two = (hat_two * gain_two + shift_two).astype(jnp.bfloat16)
    rows_two = lax.all_gather(normed_two, "mp", axis=0, tiled=True)
    pre_act = jnp.dot(rows_two, up_full, preferred_element_type=jnp.float32) + up_shift
    hidden = gelu_value(pre_act).astype(jnp.bfloat16)
    block_out = (
        resid
        + lax.psum_scatter(
            jnp.dot(hidden, down_full, preferred_element_type=jnp.float32),
            "mp",
            scatter_dimension=0,
            tiled=True,
        )
        + down_shift
    )
    back_weights = (
        lax.all_gather(w_qkv, "dp", axis=1, tiled=True),
        lax.all_gather(w_out, "dp", axis=1, tiled=True),
        lax.all_gather(w_up, "dp", axis=0, tiled=True),
        lax.all_gather(w_down, "dp", axis=1, tiled=True),
    )
    qkv_back, out_back, up_back, down_back = back_weights
    grad_low = out_grad.astype(jnp.bfloat16)
    grad_rows = lax.all_gather(grad_low, "mp", axis=0, tiled=True)
    grad_down = cross_dot(hidden, grad_rows)
    pre_grad = trans_dot(grad_rows, down_back) * gelu_slope(pre_act)
    pre_low = pre_grad.astype(jnp.bfloat16)
    grad_up = cross_dot(rows_two, pre_low)
    two_grad = lax.psum_scatter(trans_dot(pre_low, up_back), "mp", scatter_dimension=0, tiled=True)
    resid_grad = out_grad + norm_back(two_grad, hat_two, inv_two, gain_two)
    resid_low = resid_grad.astype(jnp.bfloat16)
    resid_rows = lax.all_gather(resid_low, "mp", axis=0, tiled=True)
    grad_out = cross_dot(attended, resid_rows)
    attended_grad = to_heads(trans_dot(resid_rows, out_back).astype(jnp.bfloat16), n_heads)

    def back_head(packed):
        return head_backward(
            packed[0], packed[1], packed[2], packed[3], packed[4], packed[5], packed[6], segment_ids
        )

    query_grad, key_grad, value_grad = lax.map(
        back_head,
        (query_heads, key_heads, value_heads, attended_heads, attended_grad, total_heads, slopes),
    )
    query_flat = from_heads(query_grad)
    key_flat = from_heads(key_grad)
    value_flat = from_heads(value_grad)
    query_low = query_flat.astype(jnp.bfloat16)
    key_low = key_flat.astype(jnp.bfloat16)
    value_low = value_flat.astype(jnp.bfloat16)
    grad_qkv = jnp.stack(
        [
            cross_dot(rows_one, query_low),
            cross_dot(rows_one, key_low),
            cross_dot(rows_one, value_low),
        ]
    )
    total = trans_dot(query_low, qkv_back[0])
    total = total + trans_dot(key_low, qkv_back[1])
    one_grad = lax.psum_scatter(
        total + trans_dot(value_low, qkv_back[2]), "mp", scatter_dimension=0, tiled=True
    )
    in_grad = resid_grad + norm_back(one_grad, hat_one, inv_one, gain_one)
    qkv_share, out_share, up_share, down_share = (
        lax.psum_scatter(grad_qkv, "dp", scatter_dimension=1, tiled=True),
        lax.psum_scatter(grad_out, "dp", scatter_dimension=1, tiled=True),
        lax.psum_scatter(grad_up, "dp", scatter_dimension=0, tiled=True),
        lax.psum_scatter(grad_down, "dp", scatter_dimension=1, tiled=True),
    )
    qv_part = jnp.stack([jnp.sum(query_flat, axis=0), jnp.sum(value_flat, axis=0)])
    qv_place = lax.dynamic_update_slice_in_dim(
        jnp.zeros(qv_all.shape, jnp.float32), qv_part, model_index * head_cols, 1
    )
    up_place = lax.dynamic_update_slice_in_dim(
        jnp.zeros(up_all.shape, jnp.float32), jnp.sum(pre_grad, axis=0), model_index * hid_cols, 0
    )
    vector_shares = (
        lax.psum_scatter(
            jnp.sum(one_grad * hat_one, axis=0), ("dp", "mp"), scatter_dimension=0, tiled=True
        ),
        lax.psum_scatter(jnp.sum(one_grad, axis=0), ("dp", "mp"), scatter_dimension=0, tiled=True),
        lax.psum_scatter(qv_place, ("dp", "mp"), scatter_dimension=1, tiled=True),
        lax.psum_scatter(
            jnp.sum(resid_grad, axis=0), ("dp", "mp"), scatter_dimension=0, tiled=True
        ),
        lax.psum_scatter(
            jnp.sum(two_grad * hat_two, axis=0), ("dp", "mp"), scatter_dimension=0, tiled=True
        ),
        lax.psum_scatter(jnp.sum(two_grad, axis=0), ("dp", "mp"), scatter_dimension=0, tiled=True),
        lax.psum_scatter(up_place, ("dp", "mp"), scatter_dimension=0, tiled=True),
        lax.psum_scatter(jnp.sum(out_grad, axis=0), ("dp", "mp"), scatter_dimension=0, tiled=True),
    )
    return (
        block_out,
        in_grad,
        qkv_share,
        out_share,
        up_share,
        down_share,
        vector_shares[0],
        vector_shares[1],
        vector_shares[2],
        vector_shares[3],
        vector_shares[4],
        vector_shares[5],
        vector_shares[6],
        vector_shares[7],
    )


def solution(mesh):
    return jax.shard_map(
        local,
        mesh=mesh,
        in_specs=(
            P(("dp", "mp"), None),
            P(("dp", "mp"), None),
            P("dp"),
            P(None, "dp", "mp"),
            P("mp", "dp"),
            P("dp", "mp"),
            P("mp", "dp"),
            P(("dp", "mp")),
            P(("dp", "mp")),
            P(None, ("dp", "mp")),
            P(("dp", "mp")),
            P(("dp", "mp")),
            P(("dp", "mp")),
            P(("dp", "mp")),
            P(("dp", "mp")),
        ),
        out_specs=(
            P(("dp", "mp"), None),
            P(("dp", "mp"), None),
            P(None, "dp", "mp"),
            P("mp", "dp"),
            P("dp", "mp"),
            P("mp", "dp"),
            P(("dp", "mp")),
            P(("dp", "mp")),
            P(None, ("dp", "mp")),
            P(("dp", "mp")),
            P(("dp", "mp")),
            P(("dp", "mp")),
            P(("dp", "mp")),
            P(("dp", "mp")),
        ),
        check_vma=False,
    )
```

profile of v0, /device:TPU:0, one launch (start us, length us, event | category | flops | bytes accessed | tf_op | source)
XLA Modules:
  0.0 1197.4 jit_solution(17655565238923358301)
XLA Ops:
  13.6 42.5 %all-reduce.14 = (f32[1024]{0:T(1024)S(1)}, f32[1024]{0:T(1024)S(1)}, f32[1024]{0:T(1024)S(1)}, f32[1024]{0:T(1024)S(1)}, f32[1024]{0:T(1024)S(1)}) all-reduce(f32[1024]{0:T(1024)S(1)} %dynamic-update-slice.1, f32[1024]{0:T(1024)S(1)} %dynamic-update-slice, f32[1024]{0:T(1024)S(1)} %dynamic-update-slice.2, ...), channel_id=1, replica_groups=mesh['dp'=8,'mp'=4] {'dp','mp'}, use_global_device_ids=true, to_apply=%add.1 | all-reduce | flops 5120 | bytes 40960
  58.9 68.2 %all-gather = f32[32,32,2]{1,2,0:T(2,128)S(1)} all-gather(f32[1,32,2]{1,2,0:T(2,128)S(1)} %bitcast.194), channel_id=1, replica_groups=mesh['dp'=8,'mp'=4] {'dp','mp'}, dimensions={0}, use_global_device_ids=true | all-gather | bytes 8448 | tf_op jit(solution)/shard_map/all_gather | solution.py:144
  127.3 10.7 all_gather.57
  149.5 47.8 %while.54 = (s32[]{:T(128)}, bf16[4,1152,64]{2,1,0:T(8,128)(2,1)}, f32[4,1152]{1,0:T(4,128)S(1)}, bf16[4,1152,64]{2,1,0:T(8,128)(2,1)S(1)}, bf16[4,1152,64]{2,1,...) while((s32[]{:T(128)}, bf16[4,1152,64]{2,1,0:T(8,128)(2,1)}, ...), condition=%wide.region_7.8_spmd, body=%wide.region_2.7_spmd.sunk | while | flops 179195904 | bytes 10473216 | solution.py:189
  151.2 9.2 while.57
  163.1 9.2 while.57
  175.1 9.2 while.57
  187.1 9.2 while.57
  204.1 82.5 %reduce-scatter.12.cloned.1.call-done = f32[288,1024]{1,0:T(8,128)} async-done(((f32[1152,1024]{1,0:T(8,128)}), f32[288,1024]{1,0:T(8,128)}) %reduce-scatter.12.cloned.1.call-update) | async-done | bytes 1179664 | tf_op jit(solution)/shard_map/reduce_scatter | solution.py:191
  292.5 69.3 %all-gather.1 = f32[32,1,128]{2,1,0:T(1,128)S(1)} all-gather(f32[1,1,128]{2,1,0:T(1,128)S(1)} %bitcast.197), channel_id=1, replica_groups=mesh['dp'=8,'mp'=4] {'dp','mp'}, dimensions={0}, use_global_device_ids=true | all-gather | bytes 16896 | tf_op jit(solution)/shard_map/all_gather | solution.py:148
  368.3 7.0 convolution_add_fusion.3
  375.3 43.1 %all-gather.20.cloned.1.call-done = bf16[1152,1024]{1,0:T(8,128)(2,1)} async-done(((bf16[288,1024]{1,0:T(8,128)(2,1)}), bf16[1152,1024]{1,0:T(8,128)(2,1)}) %all-gather.20.cloned.1.call-update) | async-done | bytes 2359312 | tf_op jit(solution)/shard_map/all_gather | solution.py:221
  418.4 28.8 %all-gather.18.cloned.1.call-done = bf16[1024,1024]{1,0:T(8,128)(2,1)} async-done(((bf16[1024,128]{1,0:T(8,128)(2,1)}), bf16[1024,1024]{1,0:T(8,128)(2,1)}) %all-gather.18.cloned.1.call-update) | async-done | bytes 2097168 | tf_op jit(solution)/shard_map/all_gather | solution.py:156
  447.2 8.8 fusion.49
  461.9 85.4 %reduce-scatter.16.cloned.1.call-done = f32[288,1024]{1,0:T(8,128)} async-done(((f32[1152,1024]{1,0:T(8,128)}), f32[288,1024]{1,0:T(8,128)}) %reduce-scatter.16.cloned.1.call-update) | async-done | bytes 1179664 | tf_op jit(solution)/shard_map/reduce_scatter | solution.py:226
  553.1 50.4 %all-gather.22.cloned.1.call-done = bf16[1152,1024]{1,0:T(8,128)(2,1)} async-done(((bf16[288,1024]{1,0:T(8,128)(2,1)}), bf16[1152,1024]{1,0:T(8,128)(2,1)}) %all-gather.22.cloned.1.call-update) | async-done | bytes 2359312 | tf_op jit(solution)/shard_map/all_gather | solution.py:229
  606.8 71.2 %while.56 = (s32[]{:T(128)}, f32[4,1152,64]{1,2,0:T(8,128)}, bf16[4,1152,64]{1,2,0:T(8,128)(2,1)}, f32[4,1152,64]{1,2,0:T(8,128)}, bf16[4,1152,64]{2,1,0:T(8,128...) while((s32[]{:T(128)}, f32[4,1152,64]{1,2,0:T(8,128)}, ...), condition=%wide.region_19.20_spmd, body=%wide.region_15.19_spmd.sunk | while | flops 434662848 | bytes 19240836 | solution.py:238
  611.7 10.9 while.58
  629.5 10.9 while.58
  647.3 10.9 while.58
  665.1 10.9 while.58
  687.5 8.2 fusion.43
  696.0 7.3 fusion.37
  703.3 8.4 fusion.42
  725.9 91.2 %reduce-scatter.28.cloned.1.call-done = f32[32,2]{1,0:T(8,128)} async-done(((f32[1024,2]{1,0:T(8,128)}), f32[32,2]{1,0:T(8,128)}) %reduce-scatter.28.cloned.1.call-update) | async-done | bytes 272
  818.5 83.0 %reduce-scatter.18.cloned.1.call-done = f32[288,1024]{1,0:T(8,128)} async-done(((f32[1152,1024]{1,0:T(8,128)}), f32[288,1024]{1,0:T(8,128)}) %reduce-scatter.18.cloned.1.call-update) | async-done | bytes 1179664 | tf_op jit(solution)/shard_map/reduce_scatter | solution.py:257
  903.9 45.6 %all-reduce.13 = (f32[1024]{0:T(1024)}, f32[1024]{0:T(1024)}, f32[1024]{0:T(1024)}, f32[1024]{0:T(1024)}, f32[1024]{0:T(1024)}, /*index=5*/f32[1024]{0:T(1024)}, f32[4096]{0:T(1024)}, f32[1024]{0:T(1024)}) all-reduce(f32[1024]{0:T(1024)} %copy-done.26, f32[1024]{0:T(1024)} %get-tuple-element.323, ...), channel_id=1, replica_groups=mesh['dp'=8,'mp'=4] {'dp','mp'}, use_global_device_ids=true, to_apply=%add.5 | all-reduce | flops 11264 | bytes 90112
  960.3 30.2 %reduce-scatter.14.cloned.1.call-done = f32[288,1024]{1,0:T(8,128)} async-done(((f32[1152,1024]{1,0:T(8,128)}), f32[288,1024]{1,0:T(8,128)}) %reduce-scatter.14.cloned.1.call-update) | async-done | bytes 1179664 | tf_op jit(solution)/shard_map/reduce_scatter | solution.py:205
  994.6 51.5 %reduce-scatter.24.cloned.1.call-done = f32[128,1024]{1,0:T(8,128)} async-done(((f32[1024,1024]{1,0:T(8,128)}), f32[128,1024]{1,0:T(8,128)}) %reduce-scatter.24.cloned.1.call-update) | async-done | bytes 524304 | tf_op jit(solution)/shard_map/reduce_scatter | solution.py:264
  1046.1 54.9 %reduce-scatter.26.cloned.1.call-done = f32[1024,128]{1,0:T(8,128)} async-done(((f32[1024,1024]{1,0:T(8,128)}), f32[1024,128]{1,0:T(8,128)}) %reduce-scatter.26.cloned.1.call-update) | async-done | bytes 524304 | tf_op jit(solution)/shard_map/reduce_scatter | solution.py:265
  1101.0 39.6 %reduce-scatter.22.cloned.1.call-done = f32[256,128]{1,0:T(8,128)} async-done(((f32[256,1024]{1,0:T(8,128)}), f32[256,128]{1,0:T(8,128)}) %reduce-scatter.22.cloned.1.call-update) | async-done | bytes 131088 | tf_op jit(solution)/shard_map/reduce_scatter | solution.py:263
  1140.6 49.9 %reduce-scatter.20.cloned.1.call-done = f32[3,128,256]{2,1,0:T(8,128)} async-done(((f32[3,1024,256]{2,1,0:T(8,128)}), f32[3,128,256]{2,1,0:T(8,128)}) %reduce-scatter.20.cloned.1.call-update) | async-done | bytes 393232 | tf_op jit(solution)/shard_map/reduce_scatter | solution.py:262
  (439 shorter events, 204.4 us)
Async XLA Ops:
  7.2 50.6 %copy-start = (f32[288,1024]{1,0:T(8,128)S(1)}, f32[288,1024]{1,0:T(8,128)}, u32[]{:S(2)}) copy-start(f32[288,1024]{1,0:T(8,128)} %param.23) | copy-start | bytes 3538948
  7.2 130.8 %all-gather.12.cloned.1.call-start = ((), (), s32[]{:S(2)}) async-start(), calls=%async_computation.10 | async-start | bytes 1769472 | tf_op jit(solution)/shard_map/all_gather | solution.py:153
  7.9 130.0 %all-gather.10.cloned.1.call-start = ((), (), s32[]{:S(2)}) async-start(), calls=%async_computation.9 | async-start | bytes 2949120 | tf_op jit(solution)/shard_map/all_gather | solution.py:168
  8.0 51.0 %copy-start.29 = (f32[2,32]{1,0:T(2,128)S(1)}, f32[2,32]{1,0:T(2,128)}, u32[]{:S(2)}) copy-start(f32[2,32]{1,0:T(2,128)} %param.32) | copy-start | bytes 772
  8.0 119.3 %copy-start.18 = (bf16[256,128]{1,0:T(8,128)(2,1)S(1)}, bf16[256,128]{1,0:T(8,128)(2,1)}, u32[]{:S(2)}) copy-start(bf16[256,128]{1,0:T(8,128)(2,1)} %param.27) | copy-start | bytes 196612
  56.2 84.5 %copy-start.21 = (f32[1024]{0:T(1024)}, f32[1024]{0:T(1024)S(1)}, u32[]{:S(2)}) copy-start(f32[1024]{0:T(1024)S(1)} %get-tuple-element.422) | copy-start | bytes 12292
  56.2 84.5 %copy-start.19 = (f32[288]{0:T(512)}, f32[288]{0:T(512)S(1)}, u32[]{:S(2)}) copy-start(f32[288]{0:T(512)S(1)} %broadcast_multiply_fusion.5) | copy-start | bytes 3460
  58.8 227.8 %reduce-scatter.12.cloned.1.call-start = ((), (), s32[]{:S(2)}) async-start(), calls=%async_computation.11 | async-start | bytes 5898240 | tf_op jit(solution)/shard_map/reduce_scatter | solution.py:191
  203.5 158.2 %all-gather.16.cloned.1.call-start = ((), (), s32[]{:S(2)}) async-start(), calls=%async_computation.13 | async-start | bytes 2359296 | tf_op jit(solution)/shard_map/all_gather | solution.py:155
  204.1 164.2 %all-gather.14.cloned.1.call-start = ((), (), s32[]{:S(2)}) async-start(), calls=%async_computation.12 | async-start | bytes 2949120 | tf_op jit(solution)/shard_map/all_gather | solution.py:200
  288.2 261.6 %copy-start.2 = (f32[288,1024]{1,0:T(8,128)}, f32[288,1024]{1,0:T(8,128)S(1)}, u32[]{:S(2)}) copy-start(f32[288,1024]{1,0:T(8,128)S(1)} %get-tuple-element.429) | copy-start | bytes 3538948
  289.6 128.8 %all-gather.20.cloned.1.call-start = ((), (), s32[]{:S(2)}) async-start(), calls=%async_computation.16 | async-start | bytes 2949120 | tf_op jit(solution)/shard_map/all_gather | solution.py:221
  291.6 155.6 %all-gather.18.cloned.1.call-start = ((), (), s32[]{:S(2)}) async-start(), calls=%async_computation.14 | async-start | bytes 2359296 | tf_op jit(solution)/shard_map/all_gather | solution.py:156
  292.4 254.9 %reduce-scatter.16.cloned.1.call-start = ((), (), s32[]{:S(2)}) async-start(), calls=%async_computation.17 | async-start | bytes 5898240 | tf_op jit(solution)/shard_map/reduce_scatter | solution.py:226
  447.2 10.2 copy-start.32
  461.9 141.6 %all-gather.22.cloned.1.call-start = ((), (), s32[]{:S(2)}) async-start(), calls=%async_computation.18 | async-start | bytes 2949120 | tf_op jit(solution)/shard_map/all_gather | solution.py:229
  550.9 52.6 %copy-start.14 = (bf16[256,1024]{1,0:T(8,128)(2,1)S(1)}, bf16[256,1024]{1,0:T(8,128)(2,1)}, u32[]{:S(2)}) copy-start(bf16[256,1024]{1,0:T(8,128)(2,1)} %all_gather.57) | copy-start | bytes 1572868
  552.8 264.3 %reduce-scatter.28.cloned.1.call-start = ((), (), s32[]{:S(2)}) async-start(), calls=%async_computation.24 | async-start | bytes 540672
  682.3 219.1 %reduce-scatter.18.cloned.1.call-start = ((), (), s32[]{:S(2)}) async-start(), calls=%async_computation.19 | async-start | bytes 5898240 | tf_op jit(solution)/shard_map/reduce_scatter | solution.py:257
  687.5 303.0 %reduce-scatter.14.cloned.1.call-start = ((), (), s32[]{:S(2)}) async-start(), calls=%async_computation.15 | async-start | bytes 5898240 | tf_op jit(solution)/shard_map/reduce_scatter | solution.py:205
  695.7 350.4 %reduce-scatter.24.cloned.1.call-start = ((), (), s32[]{:S(2)}) async-start(), calls=%async_computation.22 | async-start | bytes 4718592 | tf_op jit(solution)/shard_map/reduce_scatter | solution.py:264
  703.3 397.7 %reduce-scatter.26.cloned.1.call-start = ((), (), s32[]{:S(2)}) async-start(), calls=%async_computation.23 | async-start | bytes 4718592 | tf_op jit(solution)/shard_map/reduce_scatter | solution.py:265
  711.8 428.8 %reduce-scatter.22.cloned.1.call-start = ((), (), s32[]{:S(2)}) async-start(), calls=%async_computation.21 | async-start | bytes 1179648 | tf_op jit(solution)/shard_map/reduce_scatter | solution.py:263
  716.4 474.1 %reduce-scatter.20.cloned.1.call-start = ((), (), s32[]{:S(2)}) async-start(), calls=%async_computation.20 | async-start | bytes 3538944 | tf_op jit(solution)/shard_map/reduce_scatter | solution.py:262
  723.0 178.4 %copy-start.1 = (f32[288,1024]{1,0:T(8,128)S(1)}, f32[288,1024]{1,0:T(8,128)}, u32[]{:S(2)}) copy-start(f32[288,1024]{1,0:T(8,128)} %param.23) | copy-start | bytes 3538948
  723.0 178.4 %copy-start.20 = (f32[288]{0:T(512)S(1)}, f32[288]{0:T(512)}, u32[]{:S(2)}) copy-start(f32[288]{0:T(512)} %copy-done.19) | copy-start | bytes 3460
  723.0 178.4 %copy-start.22 = (f32[1024]{0:T(1024)S(1)}, f32[1024]{0:T(1024)}, u32[]{:S(2)}) copy-start(f32[1024]{0:T(1024)} %copy-done.21) | copy-start | bytes 12292
  723.0 178.4 %copy-start.24 = (f32[288]{0:T(512)S(1)}, f32[288]{0:T(512)}, u32[]{:S(2)}) copy-start(f32[288]{0:T(512)} %copy-done.23) | copy-start | bytes 3460
  723.0 180.9 %copy-start.25 = (f32[1024]{0:T(1024)S(1)}, f32[1024]{0:T(1024)}, u32[]{:S(2)}) copy-start(f32[1024]{0:T(1024)} %get-tuple-element.436) | copy-start | bytes 12292
  723.1 267.4 %copy-start.3 = (f32[288,1024]{1,0:T(8,128)S(1)}, f32[288,1024]{1,0:T(8,128)}, u32[]{:S(2)}) copy-start(f32[288,1024]{1,0:T(8,128)} %copy-done.2) | copy-start | bytes 3538948
  723.8 177.6 %copy-start.26 = (f32[1024]{0:T(1024)}, f32[1024]{0:T(1024)S(1)}, u32[]{:S(2)}) copy-start(f32[1024]{0:T(1024)S(1)} %dynamic-update-slice.5) | copy-start | bytes 12292
  903.9 89.2 %copy-start.6 = (f32[288,1024]{1,0:T(8,128)S(1)}, f32[288,1024]{1,0:T(8,128)}, u32[]{:S(2)}) copy-start(f32[288,1024]{1,0:T(8,128)} %copy-done.5) | copy-start | bytes 3538948
  (19 other events, 44.2 us)
Sparse Core Ops, SparseCore 0:
  9.9 28.3 all-gather.11
  59.0 50.3 all-gather.9
  203.6 82.9 reduce-scatter.11
  288.3 28.2 all-gather.15
  318.1 50.1 all-gather.13
  369.7 48.7 all-gather.19
  420.3 26.8 all-gather.17
  462.0 85.2 reduce-scatter.15
  553.0 50.4 all-gather.21
  682.5 134.5 reduce-scatter.27
  819.4 81.9 reduce-scatter.17
  903.6 86.8 reduce-scatter.13
  994.4 51.6 reduce-scatter.23
  1049.9 51.0 reduce-scatter.25
  1104.6 35.9 reduce-scatter.21
  1144.4 46.0 reduce-scatter.19
where the time goes:
time: 1210 us; the launch traced here: 1200 us
  waiting for transfers between devices  699 us (58%)
  blocking collectives  236 us (20%)
  matrix products  123 us (10%)
  local copies, waits for them, and re-layouts  74.7 us (6%)
  other arithmetic  36.3 us (3%)
  between operations  14.9 us (1%)
    unnamed x17, waiting for transfers between devices  93.3 us
    unnamed x2, blocking collectives  88.2 us
    reduce_scatter x1, waiting for transfers between devices, local(): lax.psum_scatter(trans_dot(pre_low, up_back), 'mp', scatter_dimension=0,...  85.4 us
    reduce_scatter x1, waiting for transfers between devices, local(): lax.psum_scatter(total + trans_dot(value_low, qkv_back[2]), 'mp', scatter...  83 us
    reduce_scatter x1, waiting for transfers between devices, local(): lax.psum_scatter(jnp.dot(attended, out_full, preferred_element_type=jnp.f...  82.5 us
    all_gather x1, blocking collectives, local(): lax.all_gather(bias_up, ('dp', 'mp'), axis=0, tiled=True)  69.3 us
    all_gather x1, blocking collectives, local(): lax.all_gather(bias_qv, ('dp', 'mp'), axis=1, tiled=True)  68.2 us
    dot_general x30, matrix products, trans_dot(): lax.dot_general(left, right, (((1,), (1,)), ((), ())), preferred_element_...  56.4 us
  transfers between devices with their start and end apart: 16, of which 13 were waited for; matrix products, arithmetic and copies ran while one was open for 7% of the time, Pallas kernels for 0%

commit v1 on v0

v1 whole, which is shorter than its diff:
```python
import jax
import jax.numpy as jnp
from jax import lax
from jax.experimental import pallas as pl
from jax.experimental.pallas import tpu as pltpu
from jax.sharding import PartitionSpec as P

H = 16
HD = 64
L = 1152
BLK = 128
REACH = 5

NORM_EPS = 1e-05
GELU_SCALE = 0.7978845608028654
GELU_CUBE = 0.044715
BF = jnp.bfloat16
F32 = jnp.float32


def gelu_both(pre_act):
    inner = jnp.tanh(GELU_SCALE * (pre_act + GELU_CUBE * pre_act * pre_act * pre_act))
    value = 0.5 * pre_act * (1.0 + inner)
    slope = 0.5 * (1.0 + inner) + 0.5 * pre_act * (1.0 - inner * inner) * GELU_SCALE * (
        1.0 + 3.0 * GELU_CUBE * pre_act * pre_act
    )
    return value, slope


def norm_rows(inputs):
    center = inputs - jnp.mean(inputs, axis=-1, keepdims=True)
    scale_inv = lax.rsqrt(jnp.mean(center * center, axis=-1, keepdims=True) + NORM_EPS)
    return (center * scale_inv, scale_inv)


def norm_back(norm_grad, x_hat, scale_inv, gain):
    scaled = norm_grad * gain
    return scale_inv * (
        scaled
        - jnp.mean(scaled, axis=-1, keepdims=True)
        - x_hat * jnp.mean(scaled * x_hat, axis=-1, keepdims=True)
    )


def dot(left, right):
    return jnp.dot(left, right, preferred_element_type=F32)


def cross_dot(left, right):
    return lax.dot_general(left, right, (((0,), (0,)), ((), ())), preferred_element_type=F32)


def trans_dot(left, right):
    return lax.dot_general(left, right, (((1,), (1,)), ((), ())), preferred_element_type=F32)


def flip(x):
    return x.astype(F32).T


def load_rows(order_ref, src_ref, dst_ref, nb, rb):
    for k in range(nb):
        dst_ref[k * rb : (k + 1) * rb, :] = src_ref[order_ref[k]]


def half_masks(shape):
    lane = lax.broadcasted_iota(jnp.int32, shape, 1)
    return (lane < HD, lane >= HD)


def distances(b, segr_ref, segc_ref):
    w0 = max(0, b - REACH) * BLK
    w1 = (b + 1) * BLK
    keys = w0 + lax.broadcasted_iota(jnp.int32, (w1 - w0, BLK), 0)
    rows = b * BLK + lax.broadcasted_iota(jnp.int32, (w1 - w0, BLK), 1)
    same = segc_ref[w0:w1, :] == segr_ref[:, b * BLK : (b + 1) * BLK]
    gap = rows - keys
    dist = jnp.where(same & (gap >= 0), gap.astype(F32), 1e30)
    return w0, w1, dist


def attn_fwd_kernel(
    order_ref, slope_ref, segr_ref, segc_ref, q_ref, k_ref, v_ref, att_ref, lse_ref,
    q_s, k_s, v_s, vt_s, a_s, *, nb, rb,
):
    pair = pl.program_id(0)
    load_rows(order_ref, q_ref, q_s, nb, rb)
    load_rows(order_ref, k_ref, k_s, nb, rb)
    load_rows(order_ref, v_ref, v_s, nb, rb)
    vt_s[...] = flip(v_s[...]).astype(BF)
    halves = half_masks((BLK, 2 * HD))
    for b in range(L // BLK):
        r0 = b * BLK
        w0, w1, dist = distances(b, segr_ref, segc_ref)
        q_blk = q_s[r0 : r0 + BLK, :] * BF(HD ** (-0.5))
        outs = []
        for h in range(2):
            q_h = jnp.where(halves[h], q_blk, BF(0))
            s = trans_dot(k_s[w0:w1, :], q_h) - slope_ref[2 * pair + h] * dist
            top = jnp.max(s, axis=0, keepdims=True)
            e = jnp.exp(s - top)
            total = jnp.sum(e, axis=0, keepdims=True)
            lse_ref[0, h : h + 1, r0 : r0 + BLK] = top + jnp.log(total)
            prob = (e * (1.0 / total)).astype(BF)
            outs.append(dot(vt_s[h * HD : (h + 1) * HD, w0:w1], prob))
        a_s[r0 : r0 + BLK, :] = jnp.concatenate(outs, axis=0).T.astype(BF)
    for k in range(nb):
        att_ref[order_ref[k]] = a_s[k * rb : (k + 1) * rb, :]


def attn_bwd_kernel(
    order_ref, slope_ref, segr_ref, segc_ref, q_ref, k_ref, v_ref, att_ref, grad_ref, lse_ref,
    out_ref, sum_ref, q_s, k_s, v_s, kt_s, a_s, g_s, dq_s, dk_s, dv_s, *, nb, rb,
):
    pair = pl.program_id(0)
    load_rows(order_ref, q_ref, q_s, nb, rb)
    load_rows(order_ref, k_ref, k_s, nb, rb)
    load_rows(order_ref, v_ref, v_s, nb, rb)
    load_rows(order_ref, att_ref, a_s, nb, rb)
    load_rows(order_ref, grad_ref, g_s, nb, rb)
    kt_s[...] = flip(k_s[...]).astype(BF)
    dk_s[...] = jnp.zeros(dk_s.shape, F32)
    dv_s[...] = jnp.zeros(dv_s.shape, F32)
    halves = half_masks((BLK, 2 * HD))
    q_sum = jnp.zeros((1, 2 * HD), F32)
    for b in range(L // BLK):
        r0 = b * BLK
        w0, w1, dist = distances(b, segr_ref, segc_ref)
        q_blk = q_s[r0 : r0 + BLK, :] * BF(HD ** (-0.5))
        g_blk = g_s[r0 : r0 + BLK, :]
        prod = (a_s[r0 : r0 + BLK, :].astype(F32) * g_blk.astype(F32)).T
        probs, grads, q_hs, g_hs, dq_t = [], [], [], [], []
        for h in range(2):
            q_h = jnp.where(halves[h], q_blk, BF(0))
            g_h = jnp.where(halves[h], g_blk, BF(0))
            s = trans_dot(k_s[w0:w1, :], q_h) - slope_ref[2 * pair + h] * dist
            p = jnp.exp(s - lse_ref[0, h : h + 1, r0 : r0 + BLK])
            delta = jnp.sum(prod[h * HD : (h + 1) * HD, :], axis=0, keepdims=True)
            dp = trans_dot(v_s[w0:w1, :], g_h)
            ds = (p * (dp - delta)).astype(BF)
            dq_t.append(dot(kt_s[h * HD : (h + 1) * HD, w0:w1], ds))
            probs.append(p.astype(BF))
            grads.append(ds)
            q_hs.append(q_h)
            g_hs.append(g_h)
        dv_s[w0:w1, :] += dot(jnp.concatenate(probs, axis=1), jnp.concatenate(g_hs, axis=0))
        dk_s[w0:w1, :] += dot(jnp.concatenate(grads, axis=1), jnp.concatenate(q_hs, axis=0))
        dq = jnp.concatenate(dq_t, axis=0).T * HD ** (-0.5)
        q_sum = q_sum + jnp.sum(dq, axis=0, keepdims=True)
        dq_s[r0 : r0 + BLK, :] = dq.astype(BF)
    sum_ref[0, 0:1, :] = q_sum
    sum_ref[0, 1:2, :] = jnp.sum(dv_s[...], axis=0, keepdims=True)
    for k in range(nb):
        rows = slice(k * rb, (k + 1) * rb)
        out_ref[order_ref[k], :, 0 : 2 * HD] = dq_s[rows, :]
        out_ref[order_ref[k], :, 2 * HD : 4 * HD] = dk_s[rows, :].astype(BF)
        out_ref[order_ref[k], :, 4 * HD : 6 * HD] = dv_s[rows, :].astype(BF)


def attn_specs(nb, rb):
    smem = pl.BlockSpec(memory_space=pltpu.SMEM)
    col = lambda which: pl.BlockSpec((nb, rb, 2 * HD), lambda p: (0, 0, 3 * p + which))
    base = [
        smem,
        smem,
        pl.BlockSpec((1, L), lambda p: (0, 0)),
        pl.BlockSpec((L, 1), lambda p: (0, 0)),
        col(0),
        col(1),
        col(2),
    ]
    one = pl.BlockSpec((nb, rb, 2 * HD), lambda p: (0, 0, p))
    lse = pl.BlockSpec((1, 2, L), lambda p: (p, 0, 0))
    return base, one, lse


def attn_fwd(order, slopes, segs, qkv):
    nb, rb, cols = qkv.shape
    pairs = cols // (6 * HD)
    base, one, lse = attn_specs(nb, rb)
    rows = lambda: pltpu.VMEM((L, 2 * HD), BF)
    return pl.pallas_call(
        lambda *refs: attn_fwd_kernel(*refs, nb=nb, rb=rb),
        grid=(pairs,),
        in_specs=base,
        out_specs=[one, lse],
        out_shape=[
            jax.ShapeDtypeStruct((nb, rb, pairs * 2 * HD), BF),
            jax.ShapeDtypeStruct((pairs, 2, L), F32),
        ],
        scratch_shapes=[rows(), rows(), rows(), pltpu.VMEM((2 * HD, L), BF), rows()],
        name="attn_fwd",
    )(order, slopes, segs.reshape(1, L), segs.reshape(L, 1), qkv, qkv, qkv)


def attn_bwd(order, slopes, segs, qkv, att, att_grad, lse_rows):
    nb, rb, cols = qkv.shape
    pairs = cols // (6 * HD)
    base, one, lse = attn_specs(nb, rb)
    rows = lambda dt=BF: pltpu.VMEM((L, 2 * HD), dt)
    return pl.pallas_call(
        lambda *refs: attn_bwd_kernel(*refs, nb=nb, rb=rb),
        grid=(pairs,),
        in_specs=base + [one, one, lse],
        out_specs=[
            pl.BlockSpec((nb, rb, 6 * HD), lambda p: (0, 0, p)),
            pl.BlockSpec((1, 2, 2 * HD), lambda p: (p, 0, 0)),
        ],
        out_shape=[
            jax.ShapeDtypeStruct((nb, rb, cols), BF),
            jax.ShapeDtypeStruct((pairs, 2, 2 * HD), F32),
        ],
        scratch_shapes=[rows(), rows(), rows(), pltpu.VMEM((2 * HD, L), BF), rows(), rows(),
                        rows(), rows(F32), rows(F32)],
        name="attn_bwd",
    )(order, slopes, segs.reshape(1, L), segs.reshape(L, 1), qkv, qkv, qkv, att, att_grad, lse_rows)


def gather_vectors(vecs, n_dev):
    flat = jnp.concatenate([v.reshape(-1) for v in vecs])
    spread = jnp.broadcast_to(flat[None, :], (n_dev, flat.shape[0]))
    got = lax.all_to_all(spread, ("dp", "mp"), 0, 0, tiled=True)
    full, at = [], 0
    for v in vecs:
        n = v.size
        part = got[:, at : at + n]
        if v.ndim == 2:
            part = part.reshape(n_dev, v.shape[0], v.shape[1]).transpose(1, 0, 2)
            full.append(part.reshape(v.shape[0], -1))
        else:
            full.append(part.reshape(-1))
        at += n
    return full


def scatter_vectors(fulls, n_dev):
    parts, shapes = [], []
    for v in fulls:
        if v.ndim == 2:
            part = v.reshape(v.shape[0], n_dev, -1).transpose(1, 0, 2)
            shapes.append((v.shape[0], v.shape[1] // n_dev))
        else:
            part = v
            shapes.append((v.shape[0] // n_dev,))
        parts.append(part.reshape(n_dev, -1))
    got = lax.all_to_all(jnp.concatenate(parts, axis=1), ("dp", "mp"), 0, 0, tiled=True)
    flat = jnp.sum(got, axis=0)
    outs, at = [], 0
    for shape, part in zip(shapes, parts):
        n = part.shape[1]
        outs.append(flat[at : at + n].reshape(shape))
        at += n
    return outs


def head_slopes(numbers):
    return jnp.exp2(-8.0 * (numbers + 1).astype(F32) / H)


def pair_columns(parts):
    stacked = jnp.stack([p.reshape(p.shape[:-1] + (-1, 2 * HD)) for p in parts], axis=-2)
    return stacked.reshape(stacked.shape[:-3] + (-1,))


def local_any(n_dp, n_mp):
    n_dev = n_dp * n_mp

    def scatter_rows(part):
        return lax.psum_scatter(part.astype(BF), "mp", scatter_dimension=0, tiled=True).astype(F32)

    def scatter_grad(part, dim):
        return lax.psum_scatter(part.astype(BF), "dp", scatter_dimension=dim, tiled=True).astype(F32)

    def local(block_in, out_grad, segment_ids, w_qkv, w_out, w_up, w_down, *vecs):
        model_index = lax.axis_index("mp")
        gain_one, shift_one, qv_all, out_shift, gain_two, shift_two, up_all, down_shift = (
            gather_vectors(vecs, n_dev)
        )
        qkv_full = lax.all_gather(w_qkv, "dp", axis=1, tiled=True)
        out_full = lax.all_gather(w_out, "dp", axis=1, tiled=True)
        up_full = lax.all_gather(w_up, "dp", axis=0, tiled=True)
        down_full = lax.all_gather(w_down, "dp", axis=1, tiled=True)
        head_cols = qkv_full.shape[2]
        hid_cols = up_full.shape[1]
        n_heads = head_cols // HD
        qv_shift = lax.dynamic_slice_in_dim(qv_all, model_index * head_cols, head_cols, 1)
        up_shift = lax.dynamic_slice_in_dim(up_all, model_index * hid_cols, hid_cols, 0)
        slopes = head_slopes(model_index * n_heads + jnp.arange(n_heads, dtype=jnp.int32))
        order = jnp.zeros((1,), jnp.int32)
        w_local = pair_columns([qkv_full[0], qkv_full[1], qkv_full[2]])
        b_local = pair_columns([qv_shift[0], jnp.zeros_like(qv_shift[0]), qv_shift[1]])
        hat_one, inv_one = norm_rows(block_in)
        normed_one = (hat_one * gain_one + shift_one).astype(BF)
        rows_one = lax.all_gather(normed_one, "mp", axis=0, tiled=True)
        qkv = (dot(rows_one, w_local) + b_local).astype(BF)[None]
        att, lse = attn_fwd(order, slopes, segment_ids, qkv)
        resid = block_in + scatter_rows(dot(att[0], out_full)) + out_shift
        hat_two, inv_two = norm_rows(resid)
        normed_two = (hat_two * gain_two + shift_two).astype(BF)
        rows_two = lax.all_gather(normed_two, "mp", axis=0, tiled=True)
        value, slope = gelu_both(dot(rows_two, up_full) + up_shift)
        hidden = value.astype(BF)
        block_out = resid + scatter_rows(dot(hidden, down_full)) + down_shift
        grad_rows = lax.all_gather(out_grad.astype(BF), "mp", axis=0, tiled=True)
        down_share = scatter_grad(cross_dot(hidden, grad_rows), 1)
        pre_grad = trans_dot(grad_rows, down_full) * slope
        pre_low = pre_grad.astype(BF)
        up_share = scatter_grad(cross_dot(rows_two, pre_low), 0)
        two_grad = scatter_rows(trans_dot(pre_low, up_full))
        resid_grad = out_grad + norm_back(two_grad, hat_two, inv_two, gain_two)
        resid_rows = lax.all_gather(resid_grad.astype(BF), "mp", axis=0, tiled=True)
        out_share = scatter_grad(cross_dot(att[0], resid_rows), 1)
        att_grad = trans_dot(resid_rows, out_full).astype(BF)[None]
        d_qkv, sums = attn_bwd(order, slopes, segment_ids, qkv, att, att_grad, lse)
        grad_w = cross_dot(rows_one, d_qkv[0])
        grad_w = grad_w.reshape(grad_w.shape[0], -1, 3, 2 * HD).transpose(2, 0, 1, 3)
        qkv_share = scatter_grad(grad_w.reshape(3, grad_w.shape[1], -1), 1)
        one_grad = scatter_rows(trans_dot(d_qkv[0], w_local))
        in_grad = resid_grad + norm_back(one_grad, hat_one, inv_one, gain_one)
        qv_place = lax.dynamic_update_slice_in_dim(
            jnp.zeros(qv_all.shape, F32),
            sums.transpose(1, 0, 2).reshape(2, -1),
            model_index * head_cols,
            1,
        )
        up_place = lax.dynamic_update_slice_in_dim(
            jnp.zeros(up_all.shape, F32), jnp.sum(pre_grad, axis=0), model_index * hid_cols, 0
        )
        shares = scatter_vectors(
            [
                jnp.sum(one_grad * hat_one, axis=0),
                jnp.sum(one_grad, axis=0),
                qv_place,
                jnp.sum(resid_grad, axis=0),
                jnp.sum(two_grad * hat_two, axis=0),
                jnp.sum(two_grad, axis=0),
                up_place,
                jnp.sum(out_grad, axis=0),
            ],
            n_dev,
        )
        return (block_out, in_grad, qkv_share, out_share, up_share, down_share, *shares)

    return local


CHUNK_OF_T = (0, 3, 1, 2)
T_OF_CHUNK = (0, 2, 3, 1)
PLANE_OF_T = (0, 3, 1, 2)
GROUPS = [[0, 1, 2, 3], [4, 5, 6, 7]]
TO_PLANE = [
    ((4 * y + t) * 4 + z, (4 * y + T_OF_CHUNK[z]) * 4 + PLANE_OF_T[t])
    for y in range(2)
    for t in range(4)
    for z in range(4)
]
FROM_PLANE = [(b, a) for a, b in TO_PLANE]


def swap(x, bits):
    return lax.ppermute(x, "dp", [(i, i ^ bits) for i in range(8)])


def relocate(x):
    return lax.ppermute(x, ("dp", "mp"), TO_PLANE)


def bring_back(x):
    return lax.ppermute(x, ("dp", "mp"), FROM_PLANE)


def gather_t(x):
    near = swap(x, 1)
    far = swap(x, 2)
    return jnp.concatenate([x, near, far, swap(far, 1)], axis=0)


def scatter_t(part):
    n = part.shape[0] // 4
    low = part.astype(BF)
    near = swap(jnp.concatenate([low[n : 2 * n], low[3 * n :]], axis=0), 1)
    far = (part[2 * n : 3 * n] + near[n:].astype(F32)).astype(BF)
    return part[:n] + near[:n].astype(F32) + swap(far, 2).astype(F32)


def exchange_t(x):
    return lax.all_to_all(x, "dp", 0, 0, tiled=True, axis_index_groups=GROUPS)


def gather_yz(x, y_index):
    mine = lax.all_gather(x, "mp", axis=0, tiled=False)
    other = swap(mine, 4)
    first = jnp.where(y_index == 0, mine, other)
    second = jnp.where(y_index == 0, other, mine)
    return jnp.stack([first, second])


def scatter_yz(part, y_index):
    keep = jnp.where(y_index == 0, part[0], part[1])
    send = jnp.where(y_index == 0, part[1], part[0]).astype(BF)
    both = (keep.astype(F32) + swap(send, 4).astype(F32)).astype(BF)
    return lax.psum_scatter(both, "mp", scatter_dimension=0, tiled=False)


def local_plane(block_in, out_grad, segment_ids, w_qkv, w_out, w_up, w_down, *vecs):
    n_dev = 32
    d_index = lax.axis_index("dp")
    t_index = d_index % 4
    y_index = d_index // 4
    width = block_in.shape[1]
    sub = width // 2

    pack = jnp.concatenate(
        [
            w_qkv.reshape(3, -1, 4, HD).transpose(2, 1, 0, 3).reshape(4, -1, 3 * HD),
            w_out.reshape(4, HD, -1).transpose(0, 2, 1),
            w_up.reshape(w_up.shape[0], 4, -1).transpose(1, 0, 2),
            w_down.reshape(4, -1, w_down.shape[1]).transpose(0, 2, 1),
        ],
        axis=2,
    )
    pack = exchange_t(pack).reshape(sub, -1)
    heads = gather_yz(pack[:, : 4 * HD], y_index)
    hids = gather_yz(pack[:, 4 * HD :], y_index)
    heads = heads.reshape(2, 2, 2, sub, 4, HD).transpose(0, 3, 1, 4, 2, 5)
    heads = heads.reshape(width, 2, 4, 2 * HD)
    w_local = heads[:, :, :3].reshape(width, -1)
    w_out_t = heads[:, :, 3].reshape(width, -1)
    units = hids.shape[3] // 2
    up_local = hids[..., :units].transpose(0, 2, 1, 3).reshape(width, -1)
    down_t = hids[..., units:].transpose(0, 2, 1, 3).reshape(width, -1)

    gain_one, shift_one, qv_all, out_shift, gain_two, shift_two, up_all, down_shift = (
        gather_vectors(vecs, n_dev)
    )
    qv_mine = lax.dynamic_index_in_dim(qv_all.reshape(2, 4, 4, HD), t_index, 2, False)
    qv_mine = qv_mine.reshape(2, -1)
    b_local = pair_columns([qv_mine[0], jnp.zeros_like(qv_mine[0]), qv_mine[1]])
    up_shift = lax.dynamic_index_in_dim(up_all.reshape(4, 4, -1), t_index, 1, False).reshape(-1)
    slopes = head_slopes(4 * jnp.arange(4, dtype=jnp.int32) + t_index)
    chunk = jnp.asarray(CHUNK_OF_T, jnp.int32)[t_index]
    order = jnp.asarray(T_OF_CHUNK, jnp.int32)[jnp.arange(4, dtype=jnp.int32) ^ chunk]

    hat_one, inv_one = norm_rows(block_in)
    rows_one = gather_t(relocate((hat_one * gain_one + shift_one).astype(BF)))
    segs = relocate(segment_ids)
    block_here = relocate(block_in.astype(BF)).astype(F32)
    grad_low = relocate(out_grad.astype(BF))
    grad_here = grad_low.astype(F32)
    grad_rows = gather_t(grad_low)

    qkv = (dot(rows_one, w_local) + b_local).astype(BF).reshape(4, -1, w_local.shape[1])
    att, lse = attn_fwd(order, slopes, segs, qkv)
    att_rows = att.reshape(-1, att.shape[2])
    resid = block_here + scatter_t(trans_dot(att_rows, w_out_t)) + out_shift
    hat_two, inv_two = norm_rows(resid)
    rows_two = gather_t((hat_two * gain_two + shift_two).astype(BF))
    value, slope = gelu_both(dot(rows_two, up_local) + up_shift)
    hidden = value.astype(BF)
    pre_grad = dot(grad_rows, down_t) * slope
    pre_low = pre_grad.astype(BF)
    two_grad = scatter_t(trans_dot(pre_low, up_local))
    resid_grad = grad_here + norm_back(two_grad, hat_two, inv_two, gain_two)
    resid_low = resid_grad.astype(BF)
    resid_rows = gather_t(resid_low)

    block_out = resid + scatter_t(trans_dot(hidden, down_t)) + down_shift
    block_out = bring_back(block_out.astype(BF)).astype(F32)
    resid_back = bring_back(resid_low).astype(F32)

    g_up = cross_dot(rows_two, pre_low).astype(BF).reshape(2, sub, 4, units)
    g_down = cross_dot(grad_rows, hidden).astype(BF).reshape(2, sub, 4, units)
    g_hid = jnp.concatenate([g_up, g_down], axis=3).transpose(0, 2, 1, 3)
    g_hid = scatter_yz(g_hid, y_index).reshape(4, sub // 4, 2 * units)
    g_hid = exchange_t(g_hid).astype(F32)
    up_share = g_hid[..., :units].transpose(1, 0, 2).reshape(w_up.shape)
    down_share = g_hid[..., units:].transpose(0, 2, 1).reshape(w_down.shape)

    att_grad = dot(resid_rows, w_out_t).astype(BF).reshape(att.shape)
    d_qkv, sums = attn_bwd(order, slopes, segs, qkv, att, att_grad, lse)
    d_rows = d_qkv.reshape(-1, d_qkv.shape[2])
    one_grad = bring_back(scatter_t(trans_dot(d_rows, w_local)).astype(BF)).astype(F32)
    in_grad = resid_back + norm_back(one_grad, hat_one, inv_one, gain_one)

    g_qkv = cross_dot(rows_one, d_rows).astype(BF).reshape(2, sub, 2, 3, 2, HD)
    g_out = cross_dot(resid_rows, att_rows).astype(BF).reshape(2, sub, 2, 1, 2, HD)
    g_head = jnp.concatenate([g_qkv, g_out], axis=3).transpose(0, 2, 4, 1, 3, 5)
    g_head = scatter_yz(g_head.reshape(2, 4, sub, 4 * HD), y_index)
    g_head = exchange_t(g_head.reshape(4, sub // 4, 4 * HD)).astype(F32)
    g_head = g_head.reshape(4, sub // 4, 4, HD)
    qkv_share = g_head[:, :, :3].transpose(2, 1, 0, 3).reshape(w_qkv.shape)
    out_share = g_head[:, :, 3].transpose(0, 2, 1).reshape(w_out.shape)

    mine = jnp.arange(4, dtype=jnp.int32) == t_index
    qv_part = sums.transpose(1, 0, 2).reshape(2, 4, 1, HD)
    qv_place = jnp.where(mine[None, None, :, None], qv_part, 0.0).reshape(2, width)
    up_part = jnp.sum(pre_grad, axis=0).reshape(4, 1, units)
    up_place = jnp.where(mine[None, :, None], up_part, 0.0).reshape(-1)
    shares = scatter_vectors(
        [
            jnp.sum(one_grad * hat_one, axis=0),
            jnp.sum(one_grad, axis=0),
            qv_place,
            jnp.sum(resid_grad, axis=0),
            jnp.sum(two_grad * hat_two, axis=0),
            jnp.sum(two_grad, axis=0),
            up_place,
            jnp.sum(out_grad, axis=0),
        ],
        n_dev,
    )
    return (block_out, in_grad, qkv_share, out_share, up_share, down_share, *shares)


def solution(mesh):
    n_dp, n_mp = mesh.shape["dp"], mesh.shape["mp"]
    local = local_plane if (n_dp, n_mp) == (8, 4) else local_any(n_dp, n_mp)
    both = ("dp", "mp")
    weights = (P(None, "dp", "mp"), P("mp", "dp"), P("dp", "mp"), P("mp", "dp"))
    vectors = (P(both), P(both), P(None, both), P(both), P(both), P(both), P(both), P(both))
    return jax.shard_map(
        local,
        mesh=mesh,
        in_specs=(P(both, None), P(both, None), P("dp"), *weights, *vectors),
        out_specs=(P(both, None), P(both, None), *weights, *vectors),
        check_vma=False,
    )
```

time: 1210 us -> 574 us (0.47)
  waiting for transfers between devices: 699 us -> 185 us
  blocking collectives: 236 us -> 0 us
  starting transfers between devices: 1.12 us -> 173 us
  matrix products: 123 us -> 44.3 us
  Pallas kernels: 0 us -> 27.7 us
    reduce_scatter x8 -> x2, waiting for transfers between devices: 477 us -> 0.02 us  [scatter_yz(): return lax.psum_scatter(both, 'mp', scatter_dimension=0, tiled=False)]
    ppermute x0 -> x31, waiting for transfers between devices: none -> 153 us  [the longest x24 153 us: swap(): return lax.ppermute(x, 'dp', [(i, i ^ bits) for i in range(8)])]
    all_gather x3 -> x0, blocking collectives: 148 us -> none  [the longest x1 69.3 us: local(): lax.all_gather(bias_up, ('dp', 'mp'), axis=0, tiled=True)]
    all_gather x7 -> x2, waiting for transfers between devices: 129 us -> 0.01 us  [gather_yz(): mine = lax.all_gather(x, 'mp', axis=0, tiled=False)]
    ppermute x0 -> x31, starting transfers between devices: none -> 99.5 us  [the longest x24 90.4 us: swap(): return lax.ppermute(x, 'dp', [(i, i ^ bits) for i in range(8)])]
    unnamed x17 -> x4, waiting for transfers between devices: 93.3 us -> 0.07 us
    unnamed x2 -> x0, blocking collectives: 88.2 us -> none
    all_to_all x0 -> x5, starting transfers between devices: none -> 72.9 us  [the longest x1 56.1 us: scatter_vectors(): lax.all_to_all(jnp.concatenate(parts, axis=1), ('dp', 'mp'), 0, 0, tiled=...]
  transfers between devices with their start and end apart: 16 -> 40, of which waited for: 13 -> 17; matrix products, arithmetic and copies ran while one was open for 7% -> 19% of each run, Pallas kernels for 0% -> 2%
where the time goes in v1:
time: 574 us; the launch traced here: 569 us
  waiting for transfers between devices  185 us (32%)
  starting transfers between devices  173 us (30%)
  local copies, waits for them, and re-layouts  81.4 us (14%)
  matrix products  44.3 us (8%)
  other arithmetic  42.4 us (7%)
  Pallas kernels  27.7 us (5%)
  between operations  15.3 us (3%)
    ppermute x24, waiting for transfers between devices, swap(): return lax.ppermute(x, 'dp', [(i, i ^ bits) for i in range(8)])  153 us
    ppermute x24, starting transfers between devices, swap(): return lax.ppermute(x, 'dp', [(i, i ^ bits) for i in range(8)])  90.4 us
    all_to_all x1, starting transfers between devices, scatter_vectors(): lax.all_to_all(jnp.concatenate(parts, axis=1), ('dp', 'mp'), 0, 0, tiled=...  56.1 us
    unnamed x145, local copies, waits for them, and re-layouts  21 us
    all_to_all x3, waiting for transfers between devices, exchange_t(): return lax.all_to_all(x, 'dp', 0, 0, tiled=True, axis_index_groups=GROUPS)  20.5 us
    dot_general x4, matrix products, cross_dot(): lax.dot_general(left, right, (((0,), (0,)), ((), ())), preferred_element_...  18.4 us
    pallas_call x1, Pallas kernels, attn_bwd(): pl.pallas_call(lambda *refs: attn_bwd_kernel(*refs, nb=nb, rb=rb), grid=(...  15.1 us
    dot_general x4, matrix products, dot(): return jnp.dot(left, right, preferred_element_type=F32)  14.8 us
  transfers between devices with their start and end apart: 40, of which 17 were waited for; matrix products, arithmetic and copies ran while one was open for 19% of the time, Pallas kernels for 2%

profile of v1, /device:TPU:0, one launch (start us, length us, event | category | flops | bytes accessed | tf_op | source)
XLA Modules:
  0.0 569.2 jit_solution(1736189259292826550)
XLA Ops:
  11.5 4.2 all-to-all-start.1
  16.4 10.9 %all-to-all-done.1 = bf16[4,128,768]{1,2,0:T(8,128)(2,1)S(1)} async-done(((bf16[4,128,768]{1,2,0:T(8,128)(2,1)}), bf16[4,128,768]{1,2,0:T(8,128)(2,1)S(1)}, u32[]{:S(2)}, u32[]{:S(2)}) %all-to-all-start.1) | async-done | bytes 786464 | tf_op jit(solution)/shard_map/all_to_all | solution.py:387
  28.0 5.6 all-to-all-start
  34.9 6.2 %all-to-all-done = f32[32,1,384]{2,1,0:T(1,128)S(1)} async-done(((f32[32,1,384]{2,1,0:T(1,128)}), f32[32,1,384]{2,1,0:T(1,128)S(1)}, u32[]{:S(2)}, u32[]{:S(2)}) %all-to-all-start) | async-done | bytes 49184 | tf_op jit(solution)/shard_map/all_to_all | solution.py:222
  43.9 41.6 %collective-permute-start.4 = (bf16[288,1024]{1,0:T(8,128)(2,1)}, bf16[288,1024]{1,0:T(8,128)(2,1)}, u32[]{:S(2)}, u32[]{:S(2)}) collective-permute-start(bf16[288,1024]{1,0:T(8,128)(2,1)} %collective-permute-done.2), channel_id=1, source_target_pairs={{0,8},{4,12},{8,0},{12,4},{16,24},{20,28},{24,16},{28,20},{1,9},{5... | collective-permute-start | bytes 1769480 | tf_op jit(solution)/shard_map/ppermute | solution.py:361
  101.1 13.0 %collective-permute-done.6 = bf16[4,512,256]{1,2,0:T(8,128)(2,1)} collective-permute-done((bf16[4,512,256]{1,2,0:T(8,128)(2,1)S(1)}, bf16[4,512,256]{1,2,0:T(8,128)(2,1)}, u32[]{:S(2)}, u32[]{:S(2)}) %collective-permute-start.6) | collective-permute-done | bytes 1048608 | tf_op jit(solution)/shard_map/ppermute | solution.py:361
  127.5 12.6 %attn_fwd.1 = (bf16[4,288,256]{2,1,0:T(8,128)(2,1)}, f32[2,2,1152]{2,1,0:T(2,128)}) custom-call(s32[4]{0:T(128)} %gather_fusion, f32[4]{0:T(128)} %multiply_exponential_fusion.refs_1_, s32[1,1152]{1,0:T(1,128)} %reshape.265.refs_2_, s32[1152,1]{1,0:T(8,128)} %reshape.317.refs_3_, bf16[4,288,768]{2,1,0:T(8,128)(2,1)} %bitcast.103, ...), custom_call_target="tpu_custom_call" | custom-call | tf_op jit(solution)/shard_map/attn_fwd/pallas_call | solution.py:182
  147.9 36.4 %collective-permute-start.18 = (bf16[288,1024]{1,0:T(8,128)(2,1)S(1)}, bf16[288,1024]{1,0:T(8,128)(2,1)}, u32[]{:S(2)}, u32[]{:S(2)}) collective-permute-start(bf16[288,1024]{1,0:T(8,128)(2,1)S(1)} %collective-permute-done.16), channel_id=1, source_target_pairs={{0,8},{4,12},{8,0},{12,4},{16,24},{20,28},{24,16},{28,20},{1,9},{5... | collective-permute-start | bytes 1769480 | tf_op jit(solution)/shard_map/ppermute | solution.py:361
  185.3 4.6 copy.135
  190.8 9.9 %collective-permute-done.18 = bf16[288,1024]{1,0:T(8,128)(2,1)} collective-permute-done((bf16[288,1024]{1,0:T(8,128)(2,1)S(1)}, bf16[288,1024]{1,0:T(8,128)(2,1)}, u32[]{:S(2)}, u32[]{:S(2)}) %collective-permute-start.18) | collective-permute-done | bytes 589856 | tf_op jit(solution)/shard_map/ppermute | solution.py:361
  201.5 11.7 %collective-permute-done.8 = bf16[288,1024]{1,0:T(8,128)(2,1)} collective-permute-done((bf16[288,1024]{1,0:T(8,128)(2,1)S(1)}, bf16[288,1024]{1,0:T(8,128)(2,1)}, u32[]{:S(2)}, u32[]{:S(2)}) %collective-permute-start.8) | collective-permute-done | bytes 589856 | tf_op jit(solution)/shard_map/ppermute | solution.py:361
  220.2 12.0 %collective-permute-done.10 = bf16[288,1024]{1,0:T(8,128)(2,1)S(1)} collective-permute-done((bf16[288,1024]{1,0:T(8,128)(2,1)S(1)}, bf16[288,1024]{1,0:T(8,128)(2,1)S(1)}, u32[]{:S(2)}, u32[]{:S(2)}) %collective-permute-start.10) | collective-permute-done | bytes 589856 | tf_op jit(solution)/shard_map/ppermute | solution.py:361
  232.2 4.8 select_bitcast_fusion.2
  242.7 5.7 fusion.56
  261.3 11.8 %collective-permute-done.21 = bf16[288,1024]{1,0:T(8,128)(2,1)} collective-permute-done((bf16[288,1024]{1,0:T(8,128)(2,1)}, bf16[288,1024]{1,0:T(8,128)(2,1)}, u32[]{:S(2)}, u32[]{:S(2)}) %collective-permute-start.21) | collective-permute-done | bytes 589856 | tf_op jit(solution)/shard_map/ppermute | solution.py:361
  276.0 8.9 %collective-permute-done.14 = bf16[288,1024]{1,0:T(8,128)(2,1)S(1)} collective-permute-done((bf16[288,1024]{1,0:T(8,128)(2,1)}, bf16[288,1024]{1,0:T(8,128)(2,1)S(1)}, u32[]{:S(2)}, u32[]{:S(2)}) %collective-permute-start.14) | collective-permute-done | bytes 589856 | tf_op jit(solution)/shard_map/ppermute | solution.py:361
  285.0 3.8 fusion.40
  290.5 13.3 %collective-permute-done.24 = bf16[288,1024]{1,0:T(8,128)(2,1)} collective-permute-done((bf16[288,1024]{1,0:T(8,128)(2,1)}, bf16[288,1024]{1,0:T(8,128)(2,1)}, u32[]{:S(2)}, u32[]{:S(2)}) %collective-permute-start.24) | collective-permute-done | bytes 589856 | tf_op jit(solution)/shard_map/ppermute | solution.py:361
  303.8 6.8 %convolution_convert_fusion.1 = bf16[1024,1024]{1,0:T(8,128)(2,1)} fusion(bf16[1152,1024]{1,0:T(8,128)(2,1)S(1)} %copy-done.27, f32[1152,1024]{1,0:T(8,128)} %copy-done.65), kind=kOutput, calls=%fused_computation.30 | convolution fusion | flops 2427584512 | bytes 9175040 | tf_op jit(solution)/shard_map/dot_general | solution.py:50
  310.6 3.5 reshape.290
  319.0 15.1 %attn_bwd.1 = (bf16[4,288,768]{2,1,0:T(8,128)(2,1)}, f32[2,2,128]{2,1,0:T(2,128)}) custom-call(s32[4]{0:T(128)} %gather_fusion, f32[4]{0:T(128)} %multiply_exponential_fusion.refs_1_, s32[1,1152]{1,0:T(1,128)} %reshape.265.refs_2_, s32[1152,1]{1,0:T(8,128)} %reshape.317.refs_3_, bf16[4,288,768]{2,1,0:T(8,128)(2,1)} %bitcast.106, ...), custom_call_target="tpu_custom_call" | custom-call | tf_op jit(solution)/shard_map/attn_bwd/pallas_call | solution.py:201
  334.1 5.0 convolution_convert_fusion.3
  343.5 6.6 %reshape.315 = bf16[2,512,2,3,2,64]{5,4,3,2,1,0:T(2,128)(2,1)} reshape(bf16[1024,768]{1,0:T(8,128)(2,1)} %convolution_convert_fusion.3) | data formatting | bytes 3145728 | tf_op jit(solution)/shard_map/reshape | solution.py:485
  350.1 7.1 %copy.140 = bf16[2,512,2,3,2,64]{1,5,3,4,2,0:T(8,128)(2,1)S(1)} copy(bf16[2,512,2,3,2,64]{5,4,3,2,1,0:T(2,128)(2,1)} %reshape.315) | data formatting | bytes 3145728 | tf_op jit(solution)/shard_map/reshape | solution.py:485
  360.3 4.1 convolution_convert_fusion.2
  372.4 12.9 %collective-permute-done.29 = bf16[4,512,256]{1,2,0:T(8,128)(2,1)} collective-permute-done((bf16[4,512,256]{1,2,0:T(8,128)(2,1)}, bf16[4,512,256]{1,2,0:T(8,128)(2,1)}, u32[]{:S(2)}, u32[]{:S(2)}) %collective-permute-start.29) | collective-permute-done | bytes 1048608 | tf_op jit(solution)/shard_map/ppermute | solution.py:361
  387.8 41.9 %collective-permute-done.30 = bf16[4,512,512]{2,1,0:T(8,128)(2,1)} collective-permute-done((bf16[4,512,512]{2,1,0:T(8,128)(2,1)S(1)}, bf16[4,512,512]{2,1,0:T(8,128)(2,1)}, u32[]{:S(2)}, u32[]{:S(2)}) %collective-permute-start.30) | collective-permute-done | bytes 2097184 | tf_op jit(solution)/shard_map/ppermute | solution.py:361
  429.7 5.1 fusion.5
  445.5 14.1 %collective-permute-done.27 = bf16[288,1024]{1,0:T(8,128)(2,1)S(1)} collective-permute-done((bf16[288,1024]{1,0:T(8,128)(2,1)S(1)}, bf16[288,1024]{1,0:T(8,128)(2,1)S(1)}, u32[]{:S(2)}, u32[]{:S(2)}) %collective-permute-start.27) | collective-permute-done | bytes 589856 | tf_op jit(solution)/shard_map/ppermute | solution.py:361
  474.8 56.1 %all-to-all-start.4 = ((f32[32,1,384]{2,1,0:T(1,128)}), f32[32,1,384]{2,1,0:T(1,128)S(1)}, u32[]{:S(2)}, u32[]{:S(2)}) async-start(f32[32,1,384]{2,1,0:T(1,128)} %all_to_all.26), calls=%async_computation.6 | async-start | bytes 98304 | tf_op jit(solution)/shard_map/all_to_all | solution.py:246
  532.7 5.6 all-to-all-done.4
  553.5 6.5 %all-to-all-done.3 = bf16[4,128,512]{2,1,0:T(8,128)(2,1)S(1)} async-done(((bf16[4,128,512]{2,1,0:T(8,128)(2,1)}), bf16[4,128,512]{2,1,0:T(8,128)(2,1)S(1)}, u32[]{:S(2)}, u32[]{:S(2)}) %all-to-all-start.3) | async-done | bytes 524320 | tf_op jit(solution)/shard_map/all_to_all | solution.py:387
  (340 shorter events, 146.3 us)
Async XLA Ops:
  11.5 15.9 %all-to-all-start.1 = ((bf16[4,128,768]{1,2,0:T(8,128)(2,1)}), bf16[4,128,768]{1,2,0:T(8,128)(2,1)S(1)}, u32[]{:S(2)}, u32[]{:S(2)}) async-start(bf16[4,128,768]{1,2,0:T(8,128)(2,1)} %pad_maximum_fusion.7), calls=%async_computation.1 | async-start | bytes 1572864 | tf_op jit(solution)/shard_map/all_to_all | solution.py:387
  28.0 13.0 %all-to-all-start = ((f32[32,1,384]{2,1,0:T(1,128)}), f32[32,1,384]{2,1,0:T(1,128)S(1)}, u32[]{:S(2)}, u32[]{:S(2)}) async-start(f32[32,1,384]{2,1,0:T(1,128)} %broadcast_in_dim.67), calls=%async_computation | async-start | bytes 98304 | tf_op jit(solution)/shard_map/all_to_all | solution.py:222
  33.7 53.2 %all-gather.5.cloned.1.call-start = ((), (), s32[]{:S(2)}) async-start(), calls=%async_computation.9 | async-start | bytes 1310720 | tf_op jit(solution)/shard_map/all_gather | solution.py:391
  34.8 150.5 %all-gather.7.cloned.1.call-start = ((), (), s32[]{:S(2)}) async-start(), calls=%async_computation.10 | async-start | bytes 2621440 | tf_op jit(solution)/shard_map/all_gather | solution.py:391
  43.9 50.1 %collective-permute-start.4 = (bf16[288,1024]{1,0:T(8,128)(2,1)}, bf16[288,1024]{1,0:T(8,128)(2,1)}, u32[]{:S(2)}, u32[]{:S(2)}) collective-permute-start(bf16[288,1024]{1,0:T(8,128)(2,1)} %collective-permute-done.2), channel_id=1, source_target_pairs={{0,8},{4,12},{8,0},{12,4},{16,24},{20,28},{24,16},{28,20},{1,9},{5... | collective-permute-start | bytes 1769480 | tf_op jit(solution)/shard_map/ppermute | solution.py:361
  86.8 9.6 %collective-permute-start.3 = (bf16[288,1024]{1,0:T(8,128)(2,1)}, bf16[288,1024]{1,0:T(8,128)(2,1)}, u32[]{:S(2)}, u32[]{:S(2)}) collective-permute-start(bf16[288,1024]{1,0:T(8,128)(2,1)} %collective-permute-done.2), channel_id=1, source_target_pairs={{0,4},{4,0},{8,12},{12,8},{16,20},{20,16},{24,28},{28,24},{1,5},{5... | collective-permute-start | bytes 1769480 | tf_op jit(solution)/shard_map/ppermute | solution.py:361
  88.4 25.7 %collective-permute-start.6 = (bf16[4,512,256]{1,2,0:T(8,128)(2,1)S(1)}, bf16[4,512,256]{1,2,0:T(8,128)(2,1)}, u32[]{:S(2)}, u32[]{:S(2)}) collective-permute-start(bf16[4,512,256]{1,2,0:T(8,128)(2,1)S(1)} %copy.127), channel_id=1, source_target_pairs={{0,16},{4,20},{8,24},{12,28},{16,0},{20,4},{24,8},{28,12},{1,17},{... | collective-permute-start | bytes 3145736 | tf_op jit(solution)/shard_map/ppermute | solution.py:361
  94.9 436.0 %reduce-scatter.3.cloned.1.call-start = ((), (), s32[]{:S(2)}) async-start(), calls=%async_computation.7 | async-start | bytes 1310720 | tf_op jit(solution)/shard_map/reduce_scatter | solution.py:402
  142.2 42.0 %collective-permute-start.7 = (bf16[576,1024]{1,0:T(8,128)(2,1)S(1)}, bf16[576,1024]{1,0:T(8,128)(2,1)S(1)}, u32[]{:S(2)}, u32[]{:S(2)}) collective-permute-start(bf16[576,1024]{1,0:T(8,128)(2,1)S(1)} %pad_maximum_fusion.3), channel_id=1, source_target_pairs={{0,4},{4,0},{8,12},{12,8},{16,20},{20,16},{24,28},{28,24},{1,5},{5... | collective-permute-start | bytes 3538952 | tf_op jit(solution)/shard_map/ppermute | solution.py:361
  145.6 55.1 %collective-permute-start = (bf16[288,1024]{1,0:T(8,128)(2,1)}, bf16[288,1024]{1,0:T(8,128)(2,1)S(1)}, u32[]{:S(2)}, u32[]{:S(2)}) collective-permute-start(bf16[288,1024]{1,0:T(8,128)(2,1)} %get-tuple-element.112), channel_id=1, source_target_pairs={{0,0},{1,8},{2,12},{3,4},{4,3},{5,11},{6,15},{7,7},{8,1},{9,9},{10... | collective-permute-start | bytes 1769480 | tf_op jit(solution)/shard_map/ppermute | solution.py:365
  147.9 52.8 %collective-permute-start.18 = (bf16[288,1024]{1,0:T(8,128)(2,1)S(1)}, bf16[288,1024]{1,0:T(8,128)(2,1)}, u32[]{:S(2)}, u32[]{:S(2)}) collective-permute-start(bf16[288,1024]{1,0:T(8,128)(2,1)S(1)} %collective-permute-done.16), channel_id=1, source_target_pairs={{0,8},{4,12},{8,0},{12,4},{16,24},{20,28},{24,16},{28,20},{1,9},{5... | collective-permute-start | bytes 1769480 | tf_op jit(solution)/shard_map/ppermute | solution.py:361
  185.2 28.0 %collective-permute-start.8 = (bf16[288,1024]{1,0:T(8,128)(2,1)S(1)}, bf16[288,1024]{1,0:T(8,128)(2,1)}, u32[]{:S(2)}, u32[]{:S(2)}) collective-permute-start(bf16[288,1024]{1,0:T(8,128)(2,1)S(1)} %fusion.27), channel_id=1, source_target_pairs={{0,8},{4,12},{8,0},{12,4},{16,24},{20,28},{24,16},{28,20},{1,9},{5... | collective-permute-start | bytes 1769480 | tf_op jit(solution)/shard_map/ppermute | solution.py:361
  189.9 42.3 %collective-permute-start.12 = (bf16[4,512,512]{2,0,1:T(4,128)(2,1)}, bf16[4,512,512]{2,0,1:T(4,128)(2,1)}, u32[]{:S(2)}, u32[]{:S(2)}) collective-permute-start(bf16[4,512,512]{2,0,1:T(4,128)(2,1)} %copy.135), channel_id=1, source_target_pairs={{0,16},{4,20},{8,24},{12,28},{16,0},{20,4},{24,8},{28,12},{1,17},{... | collective-permute-start | bytes 6291464 | tf_op jit(solution)/shard_map/ppermute | solution.py:361
  190.8 28.0 %collective-permute-start.17 = (bf16[288,1024]{1,0:T(8,128)(2,1)S(1)}, bf16[288,1024]{1,0:T(8,128)(2,1)S(1)}, u32[]{:S(2)}, u32[]{:S(2)}) collective-permute-start(bf16[288,1024]{1,0:T(8,128)(2,1)S(1)} %collective-permute-done.16), channel_id=1, source_target_pairs={{0,4},{4,0},{8,12},{12,8},{16,20},{20,16},{24,28},{28,24},{1,5},{5... | collective-permute-start | bytes 1769480 | tf_op jit(solution)/shard_map/ppermute | solution.py:361
  200.7 19.4 %collective-permute-start.19 = (bf16[288,1024]{1,0:T(8,128)(2,1)}, bf16[288,1024]{1,0:T(8,128)(2,1)S(1)}, u32[]{:S(2)}, u32[]{:S(2)}) collective-permute-start(bf16[288,1024]{1,0:T(8,128)(2,1)} %collective-permute-done.18), channel_id=1, source_target_pairs={{0,4},{4,0},{8,12},{12,8},{16,20},{20,16},{24,28},{28,24},{1,5},{5... | collective-permute-start | bytes 1769480 | tf_op jit(solution)/shard_map/ppermute | solution.py:361
  216.0 16.2 %collective-permute-start.10 = (bf16[288,1024]{1,0:T(8,128)(2,1)S(1)}, bf16[288,1024]{1,0:T(8,128)(2,1)S(1)}, u32[]{:S(2)}, u32[]{:S(2)}) collective-permute-start(bf16[288,1024]{1,0:T(8,128)(2,1)S(1)} %add_convert_fusion), channel_id=1, source_target_pairs={{0,8},{4,12},{8,0},{12,4},{16,24},{20,28},{24,16},{28,20},{1,9},{5... | collective-permute-start | bytes 1769480 | tf_op jit(solution)/shard_map/ppermute | solution.py:361
  220.1 19.8 %collective-permute-start.9 = (bf16[288,1024]{1,0:T(8,128)(2,1)S(1)}, bf16[288,1024]{1,0:T(8,128)(2,1)S(1)}, u32[]{:S(2)}, u32[]{:S(2)}) collective-permute-start(bf16[288,1024]{1,0:T(8,128)(2,1)S(1)} %add_convert_fusion), channel_id=1, source_target_pairs={{0,4},{4,0},{8,12},{12,8},{16,20},{20,16},{24,28},{28,24},{1,5},{5... | collective-permute-start | bytes 1769480 | tf_op jit(solution)/shard_map/ppermute | solution.py:361
  256.6 16.5 %collective-permute-start.21 = (bf16[288,1024]{1,0:T(8,128)(2,1)}, bf16[288,1024]{1,0:T(8,128)(2,1)}, u32[]{:S(2)}, u32[]{:S(2)}) collective-permute-start(bf16[288,1024]{1,0:T(8,128)(2,1)} %fusion.20), channel_id=1, source_target_pairs={{0,8},{4,12},{8,0},{12,4},{16,24},{20,28},{24,16},{28,20},{1,9},{5... | collective-permute-start | bytes 1769480 | tf_op jit(solution)/shard_map/ppermute | solution.py:361
  259.6 25.4 %collective-permute-start.14 = (bf16[288,1024]{1,0:T(8,128)(2,1)}, bf16[288,1024]{1,0:T(8,128)(2,1)S(1)}, u32[]{:S(2)}, u32[]{:S(2)}) collective-permute-start(bf16[288,1024]{1,0:T(8,128)(2,1)} %fusion.22), channel_id=1, source_target_pairs={{0,8},{4,12},{8,0},{12,4},{16,24},{20,28},{24,16},{28,20},{1,9},{5... | collective-permute-start | bytes 1769480 | tf_op jit(solution)/shard_map/ppermute | solution.py:361
  288.8 15.0 %collective-permute-start.24 = (bf16[288,1024]{1,0:T(8,128)(2,1)}, bf16[288,1024]{1,0:T(8,128)(2,1)}, u32[]{:S(2)}, u32[]{:S(2)}) collective-permute-start(bf16[288,1024]{1,0:T(8,128)(2,1)} %get-tuple-element.89), channel_id=1, source_target_pairs={{0,8},{4,12},{8,0},{12,4},{16,24},{20,28},{24,16},{28,20},{1,9},{5... | collective-permute-start | bytes 1769480 | tf_op jit(solution)/shard_map/ppermute | solution.py:361
  290.5 25.2 %collective-permute-start.23 = (bf16[288,1024]{1,0:T(8,128)(2,1)}, bf16[288,1024]{1,0:T(8,128)(2,1)}, u32[]{:S(2)}, u32[]{:S(2)}) collective-permute-start(bf16[288,1024]{1,0:T(8,128)(2,1)} %get-tuple-element.89), channel_id=1, source_target_pairs={{0,4},{4,0},{8,12},{12,8},{16,20},{20,16},{24,28},{28,24},{1,5},{5... | collective-permute-start | bytes 1769480 | tf_op jit(solution)/shard_map/ppermute | solution.py:361
  303.8 12.0 %collective-permute-start.25 = (bf16[288,1024]{1,0:T(8,128)(2,1)}, bf16[288,1024]{1,0:T(8,128)(2,1)}, u32[]{:S(2)}, u32[]{:S(2)}) collective-permute-start(bf16[288,1024]{1,0:T(8,128)(2,1)} %collective-permute-done.24), channel_id=1, source_target_pairs={{0,4},{4,0},{8,12},{12,8},{16,20},{20,16},{24,28},{28,24},{1,5},{5... | collective-permute-start | bytes 1769480 | tf_op jit(solution)/shard_map/ppermute | solution.py:361
  358.9 26.3 %collective-permute-start.29 = (bf16[4,512,256]{1,2,0:T(8,128)(2,1)}, bf16[4,512,256]{1,2,0:T(8,128)(2,1)}, u32[]{:S(2)}, u32[]{:S(2)}) collective-permute-start(bf16[4,512,256]{1,2,0:T(8,128)(2,1)} %bitcast.33), channel_id=1, source_target_pairs={{0,16},{4,20},{8,24},{12,28},{16,0},{20,4},{24,8},{28,12},{1,17},{... | collective-permute-start | bytes 3145736 | tf_op jit(solution)/shard_map/ppermute | solution.py:361
  371.7 58.0 %collective-permute-start.30 = (bf16[4,512,512]{2,1,0:T(8,128)(2,1)S(1)}, bf16[4,512,512]{2,1,0:T(8,128)(2,1)}, u32[]{:S(2)}, u32[]{:S(2)}) collective-permute-start(bf16[4,512,512]{2,1,0:T(8,128)(2,1)S(1)} %select_bitcast_fusion), channel_id=1, source_target_pairs={{0,16},{4,20},{8,24},{12,28},{16,0},{20,4},{24,8},{28,12},{1,17},{... | collective-permute-start | bytes 6291464 | tf_op jit(solution)/shard_map/ppermute | solution.py:361
  387.7 156.9 %reduce-scatter.5.cloned.1.call-start = ((), (), s32[]{:S(2)}) async-start(), calls=%async_computation.8 | async-start | bytes 2621440 | tf_op jit(solution)/shard_map/reduce_scatter | solution.py:402
  443.0 16.6 %collective-permute-start.27 = (bf16[288,1024]{1,0:T(8,128)(2,1)S(1)}, bf16[288,1024]{1,0:T(8,128)(2,1)S(1)}, u32[]{:S(2)}, u32[]{:S(2)}) collective-permute-start(bf16[288,1024]{1,0:T(8,128)(2,1)S(1)} %fusion.17), channel_id=1, source_target_pairs={{0,8},{4,12},{8,0},{12,4},{16,24},{20,28},{24,16},{28,20},{1,9},{5... | collective-permute-start | bytes 1769480 | tf_op jit(solution)/shard_map/ppermute | solution.py:361
  444.8 24.9 %collective-permute-start.15 = (bf16[288,1024]{1,0:T(8,128)(2,1)S(1)}, bf16[288,1024]{1,0:T(8,128)(2,1)S(1)}, u32[]{:S(2)}, u32[]{:S(2)}) collective-permute-start(bf16[288,1024]{1,0:T(8,128)(2,1)S(1)} %copy-done.22), channel_id=1, source_target_pairs={{0,0},{8,1},{12,2},{4,3},{3,4},{11,5},{15,6},{7,7},{1,8},{9,9},{13... | collective-permute-start | bytes 1769480 | tf_op jit(solution)/shard_map/ppermute | solution.py:369
  460.7 11.9 %collective-permute-start.28 = (bf16[288,1024]{1,0:T(8,128)(2,1)}, bf16[288,1024]{1,0:T(8,128)(2,1)S(1)}, u32[]{:S(2)}, u32[]{:S(2)}) collective-permute-start(bf16[288,1024]{1,0:T(8,128)(2,1)} %fusion.19), channel_id=1, source_target_pairs={{0,0},{8,1},{12,2},{4,3},{3,4},{11,5},{15,6},{7,7},{1,8},{9,9},{13... | collective-permute-start | bytes 1769480 | tf_op jit(solution)/shard_map/ppermute | solution.py:369
  463.9 77.8 %collective-permute-start.22 = (bf16[288,1024]{1,0:T(8,128)(2,1)}, bf16[288,1024]{1,0:T(8,128)(2,1)S(1)}, u32[]{:S(2)}, u32[]{:S(2)}) collective-permute-start(bf16[288,1024]{1,0:T(8,128)(2,1)} %get-tuple-element.89), channel_id=1, source_target_pairs={{0,0},{8,1},{12,2},{4,3},{3,4},{11,5},{15,6},{7,7},{1,8},{9,9},{13... | collective-permute-start | bytes 1769480 | tf_op jit(solution)/shard_map/ppermute | solution.py:369
  474.8 63.6 %all-to-all-start.4 = ((f32[32,1,384]{2,1,0:T(1,128)}), f32[32,1,384]{2,1,0:T(1,128)S(1)}, u32[]{:S(2)}, u32[]{:S(2)}) async-start(f32[32,1,384]{2,1,0:T(1,128)} %all_to_all.26), calls=%async_computation.6 | async-start | bytes 98304 | tf_op jit(solution)/shard_map/all_to_all | solution.py:246
  538.3 9.4 %all-to-all-start.2 = ((bf16[4,128,256]{1,2,0:T(8,128)(2,1)}), bf16[4,128,256]{1,2,0:T(8,128)(2,1)S(1)}, u32[]{:S(2)}, u32[]{:S(2)}) async-start(bf16[4,128,256]{1,2,0:T(8,128)(2,1)} %copy.142), calls=%async_computation.3 | async-start | bytes 524288 | tf_op jit(solution)/shard_map/all_to_all | solution.py:387
  547.7 12.3 %all-to-all-start.3 = ((bf16[4,128,512]{2,1,0:T(8,128)(2,1)}), bf16[4,128,512]{2,1,0:T(8,128)(2,1)S(1)}, u32[]{:S(2)}, u32[]{:S(2)}) async-start(bf16[4,128,512]{2,1,0:T(8,128)(2,1)} %bitcast.140), calls=%async_computation.5 | async-start | bytes 1048576 | tf_op jit(solution)/shard_map/all_to_all | solution.py:387
  (74 other events, 1038.2 us)
Sparse Core Ops, SparseCore 0:
  36.6 45.5 all-gather.4
  95.1 44.7 all-gather.6
  387.9 24.8 reduce-scatter.2
  434.9 84.1 reduce-scatter.4

commit v2 on v1

--- a/solution.py
+++ b/solution.py
@@ -5,6 +5,7 @@
 from jax.experimental.pallas import tpu as pltpu
 from jax.sharding import PartitionSpec as P
 
+
 H = 16
 HD = 64
 L = 1152
@@ -14,6 +15,7 @@
 NORM_EPS = 1e-05
 GELU_SCALE = 0.7978845608028654
 GELU_CUBE = 0.044715
+
 BF = jnp.bfloat16
 F32 = jnp.float32
 
@@ -190,6 +192,9 @@
         ],
         scratch_shapes=[rows(), rows(), rows(), pltpu.VMEM((2 * HD, L), BF), rows()],
         name="attn_fwd",
+        cost_estimate=pl.CostEstimate(
+            flops=pairs * 4 * L * L * HD * 4, transcendentals=pairs * L * L, bytes_accessed=1 << 24
+        ),
     )(order, slopes, segs.reshape(1, L), segs.reshape(L, 1), qkv, qkv, qkv)
 
 
@@ -213,6 +218,9 @@
         scratch_shapes=[rows(), rows(), rows(), pltpu.VMEM((2 * HD, L), BF), rows(), rows(),
                         rows(), rows(F32), rows(F32)],
         name="attn_bwd",
+        cost_estimate=pl.CostEstimate(
+            flops=pairs * 8 * L * L * HD * 4, transcendentals=pairs * L * L, bytes_accessed=1 << 25
+        ),
     )(order, slopes, segs.reshape(1, L), segs.reshape(L, 1), qkv, qkv, qkv, att, att_grad, lse_rows)
 
 
@@ -233,7 +241,7 @@
     return full
 
 
-def scatter_vectors(fulls, n_dev):
+def cut_vectors(fulls, n_dev):
     parts, shapes = [], []
     for v in fulls:
         if v.ndim == 2:
@@ -243,14 +251,22 @@
             part = v
             shapes.append((v.shape[0] // n_dev,))
         parts.append(part.reshape(n_dev, -1))
-    got = lax.all_to_all(jnp.concatenate(parts, axis=1), ("dp", "mp"), 0, 0, tiled=True)
-    flat = jnp.sum(got, axis=0)
+    return jnp.concatenate(parts, axis=1), shapes
+
+
+def share_vectors(flat, shapes):
     outs, at = [], 0
-    for shape, part in zip(shapes, parts):
-        n = part.shape[1]
+    for shape in shapes:
+        n = shape[0] * (shape[1] if len(shape) == 2 else 1)
         outs.append(flat[at : at + n].reshape(shape))
         at += n
     return outs
+
+
+def scatter_vectors(fulls, n_dev):
+    rows, shapes = cut_vectors(fulls, n_dev)
+    got = lax.all_to_all(rows, ("dp", "mp"), 0, 0, tiled=True)
+    return share_vectors(jnp.sum(got, axis=0), shapes)
 
 
 def head_slopes(numbers):
@@ -369,37 +385,69 @@
     return lax.ppermute(x, ("dp", "mp"), FROM_PLANE)
 
 
-def gather_t(x):
+def gather_t(x, *fill):
+    far = swap(x, 2)
     near = swap(x, 1)
-    far = swap(x, 2)
-    return jnp.concatenate([x, near, far, swap(far, 1)], axis=0)
-
-
-def scatter_t(part):
+    if fill:
+        far, *fill = tie(far, *fill)
+    rows = jnp.concatenate([x, near, far, swap(far, 1)], axis=0)
+    return (rows, *fill) if fill else rows
+
+
+def scatter_near(part):
     n = part.shape[0] // 4
     low = part.astype(BF)
     near = swap(jnp.concatenate([low[n : 2 * n], low[3 * n :]], axis=0), 1)
-    far = (part[2 * n : 3 * n] + near[n:].astype(F32)).astype(BF)
-    return part[:n] + near[:n].astype(F32) + swap(far, 2).astype(F32)
+    far = (part[2 * n : 3 * n].astype(F32) + near[n:].astype(F32)).astype(BF)
+    return part[:n], near[:n], far
+
+
+def scatter_far(own, near, far):
+    far = swap(far, 2)
+    return own.astype(F32) + near.astype(F32) + far.astype(F32)
+
+
+def scatter_t(part):
+    return scatter_far(*scatter_near(part))
 
 
 def exchange_t(x):
     return lax.all_to_all(x, "dp", 0, 0, tiled=True, axis_index_groups=GROUPS)
 
 
-def gather_yz(x, y_index):
-    mine = lax.all_gather(x, "mp", axis=0, tiled=False)
-    other = swap(mine, 4)
+def exchange_swaps(x, t_index):
+    got = [lax.dynamic_index_in_dim(x, t_index ^ j, 0, False) for j in range(4)]
+    got = [got[0]] + [swap(got[j], j) for j in (1, 2, 3)]
+    return jnp.stack(got)[jnp.arange(4, dtype=jnp.int32) ^ t_index]
+
+
+def across(x, bits):
+    return lax.ppermute(x, "mp", [(i, i ^ bits) for i in range(4)])
+
+
+def gather_yz(x):
+    mine = [x] + [across(x, k) for k in (1, 2, 3)]
+    other = [swap(m, 4) for m in mine]
+    return mine, other
+
+
+def by_y(mine, other, y_index):
+    mine, other = jnp.concatenate(mine, axis=1), jnp.concatenate(other, axis=1)
     first = jnp.where(y_index == 0, mine, other)
     second = jnp.where(y_index == 0, other, mine)
-    return jnp.stack([first, second])
-
-
-def scatter_yz(part, y_index):
-    keep = jnp.where(y_index == 0, part[0], part[1])
-    send = jnp.where(y_index == 0, part[1], part[0]).astype(BF)
-    both = (keep.astype(F32) + swap(send, 4).astype(F32)).astype(BF)
-    return lax.psum_scatter(both, "mp", scatter_dimension=0, tiled=False)
+    return jnp.concatenate([first, second], axis=0)
+
+
+def send_z(parts):
+    return [parts[0]] + [across(parts[k], k) for k in (1, 2, 3)]
+
+
+def total_z(parts):
+    return sum(p.astype(F32) for p in parts).astype(BF)
+
+
+def tie(*values):
+    return lax.optimization_barrier(values)
 
 
 def local_plane(block_in, out_grad, segment_ids, w_qkv, w_out, w_up, w_down, *vecs):
@@ -409,112 +457,171 @@
     y_index = d_index // 4
     width = block_in.shape[1]
     sub = width // 2
-
-    pack = jnp.concatenate(
+    rows_d = width // 8
+
+    mean_one = jnp.mean(block_in, axis=-1, keepdims=True)
+    center = block_in - mean_one
+    inv_one = lax.rsqrt(jnp.mean(center * center, axis=-1, keepdims=True) + NORM_EPS)
+    hat_low = relocate((center * inv_one).astype(BF))
+    stats = relocate(jnp.concatenate([mean_one.reshape(1, -1), inv_one.reshape(1, -1)], axis=0))
+    segs = relocate(segment_ids)
+
+    heads = jnp.concatenate(
         [
             w_qkv.reshape(3, -1, 4, HD).transpose(2, 1, 0, 3).reshape(4, -1, 3 * HD),
             w_out.reshape(4, HD, -1).transpose(0, 2, 1),
+        ],
+        axis=2,
+    )
+    heads = lax.all_to_all(jnp.concatenate([heads, heads], axis=0), "dp", 0, 0, tiled=True)
+    heads, *vecs = tie(heads, *vecs)
+    gain_one, shift_one, qv_all, out_shift, gain_two, shift_two, up_all, down_shift = (
+        gather_vectors(vecs, n_dev)
+    )
+    hat_low, stats, segs, gain_one = tie(hat_low, stats, segs, gain_one)
+    hids = jnp.concatenate(
+        [
             w_up.reshape(w_up.shape[0], 4, -1).transpose(1, 0, 2),
             w_down.reshape(4, -1, w_down.shape[1]).transpose(0, 2, 1),
         ],
         axis=2,
     )
-    pack = exchange_t(pack).reshape(sub, -1)
-    heads = gather_yz(pack[:, : 4 * HD], y_index)
-    hids = gather_yz(pack[:, 4 * HD :], y_index)
-    heads = heads.reshape(2, 2, 2, sub, 4, HD).transpose(0, 3, 1, 4, 2, 5)
+    hids, shift_one = tie(hids, shift_one)
+    hids = exchange_t(hids).reshape(sub, -1)
+    mine, other = gather_yz(hids)
+    heads = lax.all_gather(heads.reshape(width, 4 * HD), "mp", axis=0, tiled=False)
+    heads = heads.reshape(2, 2, width, 4, HD).transpose(2, 0, 3, 1, 4)
     heads = heads.reshape(width, 2, 4, 2 * HD)
     w_local = heads[:, :, :3].reshape(width, -1)
     w_out_t = heads[:, :, 3].reshape(width, -1)
-    units = hids.shape[3] // 2
-    up_local = hids[..., :units].transpose(0, 2, 1, 3).reshape(width, -1)
-    down_t = hids[..., units:].transpose(0, 2, 1, 3).reshape(width, -1)
-
-    gain_one, shift_one, qv_all, out_shift, gain_two, shift_two, up_all, down_shift = (
-        gather_vectors(vecs, n_dev)
-    )
+    units = hids.shape[1] // 2
+    up_local = by_y([m[:, :units] for m in mine], [m[:, :units] for m in other], y_index)
+    down_t = by_y([m[:, units:] for m in mine], [m[:, units:] for m in other], y_index)
+
     qv_mine = lax.dynamic_index_in_dim(qv_all.reshape(2, 4, 4, HD), t_index, 2, False)
     qv_mine = qv_mine.reshape(2, -1)
     b_local = pair_columns([qv_mine[0], jnp.zeros_like(qv_mine[0]), qv_mine[1]])
-    up_shift = lax.dynamic_index_in_dim(up_all.reshape(4, 4, -1), t_index, 1, False).reshape(-1)
+    up_shift = lax.dynamic_index_in_dim(up_all.reshape(4, 4, -1), t_index, 1, False)
+    z_order = jnp.arange(4, dtype=jnp.int32) ^ lax.axis_index("mp")
+    up_shift = up_shift[z_order].reshape(-1)
     slopes = head_slopes(4 * jnp.arange(4, dtype=jnp.int32) + t_index)
     chunk = jnp.asarray(CHUNK_OF_T, jnp.int32)[t_index]
     order = jnp.asarray(T_OF_CHUNK, jnp.int32)[jnp.arange(4, dtype=jnp.int32) ^ chunk]
 
-    hat_one, inv_one = norm_rows(block_in)
-    rows_one = gather_t(relocate((hat_one * gain_one + shift_one).astype(BF)))
-    segs = relocate(segment_ids)
-    block_here = relocate(block_in.astype(BF)).astype(F32)
-    grad_low = relocate(out_grad.astype(BF))
+    out_low, hat_low = tie(out_grad.astype(BF), hat_low)
+    hat_one = hat_low.astype(F32)
+    mean_here, inv_here = stats[0][:, None], stats[1][:, None]
+    block_here = hat_one * (1.0 / inv_here) + mean_here
+    rows_one = gather_t((hat_one * gain_one + shift_one).astype(BF))
+    grad_low, rows_one = tie(relocate(out_low), rows_one)
+    grad_rows = gather_t(grad_low)
     grad_here = grad_low.astype(F32)
-    grad_rows = gather_t(grad_low)
 
     qkv = (dot(rows_one, w_local) + b_local).astype(BF).reshape(4, -1, w_local.shape[1])
     att, lse = attn_fwd(order, slopes, segs, qkv)
+    att, grad_rows = tie(att, grad_rows)
     att_rows = att.reshape(-1, att.shape[2])
     resid = block_here + scatter_t(trans_dot(att_rows, w_out_t)) + out_shift
     hat_two, inv_two = norm_rows(resid)
     rows_two = gather_t((hat_two * gain_two + shift_two).astype(BF))
     value, slope = gelu_both(dot(rows_two, up_local) + up_shift)
     hidden = value.astype(BF)
+    g_down = cross_dot(grad_rows, hidden).astype(BF)
     pre_grad = dot(grad_rows, down_t) * slope
     pre_low = pre_grad.astype(BF)
-    two_grad = scatter_t(trans_dot(pre_low, up_local))
+    two_part = trans_dot(pre_low, up_local).astype(BF)
+    own, near, far = scatter_near(two_part)
+
+    far, pre_low = tie(far, pre_low)
+    g_up = cross_dot(rows_two, pre_low).astype(BF)
+
+    def to_y(grad):
+        halves = grad[:sub], grad[sub:]
+        keep = jnp.where(y_index == 0, *halves)
+        send = jnp.where(y_index == 0, halves[1], halves[0])
+        return keep, swap(send, 4)
+
+    def to_z(keep, got):
+        both = (keep.astype(F32) + got.astype(F32)).astype(BF)
+        return send_z([both[:, k * units : (k + 1) * units] for k in range(4)])
+
+    down_keep, down_got = to_y(g_down)
+    up_keep, up_got = to_y(g_up)
+    two_grad, up_keep = tie(scatter_far(own, near, far), up_keep)
+
     resid_grad = grad_here + norm_back(two_grad, hat_two, inv_two, gain_two)
     resid_low = resid_grad.astype(BF)
-    resid_rows = gather_t(resid_low)
-
-    block_out = resid + scatter_t(trans_dot(hidden, down_t)) + down_shift
-    block_out = bring_back(block_out.astype(BF)).astype(F32)
-    resid_back = bring_back(resid_low).astype(F32)
-
-    g_up = cross_dot(rows_two, pre_low).astype(BF).reshape(2, sub, 4, units)
-    g_down = cross_dot(grad_rows, hidden).astype(BF).reshape(2, sub, 4, units)
-    g_hid = jnp.concatenate([g_up, g_down], axis=3).transpose(0, 2, 1, 3)
-    g_hid = scatter_yz(g_hid, y_index).reshape(4, sub // 4, 2 * units)
-    g_hid = exchange_t(g_hid).astype(F32)
-    up_share = g_hid[..., :units].transpose(1, 0, 2).reshape(w_up.shape)
-    down_share = g_hid[..., units:].transpose(0, 2, 1).reshape(w_down.shape)
+    resid_low, hidden = tie(resid_low, hidden)
+    down_part = trans_dot(hidden, down_t).astype(BF)
+    resid_rows, down_part = gather_t(resid_low, down_part)
+    resid_rows, down_got = tie(resid_rows, down_got)
+    down_parts = to_z(down_keep, down_got)
+    block_sum = scatter_t(down_part)
+    block_low = (resid + block_sum + down_shift).astype(BF)
 
     att_grad = dot(resid_rows, w_out_t).astype(BF).reshape(att.shape)
     d_qkv, sums = attn_bwd(order, slopes, segs, qkv, att, att_grad, lse)
     d_rows = d_qkv.reshape(-1, d_qkv.shape[2])
-    one_grad = bring_back(scatter_t(trans_dot(d_rows, w_local)).astype(BF)).astype(F32)
-    in_grad = resid_back + norm_back(one_grad, hat_one, inv_one, gain_one)
-
-    g_qkv = cross_dot(rows_one, d_rows).astype(BF).reshape(2, sub, 2, 3, 2, HD)
-    g_out = cross_dot(resid_rows, att_rows).astype(BF).reshape(2, sub, 2, 1, 2, HD)
-    g_head = jnp.concatenate([g_qkv, g_out], axis=3).transpose(0, 2, 4, 1, 3, 5)
-    g_head = scatter_yz(g_head.reshape(2, 4, sub, 4 * HD), y_index)
-    g_head = exchange_t(g_head.reshape(4, sub // 4, 4 * HD)).astype(F32)
-    g_head = g_head.reshape(4, sub // 4, 4, HD)
-    qkv_share = g_head[:, :, :3].transpose(2, 1, 0, 3).reshape(w_qkv.shape)
-    out_share = g_head[:, :, 3].transpose(0, 2, 1).reshape(w_out.shape)
+    one_part = trans_dot(d_rows, w_local).astype(BF)
+    one_part, d_rows, block_low = tie(one_part, d_rows, block_low)
+    own, near, far = scatter_near(one_part)
+    far, up_got = tie(far, up_got)
+    up_parts = to_z(up_keep, up_got)
+
+    block_back = bring_back(block_low)
+    g_qkv = cross_dot(rows_one, d_rows).astype(BF)
+    g_qkv = g_qkv.reshape(2, 4, rows_d, 2, 3, 2, HD)
+    g_out = cross_dot(resid_rows, att_rows).astype(BF).reshape(2, 4, rows_d, 2, 1, 2, HD)
+    g_head = jnp.concatenate([g_qkv, g_out], axis=4).transpose(0, 1, 3, 5, 2, 4, 6)
+    g_head = g_head.reshape(n_dev, rows_d, 4 * HD)
+    one_grad = scatter_far(own, near, far)
+    one_grad, block_back, *down_parts = tie(one_grad, block_back, *down_parts)
+    in_grad = resid_grad + norm_back(one_grad, hat_one, inv_here, gain_one)
+    in_back = bring_back(in_grad.astype(BF))
+    in_back, *parts = tie(in_back, *up_parts, *down_parts)
+    g_hid = jnp.concatenate([total_z(parts[:4]), total_z(parts[4:])], axis=1)
+    g_hid = exchange_swaps(g_hid.reshape(4, rows_d, 2 * units), t_index).astype(F32)
 
     mine = jnp.arange(4, dtype=jnp.int32) == t_index
     qv_part = sums.transpose(1, 0, 2).reshape(2, 4, 1, HD)
     qv_place = jnp.where(mine[None, None, :, None], qv_part, 0.0).reshape(2, width)
-    up_part = jnp.sum(pre_grad, axis=0).reshape(4, 1, units)
+    up_part = jnp.sum(pre_grad, axis=0).reshape(4, units)[z_order][:, None, :]
     up_place = jnp.where(mine[None, :, None], up_part, 0.0).reshape(-1)
-    shares = scatter_vectors(
-        [
-            jnp.sum(one_grad * hat_one, axis=0),
-            jnp.sum(one_grad, axis=0),
-            qv_place,
-            jnp.sum(resid_grad, axis=0),
-            jnp.sum(two_grad * hat_two, axis=0),
-            jnp.sum(two_grad, axis=0),
-            up_place,
-            jnp.sum(out_grad, axis=0),
-        ],
-        n_dev,
-    )
-    return (block_out, in_grad, qkv_share, out_share, up_share, down_share, *shares)
+    sums = [
+        jnp.sum(one_grad * hat_one, axis=0),
+        jnp.sum(one_grad, axis=0),
+        qv_place,
+        jnp.sum(resid_grad, axis=0),
+        jnp.sum(two_grad * hat_two, axis=0),
+        jnp.sum(two_grad, axis=0),
+        up_place,
+        jnp.sum(out_grad, axis=0),
+    ]
+    rows, shapes = cut_vectors(sums, n_dev)
+    rows_hi = rows.astype(BF)
+    rows_lo = (rows - rows_hi.astype(F32)).astype(BF)
+    n_vec = rows.shape[1]
+    rows = jnp.concatenate([rows_hi, rows_lo], axis=1)
+    rows = jnp.pad(rows, ((0, 0), (0, 16 * 4 * HD - 2 * n_vec))).reshape(n_dev, 16, 4 * HD)
+    g_head = lax.all_to_all(jnp.concatenate([g_head, rows], axis=1), ("dp", "mp"), 0, 0, tiled=True)
+    flat = jnp.sum(g_head[:, rows_d:].reshape(n_dev, -1)[:, : 2 * n_vec].astype(F32), axis=0)
+    shares = share_vectors(flat[:n_vec] + flat[n_vec:], shapes)
+    g_head = g_head[:, :rows_d]
+    g_head = jnp.sum(g_head.reshape(2, 4, 4, rows_d, 4, HD).astype(F32), axis=(0, 2))
+    qkv_share = g_head[:, :, :3].transpose(2, 1, 0, 3).reshape(w_qkv.shape)
+    out_share = g_head[:, :, 3].transpose(0, 2, 1).reshape(w_out.shape)
+
+    up_share = g_hid[..., :units].transpose(1, 0, 2).reshape(w_up.shape)
+    down_share = g_hid[..., units:].transpose(0, 2, 1).reshape(w_down.shape)
+
+    block_out = block_back.astype(F32)
+    return (block_out, in_back.astype(F32), qkv_share, out_share, up_share, down_share, *shares)
 
 
 def solution(mesh):
     n_dp, n_mp = mesh.shape["dp"], mesh.shape["mp"]
-    local = local_plane if (n_dp, n_mp) == (8, 4) else local_any(n_dp, n_mp)
+    plane = (n_dp, n_mp) == (8, 4)
+    local = local_plane if plane else local_any(n_dp, n_mp)
     both = ("dp", "mp")
     weights = (P(None, "dp", "mp"), P("mp", "dp"), P("dp", "mp"), P("mp", "dp"))
     vectors = (P(both), P(both), P(None, both), P(both), P(both), P(both), P(both), P(both))

time: 574 us -> 530 us (0.923)
  the two profiles are of different devices: /device:TPU:0 before, /device:TPU:19 now
where the time goes in v2:
time: 530 us; the launch traced here: 519 us
  waiting for transfers between devices  204 us (38%)
  starting transfers between devices  113 us (21%)
  local copies, waits for them, and re-layouts  62.3 us (12%)
  other arithmetic  53.7 us (10%)
  matrix products  42.8 us (8%)
  Pallas kernels  27.9 us (5%)
  between operations  15.4 us (3%)
    ppermute x9, waiting for transfers between devices, across(): return lax.ppermute(x, 'mp', [(i, i ^ bits) for i in range(4)])  123 us
    ppermute x29, starting transfers between devices, swap(): return lax.ppermute(x, 'dp', [(i, i ^ bits) for i in range(8)])  70.5 us
    ppermute x29, waiting for transfers between devices, swap(): return lax.ppermute(x, 'dp', [(i, i ^ bits) for i in range(8)])  64 us
    dot_general x4, matrix products, trans_dot(): lax.dot_general(left, right, (((1,), (1,)), ((), ())), preferred_element_...  15.4 us
    pallas_call x1, Pallas kernels, attn_bwd(): pl.pallas_call(lambda *refs: attn_bwd_kernel(*refs, nb=nb, rb=rb), grid=(...  15.3 us
    dot_general x4, matrix products, dot(): return jnp.dot(left, right, preferred_element_type=F32)  14.3 us
    dot_general x4, matrix products, cross_dot(): lax.dot_general(left, right, (((0,), (0,)), ((), ())), preferred_element_...  13.1 us
    pallas_call x1, Pallas kernels, attn_fwd(): pl.pallas_call(lambda *refs: attn_fwd_kernel(*refs, nb=nb, rb=rb), grid=(...  12.6 us
  transfers between devices with their start and end apart: 49, of which 19 were waited for; matrix products, arithmetic and copies ran while one was open for 18% of the time, Pallas kernels for 3%

profile of v2, /device:TPU:19, one launch (start us, length us, event | category | flops | bytes accessed | tf_op | source)
XLA Modules:
  0.0 519.4 jit_solution(10650551118043608815)
XLA Ops:
  10.2 4.5 all-to-all-start
  21.3 12.2 %all-to-all-done = bf16[8,128,256]{1,2,0:T(8,128)(2,1)S(1)} async-done(((bf16[8,128,256]{1,2,0:T(8,128)(2,1)}), bf16[8,128,256]{1,2,0:T(8,128)(2,1)S(1)}, u32[]{:S(2)}, u32[]{:S(2)}) %all-to-all-start) | async-done | bytes 524320 | tf_op jit(solution)/shard_map/all_to_all | solution.py:476
  34.3 6.3 %all-to-all-start.1 = ((f32[32,1,384]{2,1,0:T(1,128)}), f32[32,1,384]{2,1,0:T(1,128)S(1)}, u32[]{:S(2)}, u32[]{:S(2)}) async-start(f32[32,1,384]{2,1,0:T(1,128)} %broadcast_in_dim.72), calls=%async_computation.1 | async-start | bytes 98304 | tf_op jit(solution)/shard_map/all_to_all | solution.py:230
  47.9 12.4 %collective-permute-done.5 = bf16[288,1024]{1,0:T(8,128)(2,1)S(1)} collective-permute-done((bf16[288,1024]{1,0:T(8,128)(2,1)S(1)}, bf16[288,1024]{1,0:T(8,128)(2,1)S(1)}, u32[]{:S(2)}, u32[]{:S(2)}) %collective-permute-start.5) | collective-permute-done | bytes 589856 | tf_op jit(solution)/shard_map/ppermute | solution.py:377
  65.0 41.1 %collective-permute-start.8 = (bf16[288,1024]{1,0:T(8,128)(2,1)S(1)}, bf16[288,1024]{1,0:T(8,128)(2,1)S(1)}, u32[]{:S(2)}, u32[]{:S(2)}) collective-permute-start(bf16[288,1024]{1,0:T(8,128)(2,1)S(1)} %collective-permute-done.3), channel_id=1, source_target_pairs={{0,8},{4,12},{8,0},{12,4},{16,24},{20,28},{24,16},{28,20},{1,9},{5... | collective-permute-start | bytes 1769480 | tf_op jit(solution)/shard_map/ppermute | solution.py:377
  106.1 10.1 %collective-permute-done.8 = bf16[288,1024]{1,0:T(8,128)(2,1)S(1)} collective-permute-done((bf16[288,1024]{1,0:T(8,128)(2,1)S(1)}, bf16[288,1024]{1,0:T(8,128)(2,1)S(1)}, u32[]{:S(2)}, u32[]{:S(2)}) %collective-permute-start.8) | collective-permute-done | bytes 589856 | tf_op jit(solution)/shard_map/ppermute | solution.py:377
  123.7 4.0 copy.84
  135.2 12.6 %attn_fwd.1 = (bf16[4,288,256]{2,1,0:T(8,128)(2,1)}, f32[2,2,1152]{2,1,0:T(2,128)}) custom-call(s32[4]{0:T(128)} %gather_fusion, f32[4]{0:T(128)} %multiply_exponential_fusion.refs_1_, s32[1,1152]{1,0:T(1,128)} %reshape.332.refs_2_, s32[1152,1]{1,0:T(8,128)} %reshape.398.refs_3_, bf16[4,288,768]{2,1,0:T(8,128)(2,1)} %bitcast.152, ...), custom_call_target="tpu_custom_call" | custom-call | flops 2717908992 | bytes 16777216 | tf_op jit(solution)/shard_map/attn_fwd/pallas_call | solution.py:184
  147.8 3.9 fusion.51
  153.4 3.6 all-to-all-start.2
  170.0 17.6 %collective-permute-done.12 = bf16[512,512]{1,0:T(8,128)(2,1)S(1)} collective-permute-done((bf16[512,512]{1,0:T(8,128)(2,1)S(1)}, bf16[512,512]{1,0:T(8,128)(2,1)S(1)}, u32[]{:S(2)}, u32[]{:S(2)}) %collective-permute-start.12) | collective-permute-done | bytes 524320 | tf_op jit(solution)/shard_map/ppermute | solution.py:425
  191.5 10.3 %collective-permute-done.13 = bf16[512,512]{1,0:T(8,128)(2,1)S(1)} collective-permute-done((bf16[512,512]{1,0:T(8,128)(2,1)S(1)}, bf16[512,512]{1,0:T(8,128)(2,1)S(1)}, u32[]{:S(2)}, u32[]{:S(2)}) %collective-permute-start.13) | collective-permute-done | bytes 524320 | tf_op jit(solution)/shard_map/ppermute | solution.py:425
  202.8 11.3 %collective-permute-done.14 = bf16[512,512]{1,0:T(8,128)(2,1)S(1)} collective-permute-done((bf16[512,512]{1,0:T(8,128)(2,1)S(1)}, bf16[512,512]{1,0:T(8,128)(2,1)S(1)}, u32[]{:S(2)}, u32[]{:S(2)}) %collective-permute-start.14) | collective-permute-done | bytes 524320 | tf_op jit(solution)/shard_map/ppermute | solution.py:425
  221.5 9.6 %collective-permute-done.20 = bf16[288,1024]{1,0:T(8,128)(2,1)S(1)} collective-permute-done((bf16[288,1024]{1,0:T(8,128)(2,1)S(1)}, bf16[288,1024]{1,0:T(8,128)(2,1)S(1)}, u32[]{:S(2)}, u32[]{:S(2)}) %collective-permute-start.20) | collective-permute-done | bytes 589856 | tf_op jit(solution)/shard_map/ppermute | solution.py:377
  238.8 5.8 %fusion.33 = (f32[1024]{0:T(1024)}, bf16[1152,1024]{1,0:T(8,128)(2,1)S(1)}) fusion(f32[1152,1024]{1,0:T(8,128)S(1)} %get-tuple-element.248, bf16[1152,1024]{1,0:T(8,128)(2,1)S(1)} %copy-done.5, bf16[512,1024]{1,0:T(8,128)(2,1)S(1)} %get-tuple-element.197, bf16[512,1024]{1,0:T(8,128)(2,1)S(1)} %get-tuple-element.196), kind=kOutput, calls=%fused_computation.146 | convolution fusion | flops 2443705344 | bytes 11538432 | tf_op jit(solution)/shard_map/dot_general | solution.py:48
  244.6 3.8 convolution_convert_fusion.2
  258.7 8.5 %collective-permute-done.23 = bf16[288,1024]{1,0:T(8,128)(2,1)S(1)} collective-permute-done((bf16[288,1024]{1,0:T(8,128)(2,1)S(1)}, bf16[288,1024]{1,0:T(8,128)(2,1)S(1)}, u32[]{:S(2)}, u32[]{:S(2)}) %collective-permute-start.23) | collective-permute-done | bytes 589856 | tf_op jit(solution)/shard_map/ppermute | solution.py:377
  274.6 3.8 convolution_convert_fusion.1
  278.4 5.5 %collective-permute-done.25 = bf16[288,1024]{1,0:T(8,128)(2,1)} collective-permute-done((bf16[288,1024]{1,0:T(8,128)(2,1)S(1)}, bf16[288,1024]{1,0:T(8,128)(2,1)}, u32[]{:S(2)}, u32[]{:S(2)}) %collective-permute-start.25) | collective-permute-done | bytes 589856 | tf_op jit(solution)/shard_map/ppermute | solution.py:377
  299.4 15.3 %attn_bwd.1 = (bf16[4,288,768]{2,1,0:T(8,128)(2,1)}, f32[2,2,128]{2,1,0:T(2,128)}) custom-call(s32[4]{0:T(128)} %gather_fusion, f32[4]{0:T(128)} %multiply_exponential_fusion.refs_1_, s32[1,1152]{1,0:T(1,128)} %reshape.332.refs_2_, s32[1152,1]{1,0:T(8,128)} %reshape.398.refs_3_, bf16[4,288,768]{2,1,0:T(8,128)(2,1)} %bitcast.155, ...), custom_call_target="tpu_custom_call" | custom-call | flops 5435817984 | bytes 33554432 | tf_op jit(solution)/shard_map/attn_bwd/pallas_call | solution.py:206
  314.7 3.9 convolution_convert_fusion
  337.4 5.9 %collective-permute-start.33 = (bf16[288,1024]{1,0:T(8,128)(2,1)}, bf16[288,1024]{1,0:T(8,128)(2,1)}, u32[]{:S(2)}, u32[]{:S(2)}) collective-permute-start(bf16[288,1024]{1,0:T(8,128)(2,1)} %add_convert_fusion.3), channel_id=1, source_target_pairs={{0,0},{8,1},{12,2},{4,3},{3,4},{11,5},{15,6},{7,7},{1,8},{9,9},{13... | collective-permute-start | bytes 1769480 | tf_op jit(solution)/shard_map/ppermute | solution.py:385
  344.8 6.6 %collective-permute-done.31 = bf16[512,1024]{1,0:T(8,128)(2,1)} collective-permute-done((bf16[512,1024]{1,0:T(8,128)(2,1)}, bf16[512,1024]{1,0:T(8,128)(2,1)}, u32[]{:S(2)}, u32[]{:S(2)}) %collective-permute-start.31) | collective-permute-done | bytes 1048608 | tf_op jit(solution)/shard_map/ppermute | solution.py:377
  352.9 5.7 %convolution_convert_fusion.6 = bf16[1024,768]{1,0:T(8,128)(2,1)} fusion(bf16[1152,1024]{1,0:T(8,128)(2,1)} %pad_maximum_fusion.1, bf16[1152,768]{1,0:T(8,128)(2,1)} %bitcast.159), kind=kOutput, calls=%fused_computation.38 | convolution fusion | flops 1812725760 | bytes 5701632 | tf_op jit(solution)/shard_map/dot_general | solution.py:52
  361.3 3.8 reshape.346
  369.8 5.4 %collective-permute-done.32 = bf16[288,1024]{1,0:T(8,128)(2,1)} collective-permute-done((bf16[288,1024]{1,0:T(8,128)(2,1)S(1)}, bf16[288,1024]{1,0:T(8,128)(2,1)}, u32[]{:S(2)}, u32[]{:S(2)}) %collective-permute-start.32) | collective-permute-done | bytes 589856 | tf_op jit(solution)/shard_map/ppermute | solution.py:377
  379.6 5.3 %pad_maximum_fusion = bf16[32,144,256]{1,2,0:T(8,128)(2,1)} fusion(bf16[32,16,256]{1,2,0:T(8,128)(2,1)} %copy.97, bf16[32,128,256]{1,2,0:T(8,128)(2,1)} %bitcast.110), kind=kLoop, calls=%fused_computation.14 | loop fusion | flops 4718592 | bytes 4718592 | tf_op jit(solution)/shard_map/concatenate | solution.py:606
  384.9 5.7 %copy.98 = bf16[32,144,256]{2,1,0:T(8,128)(2,1)} copy(bf16[32,144,256]{1,2,0:T(8,128)(2,1)} %pad_maximum_fusion) | data formatting | bytes 4718592 | tf_op jit(solution)/shard_map/concatenate | solution.py:606
  390.6 6.8 %all-to-all-start.3 = ((bf16[32,144,256]{2,1,0:T(8,128)(2,1)}), bf16[32,144,256]{2,1,0:T(8,128)(2,1)}, u32[]{:S(2)}, u32[]{:S(2)}) async-start(bf16[32,144,256]{2,1,0:T(8,128)(2,1)} %copy.98), calls=%async_computation.3 | async-start | bytes 4718592 | tf_op jit(solution)/shard_map/all_to_all | solution.py:606
  405.1 50.8 %collective-permute-done.38 = bf16[512,256]{1,0:T(8,128)(2,1)S(1)} collective-permute-done((bf16[512,256]{1,0:T(8,128)(2,1)}, bf16[512,256]{1,0:T(8,128)(2,1)S(1)}, u32[]{:S(2)}, u32[]{:S(2)}) %collective-permute-start.38) | collective-permute-done | bytes 262176 | tf_op jit(solution)/shard_map/ppermute | solution.py:425
  455.9 17.5 %collective-permute-done.39 = bf16[512,256]{1,0:T(8,128)(2,1)S(1)} collective-permute-done((bf16[512,256]{1,0:T(8,128)(2,1)S(1)}, bf16[512,256]{1,0:T(8,128)(2,1)S(1)}, u32[]{:S(2)}, u32[]{:S(2)}) %collective-permute-start.39) | collective-permute-done | bytes 262176 | tf_op jit(solution)/shard_map/ppermute | solution.py:425
  473.4 15.2 %collective-permute-done.40 = bf16[512,256]{1,0:T(8,128)(2,1)S(1)} collective-permute-done((bf16[512,256]{1,0:T(8,128)(2,1)S(1)}, bf16[512,256]{1,0:T(8,128)(2,1)S(1)}, u32[]{:S(2)}, u32[]{:S(2)}) %collective-permute-start.40) | collective-permute-done | bytes 262176 | tf_op jit(solution)/shard_map/ppermute | solution.py:425
  (333 shorter events, 169.1 us)
Async XLA Ops:
  10.2 23.3 %all-to-all-start = ((bf16[8,128,256]{1,2,0:T(8,128)(2,1)}), bf16[8,128,256]{1,2,0:T(8,128)(2,1)S(1)}, u32[]{:S(2)}, u32[]{:S(2)}) async-start(bf16[8,128,256]{1,2,0:T(8,128)(2,1)} %maximum_maximum_fusion), calls=%async_computation | async-start | bytes 1048576 | tf_op jit(solution)/shard_map/all_to_all | solution.py:476
  15.5 30.2 %collective-permute-start = (bf16[288,1024]{1,0:T(8,128)(2,1)S(1)}, bf16[288,1024]{1,0:T(8,128)(2,1)S(1)}, u32[]{:S(2)}, u32[]{:S(2)}) collective-permute-start(bf16[288,1024]{1,0:T(8,128)(2,1)S(1)} %multiply_convert_fusion.1), channel_id=1, source_target_pairs={{0,0},{1,8},{2,12},{3,4},{4,3},{5,11},{6,15},{7,7},{8,1},{9,9},{10... | collective-permute-start | bytes 1769480 | tf_op jit(solution)/shard_map/ppermute | solution.py:381
  16.2 29.4 %collective-permute-start.1 = (f32[2,288]{1,0:T(2,128)S(1)}, f32[2,288]{1,0:T(2,128)S(1)}, u32[]{:S(2)}, u32[]{:S(2)}) collective-permute-start(f32[2,288]{1,0:T(2,128)S(1)} %pad_maximum_fusion.25), channel_id=1, source_target_pairs={{0,0},{1,8},{2,12},{3,4},{4,3},{5,11},{6,15},{7,7},{8,1},{9,9},{10... | collective-permute-start | bytes 6920 | tf_op jit(solution)/shard_map/ppermute | solution.py:381
  16.9 28.8 %collective-permute-start.2 = (s32[1152]{0:T(1024)S(1)}, s32[1152]{0:T(1024)S(1)}, u32[]{:S(2)}, u32[]{:S(2)}) collective-permute-start(s32[1152]{0:T(1024)S(1)} %copy-done.39), channel_id=1, source_target_pairs={{0,0},{1,8},{2,12},{3,4},{4,3},{5,11},{6,15},{7,7},{8,1},{9,9},{10... | collective-permute-start | bytes 13832 | tf_op jit(solution)/shard_map/ppermute | solution.py:381
  40.7 83.0 %all-gather.2.cloned.1.call-start = ((), (), s32[]{:S(2)}) async-start(), calls=%async_computation.4 | async-start | bytes 2621440 | tf_op jit(solution)/shard_map/all_gather | solution.py:492
  46.9 16.5 %collective-permute-start.4 = (bf16[288,1024]{1,0:T(8,128)(2,1)S(1)}, bf16[288,1024]{1,0:T(8,128)(2,1)S(1)}, u32[]{:S(2)}, u32[]{:S(2)}) collective-permute-start(bf16[288,1024]{1,0:T(8,128)(2,1)S(1)} %fusion.7), channel_id=1, source_target_pairs={{0,4},{4,0},{8,12},{12,8},{16,20},{20,16},{24,28},{28,24},{1,5},{5... | collective-permute-start | bytes 1769480 | tf_op jit(solution)/shard_map/ppermute | solution.py:377
  65.0 51.3 %collective-permute-start.8 = (bf16[288,1024]{1,0:T(8,128)(2,1)S(1)}, bf16[288,1024]{1,0:T(8,128)(2,1)S(1)}, u32[]{:S(2)}, u32[]{:S(2)}) collective-permute-start(bf16[288,1024]{1,0:T(8,128)(2,1)S(1)} %collective-permute-done.3), channel_id=1, source_target_pairs={{0,8},{4,12},{8,0},{12,4},{16,24},{20,28},{24,16},{28,20},{1,9},{5... | collective-permute-start | bytes 1769480 | tf_op jit(solution)/shard_map/ppermute | solution.py:377
  106.1 15.8 %collective-permute-start.7 = (bf16[288,1024]{1,0:T(8,128)(2,1)S(1)}, bf16[288,1024]{1,0:T(8,128)(2,1)S(1)}, u32[]{:S(2)}, u32[]{:S(2)}) collective-permute-start(bf16[288,1024]{1,0:T(8,128)(2,1)S(1)} %collective-permute-done.3), channel_id=1, source_target_pairs={{0,4},{4,0},{8,12},{12,8},{16,20},{20,16},{24,28},{28,24},{1,5},{5... | collective-permute-start | bytes 1769480 | tf_op jit(solution)/shard_map/ppermute | solution.py:377
  152.9 35.5 %collective-permute-start.10 = (bf16[576,1024]{1,0:T(8,128)(2,1)}, bf16[576,1024]{1,0:T(8,128)(2,1)S(1)}, u32[]{:S(2)}, u32[]{:S(2)}) collective-permute-start(bf16[576,1024]{1,0:T(8,128)(2,1)} %pad_maximum_fusion.11), channel_id=1, source_target_pairs={{0,4},{4,0},{8,12},{12,8},{16,20},{20,16},{24,28},{28,24},{1,5},{5... | collective-permute-start | bytes 3538952 | tf_op jit(solution)/shard_map/ppermute | solution.py:377
  163.6 23.9 %collective-permute-start.12 = (bf16[512,512]{1,0:T(8,128)(2,1)S(1)}, bf16[512,512]{1,0:T(8,128)(2,1)S(1)}, u32[]{:S(2)}, u32[]{:S(2)}) collective-permute-start(bf16[512,512]{1,0:T(8,128)(2,1)S(1)} %bitcast.114), channel_id=1, source_target_pairs={{0,1},{1,0},{2,3},{3,2},{4,5},{5,4},{6,7},{7,6},{8,9},{9,8},{10,11... | collective-permute-start | bytes 1572872 | tf_op jit(solution)/shard_map/ppermute | solution.py:425
  167.5 34.4 %collective-permute-start.13 = (bf16[512,512]{1,0:T(8,128)(2,1)S(1)}, bf16[512,512]{1,0:T(8,128)(2,1)S(1)}, u32[]{:S(2)}, u32[]{:S(2)}) collective-permute-start(bf16[512,512]{1,0:T(8,128)(2,1)S(1)} %bitcast.115), channel_id=1, source_target_pairs={{0,2},{1,3},{2,0},{3,1},{4,6},{5,7},{6,4},{7,5},{8,10},{9,11},{10,... | collective-permute-start | bytes 1572872 | tf_op jit(solution)/shard_map/ppermute | solution.py:425
  168.6 45.5 %collective-permute-start.14 = (bf16[512,512]{1,0:T(8,128)(2,1)S(1)}, bf16[512,512]{1,0:T(8,128)(2,1)S(1)}, u32[]{:S(2)}, u32[]{:S(2)}) collective-permute-start(bf16[512,512]{1,0:T(8,128)(2,1)S(1)} %bitcast.116), channel_id=1, source_target_pairs={{0,3},{1,2},{2,1},{3,0},{4,7},{5,6},{6,5},{7,4},{8,11},{9,10},{10,... | collective-permute-start | bytes 1572872 | tf_op jit(solution)/shard_map/ppermute | solution.py:425
  169.0 50.3 %collective-permute-start.15 = (bf16[512,512]{1,0:T(8,128)(2,1)S(1)}, bf16[512,512]{1,0:T(8,128)(2,1)S(1)}, u32[]{:S(2)}, u32[]{:S(2)}) collective-permute-start(bf16[512,512]{1,0:T(8,128)(2,1)S(1)} %bitcast.117), channel_id=1, source_target_pairs={{0,16},{4,20},{8,24},{12,28},{16,0},{20,4},{24,8},{28,12},{1,17},{... | collective-permute-start | bytes 1572872 | tf_op jit(solution)/shard_map/ppermute | solution.py:377
  187.6 31.8 %collective-permute-start.16 = (bf16[512,512]{1,0:T(8,128)(2,1)S(1)}, bf16[512,512]{1,0:T(8,128)(2,1)S(1)}, u32[]{:S(2)}, u32[]{:S(2)}) collective-permute-start(bf16[512,512]{1,0:T(8,128)(2,1)S(1)} %collective-permute-done.12), channel_id=1, source_target_pairs={{0,16},{4,20},{8,24},{12,28},{16,0},{20,4},{24,8},{28,12},{1,17},{... | collective-permute-start | bytes 1572872 | tf_op jit(solution)/shard_map/ppermute | solution.py:377
  190.3 24.9 %collective-permute-start.11 = (bf16[288,1024]{1,0:T(8,128)(2,1)S(1)}, bf16[288,1024]{1,0:T(8,128)(2,1)S(1)}, u32[]{:S(2)}, u32[]{:S(2)}) collective-permute-start(bf16[288,1024]{1,0:T(8,128)(2,1)S(1)} %fusion.17), channel_id=1, source_target_pairs={{0,8},{4,12},{8,0},{12,4},{16,24},{20,28},{24,16},{28,20},{1,9},{5... | collective-permute-start | bytes 1769480 | tf_op jit(solution)/shard_map/ppermute | solution.py:377
  201.9 17.5 %collective-permute-start.17 = (bf16[512,512]{1,0:T(8,128)(2,1)S(1)}, bf16[512,512]{1,0:T(8,128)(2,1)S(1)}, u32[]{:S(2)}, u32[]{:S(2)}) collective-permute-start(bf16[512,512]{1,0:T(8,128)(2,1)S(1)} %collective-permute-done.13), channel_id=1, source_target_pairs={{0,16},{4,20},{8,24},{12,28},{16,0},{20,4},{24,8},{28,12},{1,17},{... | collective-permute-start | bytes 1572872 | tf_op jit(solution)/shard_map/ppermute | solution.py:377
  214.1 19.4 %collective-permute-start.18 = (bf16[512,512]{1,0:T(8,128)(2,1)S(1)}, bf16[512,512]{1,0:T(8,128)(2,1)S(1)}, u32[]{:S(2)}, u32[]{:S(2)}) collective-permute-start(bf16[512,512]{1,0:T(8,128)(2,1)S(1)} %collective-permute-done.14), channel_id=1, source_target_pairs={{0,16},{4,20},{8,24},{12,28},{16,0},{20,4},{24,8},{28,12},{1,17},{... | collective-permute-start | bytes 1572872 | tf_op jit(solution)/shard_map/ppermute | solution.py:377
  219.4 15.2 %collective-permute-start.19 = (bf16[288,1024]{1,0:T(8,128)(2,1)S(1)}, bf16[288,1024]{1,0:T(8,128)(2,1)S(1)}, u32[]{:S(2)}, u32[]{:S(2)}) collective-permute-start(bf16[288,1024]{1,0:T(8,128)(2,1)S(1)} %add_convert_fusion.6), channel_id=1, source_target_pairs={{0,4},{4,0},{8,12},{12,8},{16,20},{20,16},{24,28},{28,24},{1,5},{5... | collective-permute-start | bytes 1769480 | tf_op jit(solution)/shard_map/ppermute | solution.py:377
  272.4 23.8 %collective-permute-start.27 = (bf16[512,1024]{1,0:T(8,128)(2,1)}, bf16[512,1024]{1,0:T(8,128)(2,1)}, u32[]{:S(2)}, u32[]{:S(2)}) collective-permute-start(bf16[512,1024]{1,0:T(8,128)(2,1)} %broadcast_select_fusion.1), channel_id=1, source_target_pairs={{0,16},{4,20},{8,24},{12,28},{16,0},{20,4},{24,8},{28,12},{1,17},{... | collective-permute-start | bytes 3145736 | tf_op jit(solution)/shard_map/ppermute | solution.py:377
  273.1 18.6 %collective-permute-start.24 = (bf16[288,1024]{1,0:T(8,128)(2,1)S(1)}, bf16[288,1024]{1,0:T(8,128)(2,1)}, u32[]{:S(2)}, u32[]{:S(2)}) collective-permute-start(bf16[288,1024]{1,0:T(8,128)(2,1)S(1)} %convert_element_type.231), channel_id=1, source_target_pairs={{0,4},{4,0},{8,12},{12,8},{16,20},{20,16},{24,28},{28,24},{1,5},{5... | collective-permute-start | bytes 1769480 | tf_op jit(solution)/shard_map/ppermute | solution.py:377
  299.3 19.4 %collective-permute-start.29 = (bf16[288,1024]{1,0:T(8,128)(2,1)S(1)}, bf16[288,1024]{1,0:T(8,128)(2,1)}, u32[]{:S(2)}, u32[]{:S(2)}) collective-permute-start(bf16[288,1024]{1,0:T(8,128)(2,1)S(1)} %add_convert_fusion.4), channel_id=1, source_target_pairs={{0,8},{4,12},{8,0},{12,4},{16,24},{20,28},{24,16},{28,20},{1,9},{5... | collective-permute-start | bytes 1769480 | tf_op jit(solution)/shard_map/ppermute | solution.py:377
  326.4 25.0 %collective-permute-start.31 = (bf16[512,1024]{1,0:T(8,128)(2,1)}, bf16[512,1024]{1,0:T(8,128)(2,1)}, u32[]{:S(2)}, u32[]{:S(2)}) collective-permute-start(bf16[512,1024]{1,0:T(8,128)(2,1)} %get-tuple-element.194), channel_id=1, source_target_pairs={{0,16},{4,20},{8,24},{12,28},{16,0},{20,4},{24,8},{28,12},{1,17},{... | collective-permute-start | bytes 3145736 | tf_op jit(solution)/shard_map/ppermute | solution.py:377
  331.6 45.3 %collective-permute-start.34 = (bf16[512,256]{1,0:T(8,128)(2,1)}, bf16[512,256]{1,0:T(8,128)(2,1)}, u32[]{:S(2)}, u32[]{:S(2)}) collective-permute-start(bf16[512,256]{1,0:T(8,128)(2,1)} %get-tuple-element.210), channel_id=1, source_target_pairs={{0,1},{1,0},{2,3},{3,2},{4,5},{5,4},{6,7},{7,6},{8,9},{9,8},{10,11... | collective-permute-start | bytes 786440 | tf_op jit(solution)/shard_map/ppermute | solution.py:425
  331.6 45.4 %collective-permute-start.35 = (bf16[512,256]{1,0:T(8,128)(2,1)}, bf16[512,256]{1,0:T(8,128)(2,1)}, u32[]{:S(2)}, u32[]{:S(2)}) collective-permute-start(bf16[512,256]{1,0:T(8,128)(2,1)} %get-tuple-element.209), channel_id=1, source_target_pairs={{0,2},{1,3},{2,0},{3,1},{4,6},{5,7},{6,4},{7,5},{8,10},{9,11},{10,... | collective-permute-start | bytes 786440 | tf_op jit(solution)/shard_map/ppermute | solution.py:425
  333.7 43.2 %collective-permute-start.36 = (bf16[512,256]{1,0:T(8,128)(2,1)}, bf16[512,256]{1,0:T(8,128)(2,1)}, u32[]{:S(2)}, u32[]{:S(2)}) collective-permute-start(bf16[512,256]{1,0:T(8,128)(2,1)} %get-tuple-element.208), channel_id=1, source_target_pairs={{0,3},{1,2},{2,1},{3,0},{4,7},{5,6},{6,5},{7,4},{8,11},{9,10},{10,... | collective-permute-start | bytes 786440 | tf_op jit(solution)/shard_map/ppermute | solution.py:425
  337.4 39.5 %collective-permute-start.33 = (bf16[288,1024]{1,0:T(8,128)(2,1)}, bf16[288,1024]{1,0:T(8,128)(2,1)}, u32[]{:S(2)}, u32[]{:S(2)}) collective-permute-start(bf16[288,1024]{1,0:T(8,128)(2,1)} %add_convert_fusion.3), channel_id=1, source_target_pairs={{0,0},{8,1},{12,2},{4,3},{3,4},{11,5},{15,6},{7,7},{1,8},{9,9},{13... | collective-permute-start | bytes 1769480 | tf_op jit(solution)/shard_map/ppermute | solution.py:385
  351.4 23.7 %collective-permute-start.32 = (bf16[288,1024]{1,0:T(8,128)(2,1)S(1)}, bf16[288,1024]{1,0:T(8,128)(2,1)}, u32[]{:S(2)}, u32[]{:S(2)}) collective-permute-start(bf16[288,1024]{1,0:T(8,128)(2,1)S(1)} %add_convert_fusion.2), channel_id=1, source_target_pairs={{0,8},{4,12},{8,0},{12,4},{16,24},{20,28},{24,16},{28,20},{1,9},{5... | collective-permute-start | bytes 1769480 | tf_op jit(solution)/shard_map/ppermute | solution.py:377
  390.6 110.4 %all-to-all-start.3 = ((bf16[32,144,256]{2,1,0:T(8,128)(2,1)}), bf16[32,144,256]{2,1,0:T(8,128)(2,1)}, u32[]{:S(2)}, u32[]{:S(2)}) async-start(bf16[32,144,256]{2,1,0:T(8,128)(2,1)} %copy.98), calls=%async_computation.3 | async-start | bytes 4718592 | tf_op jit(solution)/shard_map/all_to_all | solution.py:606
  397.8 90.8 %collective-permute-start.37 = (bf16[288,1024]{1,0:T(8,128)(2,1)S(1)}, bf16[288,1024]{1,0:T(8,128)(2,1)S(1)}, u32[]{:S(2)}, u32[]{:S(2)}) collective-permute-start(bf16[288,1024]{1,0:T(8,128)(2,1)S(1)} %fusion.15), channel_id=1, source_target_pairs={{0,0},{8,1},{12,2},{4,3},{3,4},{11,5},{15,6},{7,7},{1,8},{9,9},{13... | collective-permute-start | bytes 1769480 | tf_op jit(solution)/shard_map/ppermute | solution.py:385
  401.1 54.8 %collective-permute-start.38 = (bf16[512,256]{1,0:T(8,128)(2,1)}, bf16[512,256]{1,0:T(8,128)(2,1)S(1)}, u32[]{:S(2)}, u32[]{:S(2)}) collective-permute-start(bf16[512,256]{1,0:T(8,128)(2,1)} %get-tuple-element.206), channel_id=1, source_target_pairs={{0,1},{1,0},{2,3},{3,2},{4,5},{5,4},{6,7},{7,6},{8,9},{9,8},{10,11... | collective-permute-start | bytes 786440 | tf_op jit(solution)/shard_map/ppermute | solution.py:425
  403.6 69.8 %collective-permute-start.39 = (bf16[512,256]{1,0:T(8,128)(2,1)S(1)}, bf16[512,256]{1,0:T(8,128)(2,1)S(1)}, u32[]{:S(2)}, u32[]{:S(2)}) collective-permute-start(bf16[512,256]{1,0:T(8,128)(2,1)S(1)} %get-tuple-element.205), channel_id=1, source_target_pairs={{0,2},{1,3},{2,0},{3,1},{4,6},{5,7},{6,4},{7,5},{8,10},{9,11},{10,... | collective-permute-start | bytes 786440 | tf_op jit(solution)/shard_map/ppermute | solution.py:425
  405.1 83.5 %collective-permute-start.40 = (bf16[512,256]{1,0:T(8,128)(2,1)S(1)}, bf16[512,256]{1,0:T(8,128)(2,1)S(1)}, u32[]{:S(2)}, u32[]{:S(2)}) collective-permute-start(bf16[512,256]{1,0:T(8,128)(2,1)S(1)} %get-tuple-element.204), channel_id=1, source_target_pairs={{0,3},{1,2},{2,1},{3,0},{4,7},{5,6},{6,5},{7,4},{8,11},{9,10},{10,... | collective-permute-start | bytes 786440 | tf_op jit(solution)/shard_map/ppermute | solution.py:425
  (59 other events, 804.1 us)
Sparse Core Ops, SparseCore 0:
  43.6 57.6 all-gather.1

commit v3 on v2

--- a/solution.py
+++ b/solution.py
@@ -421,6 +421,18 @@
     return jnp.stack(got)[jnp.arange(4, dtype=jnp.int32) ^ t_index]
 
 
+def halve_sums(rows, d_index):
+    rows = rows.reshape(2, 2, 2, 2, 2, -1)
+    z_index = lax.axis_index("mp")
+    bits = (d_index & 1, (d_index >> 1) & 1, d_index >> 2, z_index & 1, z_index >> 1)
+    moves = (lambda v: swap(v, 1), lambda v: swap(v, 2), lambda v: swap(v, 4),
+             lambda v: across(v, 1), lambda v: across(v, 2))
+    for axis, bit, move in zip((2, 1, 0, 1, 0), bits, moves):
+        keep = lax.dynamic_index_in_dim(rows, bit, axis, False)
+        rows = keep + move(lax.dynamic_index_in_dim(rows, 1 - bit, axis, False))
+    return rows
+
+
 def across(x, bits):
     return lax.ppermute(x, "mp", [(i, i ^ bits) for i in range(4)])
 
@@ -488,6 +500,9 @@
     )
     hids, shift_one = tie(hids, shift_one)
     hids = exchange_t(hids).reshape(sub, -1)
+    out_low, hat_low = tie(out_grad.astype(BF), hat_low)
+    grad_low = relocate(out_low)
+    hids, grad_low = tie(hids, grad_low)
     mine, other = gather_yz(hids)
     heads = lax.all_gather(heads.reshape(width, 4 * HD), "mp", axis=0, tiled=False)
     heads = heads.reshape(2, 2, width, 4, HD).transpose(2, 0, 3, 1, 4)
@@ -508,12 +523,11 @@
     chunk = jnp.asarray(CHUNK_OF_T, jnp.int32)[t_index]
     order = jnp.asarray(T_OF_CHUNK, jnp.int32)[jnp.arange(4, dtype=jnp.int32) ^ chunk]
 
-    out_low, hat_low = tie(out_grad.astype(BF), hat_low)
     hat_one = hat_low.astype(F32)
     mean_here, inv_here = stats[0][:, None], stats[1][:, None]
     block_here = hat_one * (1.0 / inv_here) + mean_here
     rows_one = gather_t((hat_one * gain_one + shift_one).astype(BF))
-    grad_low, rows_one = tie(relocate(out_low), rows_one)
+    grad_low, rows_one = tie(grad_low, rows_one)
     grad_rows = gather_t(grad_low)
     grad_here = grad_low.astype(F32)
 
@@ -521,12 +535,18 @@
     att, lse = attn_fwd(order, slopes, segs, qkv)
     att, grad_rows = tie(att, grad_rows)
     att_rows = att.reshape(-1, att.shape[2])
-    resid = block_here + scatter_t(trans_dot(att_rows, w_out_t)) + out_shift
+    att_part = trans_dot(att_rows, w_out_t).astype(BF)
+    resid = block_here + scatter_t(att_part) + out_shift
     hat_two, inv_two = norm_rows(resid)
     rows_two = gather_t((hat_two * gain_two + shift_two).astype(BF))
     value, slope = gelu_both(dot(rows_two, up_local) + up_shift)
     hidden = value.astype(BF)
+    down_part = trans_dot(hidden, down_t).astype(BF)
+    own_d, near_d, far_d = scatter_near(down_part)
+    hidden, own_d = tie(hidden, own_d)
     g_down = cross_dot(grad_rows, hidden).astype(BF)
+    far_d, g_down, grad_rows = tie(far_d, g_down, grad_rows)
+    block_sum = scatter_far(own_d, near_d, far_d)
     pre_grad = dot(grad_rows, down_t) * slope
     pre_low = pre_grad.astype(BF)
     two_part = trans_dot(pre_low, up_local).astype(BF)
@@ -534,6 +554,7 @@
 
     far, pre_low = tie(far, pre_low)
     g_up = cross_dot(rows_two, pre_low).astype(BF)
+    block_low = (resid + block_sum + down_shift).astype(BF)
 
     def to_y(grad):
         halves = grad[:sub], grad[sub:]
@@ -547,66 +568,62 @@
 
     down_keep, down_got = to_y(g_down)
     up_keep, up_got = to_y(g_up)
-    two_grad, up_keep = tie(scatter_far(own, near, far), up_keep)
+    two_grad, up_keep, block_low = tie(scatter_far(own, near, far), up_keep, block_low)
+    block_back = bring_back(block_low)
 
     resid_grad = grad_here + norm_back(two_grad, hat_two, inv_two, gain_two)
     resid_low = resid_grad.astype(BF)
-    resid_low, hidden = tie(resid_low, hidden)
-    down_part = trans_dot(hidden, down_t).astype(BF)
-    resid_rows, down_part = gather_t(resid_low, down_part)
+    resid_rows = gather_t(resid_low)
     resid_rows, down_got = tie(resid_rows, down_got)
     down_parts = to_z(down_keep, down_got)
-    block_sum = scatter_t(down_part)
-    block_low = (resid + block_sum + down_shift).astype(BF)
 
     att_grad = dot(resid_rows, w_out_t).astype(BF).reshape(att.shape)
     d_qkv, sums = attn_bwd(order, slopes, segs, qkv, att, att_grad, lse)
     d_rows = d_qkv.reshape(-1, d_qkv.shape[2])
     one_part = trans_dot(d_rows, w_local).astype(BF)
-    one_part, d_rows, block_low = tie(one_part, d_rows, block_low)
+    one_part, d_rows, block_back = tie(one_part, d_rows, block_back)
     own, near, far = scatter_near(one_part)
-    far, up_got = tie(far, up_got)
+    early = (
+        sums,
+        jnp.sum(resid_grad, axis=0),
+        jnp.sum(two_grad * hat_two, axis=0),
+        jnp.sum(two_grad, axis=0),
+        jnp.sum(pre_grad, axis=0),
+        jnp.sum(out_grad, axis=0),
+    )
+    far, d_rows, resid_rows, up_got, *early = tie(far, d_rows, resid_rows, up_got, *early)
+    sums, resid_sum, two_hat_sum, two_sum, pre_sum, out_sum = early
     up_parts = to_z(up_keep, up_got)
-
-    block_back = bring_back(block_low)
     g_qkv = cross_dot(rows_one, d_rows).astype(BF)
     g_qkv = g_qkv.reshape(2, 4, rows_d, 2, 3, 2, HD)
     g_out = cross_dot(resid_rows, att_rows).astype(BF).reshape(2, 4, rows_d, 2, 1, 2, HD)
     g_head = jnp.concatenate([g_qkv, g_out], axis=4).transpose(0, 1, 3, 5, 2, 4, 6)
     g_head = g_head.reshape(n_dev, rows_d, 4 * HD)
     one_grad = scatter_far(own, near, far)
-    one_grad, block_back, *down_parts = tie(one_grad, block_back, *down_parts)
+    g_head = lax.all_to_all(g_head, ("dp", "mp"), 0, 0, tiled=True)
+    one_grad, *parts = tie(one_grad, *up_parts, *down_parts)
     in_grad = resid_grad + norm_back(one_grad, hat_one, inv_here, gain_one)
     in_back = bring_back(in_grad.astype(BF))
-    in_back, *parts = tie(in_back, *up_parts, *down_parts)
     g_hid = jnp.concatenate([total_z(parts[:4]), total_z(parts[4:])], axis=1)
     g_hid = exchange_swaps(g_hid.reshape(4, rows_d, 2 * units), t_index).astype(F32)
 
     mine = jnp.arange(4, dtype=jnp.int32) == t_index
     qv_part = sums.transpose(1, 0, 2).reshape(2, 4, 1, HD)
     qv_place = jnp.where(mine[None, None, :, None], qv_part, 0.0).reshape(2, width)
-    up_part = jnp.sum(pre_grad, axis=0).reshape(4, units)[z_order][:, None, :]
+    up_part = pre_sum.reshape(4, units)[z_order][:, None, :]
     up_place = jnp.where(mine[None, :, None], up_part, 0.0).reshape(-1)
     sums = [
         jnp.sum(one_grad * hat_one, axis=0),
         jnp.sum(one_grad, axis=0),
         qv_place,
-        jnp.sum(resid_grad, axis=0),
-        jnp.sum(two_grad * hat_two, axis=0),
-        jnp.sum(two_grad, axis=0),
+        resid_sum,
+        two_hat_sum,
+        two_sum,
         up_place,
-        jnp.sum(out_grad, axis=0),
+        out_sum,
     ]
     rows, shapes = cut_vectors(sums, n_dev)
-    rows_hi = rows.astype(BF)
-    rows_lo = (rows - rows_hi.astype(F32)).astype(BF)
-    n_vec = rows.shape[1]
-    rows = jnp.concatenate([rows_hi, rows_lo], axis=1)
-    rows = jnp.pad(rows, ((0, 0), (0, 16 * 4 * HD - 2 * n_vec))).reshape(n_dev, 16, 4 * HD)
-    g_head = lax.all_to_all(jnp.concatenate([g_head, rows], axis=1), ("dp", "mp"), 0, 0, tiled=True)
-    flat = jnp.sum(g_head[:, rows_d:].reshape(n_dev, -1)[:, : 2 * n_vec].astype(F32), axis=0)
-    shares = share_vectors(flat[:n_vec] + flat[n_vec:], shapes)
-    g_head = g_head[:, :rows_d]
+    shares = share_vectors(halve_sums(rows, d_index), shapes)
     g_head = jnp.sum(g_head.reshape(2, 4, 4, rows_d, 4, HD).astype(F32), axis=(0, 2))
     qkv_share = g_head[:, :, :3].transpose(2, 1, 0, 3).reshape(w_qkv.shape)
     out_share = g_head[:, :, 3].transpose(0, 2, 1).reshape(w_out.shape)

time: 530 us -> 527 us (level)
  the two profiles are of different devices: /device:TPU:19 before, /device:TPU:0 now
where the time goes in v3:
time: 527 us; the launch traced here: 517 us
  waiting for transfers between devices  217 us (41%)
  starting transfers between devices  101 us (19%)
  local copies, waits for them, and re-layouts  54 us (10%)
  other arithmetic  46.7 us (9%)
  matrix products  41.5 us (8%)
  Pallas kernels  28.1 us (5%)
  between operations  15.6 us (3%)
  blocking collectives  12.8 us (2%)
    ppermute x11, waiting for transfers between devices, across(): return lax.ppermute(x, 'mp', [(i, i ^ bits) for i in range(4)])  105 us
    ppermute x32, waiting for transfers between devices, swap(): return lax.ppermute(x, 'dp', [(i, i ^ bits) for i in range(8)])  102 us
    ppermute x32, starting transfers between devices, swap(): return lax.ppermute(x, 'dp', [(i, i ^ bits) for i in range(8)])  50.8 us
    ppermute x11, starting transfers between devices, across(): return lax.ppermute(x, 'mp', [(i, i ^ bits) for i in range(4)])  18.5 us
    all_to_all x1, starting transfers between devices, gather_vectors(): got = lax.all_to_all(spread, ('dp', 'mp'), 0, 0, tiled=True)  15.8 us
    pallas_call x1, Pallas kernels, attn_bwd(): pl.pallas_call(lambda *refs: attn_bwd_kernel(*refs, nb=nb, rb=rb), grid=(...  15.4 us
    dot_general x4, matrix products, dot(): return jnp.dot(left, right, preferred_element_type=F32)  14.4 us
    dot_general x4, matrix products, cross_dot(): lax.dot_general(left, right, (((0,), (0,)), ((), ())), preferred_element_...  13.8 us
  transfers between devices with their start and end apart: 53, of which 21 were waited for; matrix products, arithmetic and copies ran while one was open for 18% of the time, Pallas kernels for 3%

profile of v3, /device:TPU:0, one launch (start us, length us, event | category | flops | bytes accessed | tf_op | source)
XLA Modules:
  0.0 516.8 jit_solution(1981406135622632015)
XLA Ops:
  10.2 5.2 %all-to-all-start = ((bf16[8,128,256]{1,2,0:T(8,128)(2,1)}), bf16[8,128,256]{1,2,0:T(8,128)(2,1)S(1)}, u32[]{:S(2)}, u32[]{:S(2)}) async-start(bf16[8,128,256]{1,2,0:T(8,128)(2,1)} %maximum_maximum_fusion), calls=%async_computation | async-start | bytes 1048576 | tf_op jit(solution)/shard_map/all_to_all | solution.py:488
  25.9 15.8 %all-to-all-start.1 = ((f32[32,1,384]{2,1,0:T(1,128)}), f32[32,1,384]{2,1,0:T(1,128)S(1)}, u32[]{:S(2)}, u32[]{:S(2)}) async-start(f32[32,1,384]{2,1,0:T(1,128)} %broadcast_in_dim.74), calls=%async_computation.1 | async-start | bytes 98304 | tf_op jit(solution)/shard_map/all_to_all | solution.py:230
  42.9 6.3 %all-to-all-done.1 = f32[32,1,384]{2,1,0:T(1,128)S(1)} async-done(((f32[32,1,384]{2,1,0:T(1,128)}), f32[32,1,384]{2,1,0:T(1,128)S(1)}, u32[]{:S(2)}, u32[]{:S(2)}) %all-to-all-start.1) | async-done | bytes 49184 | tf_op jit(solution)/shard_map/all_to_all | solution.py:230
  54.0 12.2 %collective-permute-done.5 = bf16[288,1024]{1,0:T(8,128)(2,1)S(1)} collective-permute-done((bf16[288,1024]{1,0:T(8,128)(2,1)S(1)}, bf16[288,1024]{1,0:T(8,128)(2,1)S(1)}, u32[]{:S(2)}, u32[]{:S(2)}) %collective-permute-start.5) | collective-permute-done | bytes 589856 | tf_op jit(solution)/shard_map/ppermute | solution.py:377
  66.1 12.8 %all_to_all.24 = bf16[4,128,512]{2,1,0:T(8,128)(2,1)} all-to-all(bf16[4,128,512]{2,1,0:T(8,128)(2,1)S(1)} %pad_maximum_fusion.18), channel_id=1, replica_groups={{0,4,8,12},{16,20,24,28},{1,5,9,13},{17,21,25,29},{2,6,10,14},{18,22,26..., dimensions={0} | all-to-all | bytes 1048576 | tf_op jit(solution)/shard_map/all_to_all | solution.py:415
  80.6 28.4 %collective-permute-start.8 = (bf16[288,1024]{1,0:T(8,128)(2,1)S(1)}, bf16[288,1024]{1,0:T(8,128)(2,1)S(1)}, u32[]{:S(2)}, u32[]{:S(2)}) collective-permute-start(bf16[288,1024]{1,0:T(8,128)(2,1)S(1)} %collective-permute-done.3), channel_id=1, source_target_pairs={{0,8},{4,12},{8,0},{12,4},{16,24},{20,28},{24,16},{28,20},{1,9},{5... | collective-permute-start | bytes 1769480 | tf_op jit(solution)/shard_map/ppermute | solution.py:377
  109.0 7.9 %collective-permute-done.8 = bf16[288,1024]{1,0:T(8,128)(2,1)S(1)} collective-permute-done((bf16[288,1024]{1,0:T(8,128)(2,1)S(1)}, bf16[288,1024]{1,0:T(8,128)(2,1)S(1)}, u32[]{:S(2)}, u32[]{:S(2)}) %collective-permute-start.8) | collective-permute-done | bytes 589856 | tf_op jit(solution)/shard_map/ppermute | solution.py:377
  133.0 12.8 %attn_fwd.1 = (bf16[4,288,256]{2,1,0:T(8,128)(2,1)}, f32[2,2,1152]{2,1,0:T(2,128)}) custom-call(s32[4]{0:T(128)} %gather_fusion, f32[4]{0:T(128)} %multiply_exponential_fusion.refs_1_, s32[1,1152]{1,0:T(1,128)} %reshape.321.refs_2_, s32[1152,1]{1,0:T(8,128)} %reshape.378.refs_3_, bf16[4,288,768]{2,1,0:T(8,128)(2,1)} %bitcast.156, ...), custom_call_target="tpu_custom_call" | custom-call | flops 2717908992 | bytes 16777216 | tf_op jit(solution)/shard_map/attn_fwd/pallas_call | solution.py:184
  164.0 10.0 %collective-permute-done.17 = bf16[512,512]{1,0:T(8,128)(2,1)S(1)} collective-permute-done((bf16[512,512]{1,0:T(8,128)(2,1)}, bf16[512,512]{1,0:T(8,128)(2,1)S(1)}, u32[]{:S(2)}, u32[]{:S(2)}) %collective-permute-start.17) | collective-permute-done | bytes 524320 | tf_op jit(solution)/shard_map/ppermute | solution.py:437
  177.0 27.3 %collective-permute-done.16 = bf16[512,512]{1,0:T(8,128)(2,1)S(1)} collective-permute-done((bf16[512,512]{1,0:T(8,128)(2,1)}, bf16[512,512]{1,0:T(8,128)(2,1)S(1)}, u32[]{:S(2)}, u32[]{:S(2)}) %collective-permute-start.16) | collective-permute-done | bytes 524320 | tf_op jit(solution)/shard_map/ppermute | solution.py:437
  208.9 10.2 %collective-permute-done.20 = bf16[512,512]{1,0:T(8,128)(2,1)S(1)} collective-permute-done((bf16[512,512]{1,0:T(8,128)(2,1)S(1)}, bf16[512,512]{1,0:T(8,128)(2,1)S(1)}, u32[]{:S(2)}, u32[]{:S(2)}) %collective-permute-start.20) | collective-permute-done | bytes 524320 | tf_op jit(solution)/shard_map/ppermute | solution.py:377
  219.2 3.4 collective-permute-done.13
  222.6 5.9 %collective-permute-done.19 = bf16[512,512]{1,0:T(8,128)(2,1)S(1)} collective-permute-done((bf16[512,512]{1,0:T(8,128)(2,1)S(1)}, bf16[512,512]{1,0:T(8,128)(2,1)S(1)}, u32[]{:S(2)}, u32[]{:S(2)}) %collective-permute-start.19) | collective-permute-done | bytes 524320 | tf_op jit(solution)/shard_map/ppermute | solution.py:377
  229.7 3.6 multiply_convert_fusion
  233.3 3.8 convolution_convert_fusion.2
  239.0 4.1 convolution_convert_fusion.6
  244.3 6.0 %fusion.32 = (f32[1024]{0:T(1024)}, bf16[1152,1024]{1,0:T(8,128)(2,1)S(1)}) fusion(f32[1152,1024]{1,0:T(8,128)S(1)} %get-tuple-element.260, bf16[1152,1024]{1,0:T(8,128)(2,1)S(1)} %copy-done.9, bf16[512,1024]{1,0:T(8,128)(2,1)S(1)} %get-tuple-element.210, bf16[512,1024]{1,0:T(8,128)(2,1)S(1)} %get-tuple-element.209), kind=kOutput, calls=%fused_computation.153 | convolution fusion | flops 2443705344 | bytes 11538432 | tf_op jit(solution)/shard_map/dot_general | solution.py:48
  250.3 3.7 convolution_convert_fusion.1
  256.8 14.6 %collective-permute-done.25 = bf16[288,1024]{1,0:T(8,128)(2,1)} collective-permute-done((bf16[288,1024]{1,0:T(8,128)(2,1)}, bf16[288,1024]{1,0:T(8,128)(2,1)}, u32[]{:S(2)}, u32[]{:S(2)}) %collective-permute-start.25) | collective-permute-done | bytes 589856 | tf_op jit(solution)/shard_map/ppermute | solution.py:377
  280.0 10.3 %collective-permute-done.24 = bf16[288,1024]{1,0:T(8,128)(2,1)S(1)} collective-permute-done((bf16[288,1024]{1,0:T(8,128)(2,1)S(1)}, bf16[288,1024]{1,0:T(8,128)(2,1)S(1)}, u32[]{:S(2)}, u32[]{:S(2)}) %collective-permute-start.24) | collective-permute-done | bytes 589856 | tf_op jit(solution)/shard_map/ppermute | solution.py:377
  294.9 12.2 %collective-permute-done.27 = bf16[288,1024]{1,0:T(8,128)(2,1)S(1)} collective-permute-done((bf16[288,1024]{1,0:T(8,128)(2,1)S(1)}, bf16[288,1024]{1,0:T(8,128)(2,1)S(1)}, u32[]{:S(2)}, u32[]{:S(2)}) %collective-permute-start.27) | collective-permute-done | bytes 589856 | tf_op jit(solution)/shard_map/ppermute | solution.py:377
  309.4 8.7 %collective-permute-done.29 = bf16[512,1024]{1,0:T(8,128)(2,1)S(1)} collective-permute-done((bf16[512,1024]{1,0:T(8,128)(2,1)S(1)}, bf16[512,1024]{1,0:T(8,128)(2,1)S(1)}, u32[]{:S(2)}, u32[]{:S(2)}) %collective-permute-start.29) | collective-permute-done | bytes 1048608 | tf_op jit(solution)/shard_map/ppermute | solution.py:377
  319.8 15.4 %attn_bwd.1 = (bf16[4,288,768]{2,1,0:T(8,128)(2,1)}, f32[2,2,128]{2,1,0:T(2,128)}) custom-call(s32[4]{0:T(128)} %gather_fusion, f32[4]{0:T(128)} %multiply_exponential_fusion.refs_1_, s32[1,1152]{1,0:T(1,128)} %reshape.321.refs_2_, s32[1152,1]{1,0:T(8,128)} %reshape.378.refs_3_, bf16[4,288,768]{2,1,0:T(8,128)(2,1)} %bitcast.159, ...), custom_call_target="tpu_custom_call" | custom-call | flops 5435817984 | bytes 33554432 | tf_op jit(solution)/shard_map/attn_bwd/pallas_call | solution.py:206
  335.1 3.9 convolution_convert_fusion
  354.9 12.2 %collective-permute-done.32 = bf16[512,1024]{1,0:T(8,128)(2,1)S(1)} collective-permute-done((bf16[512,1024]{1,0:T(8,128)(2,1)}, bf16[512,1024]{1,0:T(8,128)(2,1)S(1)}, u32[]{:S(2)}, u32[]{:S(2)}) %collective-permute-start.32) | collective-permute-done | bytes 1048608 | tf_op jit(solution)/shard_map/ppermute | solution.py:377
  372.9 5.6 %convolution_convert_fusion.7 = bf16[1024,768]{1,0:T(8,128)(2,1)} fusion(bf16[1152,1024]{1,0:T(8,128)(2,1)} %pad_maximum_fusion, bf16[1152,768]{1,0:T(8,128)(2,1)} %bitcast.163), kind=kOutput, calls=%fused_computation.38 | convolution fusion | flops 1812725760 | bytes 5701632 | tf_op jit(solution)/shard_map/dot_general | solution.py:52
  381.1 3.8 reshape.335
  389.7 3.6 all-to-all-start.3
  403.5 56.0 %collective-permute-done.35 = bf16[512,256]{1,0:T(8,128)(2,1)S(1)} collective-permute-done((bf16[512,256]{1,0:T(8,128)(2,1)}, bf16[512,256]{1,0:T(8,128)(2,1)S(1)}, u32[]{:S(2)}, u32[]{:S(2)}) %collective-permute-start.35) | collective-permute-done | bytes 262176 | tf_op jit(solution)/shard_map/ppermute | solution.py:437
  466.3 6.8 %collective-permute-start.45 = (f32[2,2,2,384]{3,2,1,0:T(2,128)S(1)}, f32[2,2,2,384]{3,2,1,0:T(2,128)S(1)}, u32[]{:S(2)}, u32[]{:S(2)}) collective-permute-start(f32[2,2,2,384]{3,2,1,0:T(2,128)S(1)} %dynamic-slice_bitcast_fusion.4), channel_id=1, source_target_pairs={{0,8},{4,12},{8,0},{12,4},{16,24},{20,28},{24,16},{28,20},{1,9},{5... | collective-permute-start | bytes 36872 | tf_op jit(solution)/shard_map/ppermute | solution.py:377
  479.1 11.9 %collective-permute-done.47 = f32[2,384]{1,0:T(2,128)S(1)} collective-permute-done((f32[2,384]{1,0:T(2,128)S(1)}, f32[2,384]{1,0:T(2,128)S(1)}, u32[]{:S(2)}, u32[]{:S(2)}) %collective-permute-start.47) | collective-permute-done | bytes 3104 | tf_op jit(solution)/shard_map/ppermute | solution.py:437
  491.1 4.5 collective-permute-start.48
  (386 shorter events, 152.4 us)
Async XLA Ops:
  17.0 33.1 %collective-permute-start = (bf16[288,1024]{1,0:T(8,128)(2,1)}, bf16[288,1024]{1,0:T(8,128)(2,1)S(1)}, u32[]{:S(2)}, u32[]{:S(2)}) collective-permute-start(bf16[288,1024]{1,0:T(8,128)(2,1)} %multiply_convert_fusion.1), channel_id=1, source_target_pairs={{0,0},{1,8},{2,12},{3,4},{4,3},{5,11},{6,15},{7,7},{8,1},{9,9},{10... | collective-permute-start | bytes 1769480 | tf_op jit(solution)/shard_map/ppermute | solution.py:381
  18.7 31.3 %collective-permute-start.1 = (f32[2,288]{1,0:T(2,128)S(1)}, f32[2,288]{1,0:T(2,128)S(1)}, u32[]{:S(2)}, u32[]{:S(2)}) collective-permute-start(f32[2,288]{1,0:T(2,128)S(1)} %pad_maximum_fusion.24), channel_id=1, source_target_pairs={{0,0},{1,8},{2,12},{3,4},{4,3},{5,11},{6,15},{7,7},{8,1},{9,9},{10... | collective-permute-start | bytes 6920 | tf_op jit(solution)/shard_map/ppermute | solution.py:381
  19.4 30.7 %collective-permute-start.2 = (s32[1152]{0:T(1024)S(1)}, s32[1152]{0:T(1024)S(1)}, u32[]{:S(2)}, u32[]{:S(2)}) collective-permute-start(s32[1152]{0:T(1024)S(1)} %copy-done.59), channel_id=1, source_target_pairs={{0,0},{1,8},{2,12},{3,4},{4,3},{5,11},{6,15},{7,7},{8,1},{9,9},{10... | collective-permute-start | bytes 13832 | tf_op jit(solution)/shard_map/ppermute | solution.py:381
  25.9 23.2 %all-to-all-start.1 = ((f32[32,1,384]{2,1,0:T(1,128)}), f32[32,1,384]{2,1,0:T(1,128)S(1)}, u32[]{:S(2)}, u32[]{:S(2)}) async-start(f32[32,1,384]{2,1,0:T(1,128)} %broadcast_in_dim.74), calls=%async_computation.1 | async-start | bytes 98304 | tf_op jit(solution)/shard_map/all_to_all | solution.py:230
  41.8 82.4 %all-gather.2.cloned.1.call-start = ((), (), s32[]{:S(2)}) async-start(), calls=%async_computation.4 | async-start | bytes 2621440 | tf_op jit(solution)/shard_map/all_gather | solution.py:507
  50.6 15.5 %collective-permute-start.5 = (bf16[288,1024]{1,0:T(8,128)(2,1)S(1)}, bf16[288,1024]{1,0:T(8,128)(2,1)S(1)}, u32[]{:S(2)}, u32[]{:S(2)}) collective-permute-start(bf16[288,1024]{1,0:T(8,128)(2,1)S(1)} %fusion.7), channel_id=1, source_target_pairs={{0,8},{4,12},{8,0},{12,4},{16,24},{20,28},{24,16},{28,20},{1,9},{5... | collective-permute-start | bytes 1769480 | tf_op jit(solution)/shard_map/ppermute | solution.py:377
  51.3 27.6 %collective-permute-start.3 = (bf16[288,1024]{1,0:T(8,128)(2,1)S(1)}, bf16[288,1024]{1,0:T(8,128)(2,1)S(1)}, u32[]{:S(2)}, u32[]{:S(2)}) collective-permute-start(bf16[288,1024]{1,0:T(8,128)(2,1)S(1)} %copy-done.28), channel_id=1, source_target_pairs={{0,0},{1,8},{2,12},{3,4},{4,3},{5,11},{6,15},{7,7},{8,1},{9,9},{10... | collective-permute-start | bytes 1769480 | tf_op jit(solution)/shard_map/ppermute | solution.py:381
  52.0 27.0 %collective-permute-start.4 = (bf16[288,1024]{1,0:T(8,128)(2,1)S(1)}, bf16[288,1024]{1,0:T(8,128)(2,1)S(1)}, u32[]{:S(2)}, u32[]{:S(2)}) collective-permute-start(bf16[288,1024]{1,0:T(8,128)(2,1)S(1)} %fusion.7), channel_id=1, source_target_pairs={{0,4},{4,0},{8,12},{12,8},{16,20},{20,16},{24,28},{28,24},{1,5},{5... | collective-permute-start | bytes 1769480 | tf_op jit(solution)/shard_map/ppermute | solution.py:377
  80.6 36.3 %collective-permute-start.8 = (bf16[288,1024]{1,0:T(8,128)(2,1)S(1)}, bf16[288,1024]{1,0:T(8,128)(2,1)S(1)}, u32[]{:S(2)}, u32[]{:S(2)}) collective-permute-start(bf16[288,1024]{1,0:T(8,128)(2,1)S(1)} %collective-permute-done.3), channel_id=1, source_target_pairs={{0,8},{4,12},{8,0},{12,4},{16,24},{20,28},{24,16},{28,20},{1,9},{5... | collective-permute-start | bytes 1769480 | tf_op jit(solution)/shard_map/ppermute | solution.py:377
  148.8 25.8 %collective-permute-start.10 = (bf16[576,1024]{1,0:T(8,128)(2,1)}, bf16[576,1024]{1,0:T(8,128)(2,1)S(1)}, u32[]{:S(2)}, u32[]{:S(2)}) collective-permute-start(bf16[576,1024]{1,0:T(8,128)(2,1)} %pad_maximum_fusion.10), channel_id=1, source_target_pairs={{0,4},{4,0},{8,12},{12,8},{16,20},{20,16},{24,28},{28,24},{1,5},{5... | collective-permute-start | bytes 3538952 | tf_op jit(solution)/shard_map/ppermute | solution.py:377
  157.0 16.9 %collective-permute-start.17 = (bf16[512,512]{1,0:T(8,128)(2,1)}, bf16[512,512]{1,0:T(8,128)(2,1)S(1)}, u32[]{:S(2)}, u32[]{:S(2)}) collective-permute-start(bf16[512,512]{1,0:T(8,128)(2,1)} %bitcast.10), channel_id=1, source_target_pairs={{0,3},{1,2},{2,1},{3,0},{4,7},{5,6},{6,5},{7,4},{8,11},{9,10},{10,... | collective-permute-start | bytes 1572872 | tf_op jit(solution)/shard_map/ppermute | solution.py:437
  157.8 46.5 %collective-permute-start.16 = (bf16[512,512]{1,0:T(8,128)(2,1)}, bf16[512,512]{1,0:T(8,128)(2,1)S(1)}, u32[]{:S(2)}, u32[]{:S(2)}) collective-permute-start(bf16[512,512]{1,0:T(8,128)(2,1)} %bitcast.10), channel_id=1, source_target_pairs={{0,2},{1,3},{2,0},{3,1},{4,6},{5,7},{6,4},{7,5},{8,10},{9,11},{10,... | collective-permute-start | bytes 1572872 | tf_op jit(solution)/shard_map/ppermute | solution.py:437
  159.4 45.5 %collective-permute-start.15 = (bf16[512,512]{1,0:T(8,128)(2,1)}, bf16[512,512]{1,0:T(8,128)(2,1)S(1)}, u32[]{:S(2)}, u32[]{:S(2)}) collective-permute-start(bf16[512,512]{1,0:T(8,128)(2,1)} %bitcast.10), channel_id=1, source_target_pairs={{0,1},{1,0},{2,3},{3,2},{4,5},{5,4},{6,7},{7,6},{8,9},{9,8},{10,11... | collective-permute-start | bytes 1572872 | tf_op jit(solution)/shard_map/ppermute | solution.py:437
  162.3 46.5 %collective-permute-start.18 = (bf16[512,512]{1,0:T(8,128)(2,1)}, bf16[512,512]{1,0:T(8,128)(2,1)S(1)}, u32[]{:S(2)}, u32[]{:S(2)}) collective-permute-start(bf16[512,512]{1,0:T(8,128)(2,1)} %bitcast.10), channel_id=1, source_target_pairs={{0,16},{4,20},{8,24},{12,28},{16,0},{20,4},{24,8},{28,12},{1,17},{... | collective-permute-start | bytes 1572872 | tf_op jit(solution)/shard_map/ppermute | solution.py:377
  174.0 34.9 %collective-permute-start.21 = (bf16[512,512]{1,0:T(8,128)(2,1)S(1)}, bf16[512,512]{1,0:T(8,128)(2,1)S(1)}, u32[]{:S(2)}, u32[]{:S(2)}) collective-permute-start(bf16[512,512]{1,0:T(8,128)(2,1)S(1)} %collective-permute-done.17), channel_id=1, source_target_pairs={{0,16},{4,20},{8,24},{12,28},{16,0},{20,4},{24,8},{28,12},{1,17},{... | collective-permute-start | bytes 1572872 | tf_op jit(solution)/shard_map/ppermute | solution.py:377
  174.8 31.6 %collective-permute-start.11 = (bf16[288,1024]{1,0:T(8,128)(2,1)S(1)}, bf16[288,1024]{1,0:T(8,128)(2,1)S(1)}, u32[]{:S(2)}, u32[]{:S(2)}) collective-permute-start(bf16[288,1024]{1,0:T(8,128)(2,1)S(1)} %add_convert_fusion.7), channel_id=1, source_target_pairs={{0,8},{4,12},{8,0},{12,4},{16,24},{20,28},{24,16},{28,20},{1,9},{5... | collective-permute-start | bytes 1769480 | tf_op jit(solution)/shard_map/ppermute | solution.py:377
  204.9 23.6 %collective-permute-start.19 = (bf16[512,512]{1,0:T(8,128)(2,1)S(1)}, bf16[512,512]{1,0:T(8,128)(2,1)S(1)}, u32[]{:S(2)}, u32[]{:S(2)}) collective-permute-start(bf16[512,512]{1,0:T(8,128)(2,1)S(1)} %collective-permute-done.15), channel_id=1, source_target_pairs={{0,16},{4,20},{8,24},{12,28},{16,0},{20,4},{24,8},{28,12},{1,17},{... | collective-permute-start | bytes 1572872 | tf_op jit(solution)/shard_map/ppermute | solution.py:377
  255.4 18.7 %collective-permute-start.23 = (bf16[576,1024]{1,0:T(8,128)(2,1)}, bf16[576,1024]{1,0:T(8,128)(2,1)}, u32[]{:S(2)}, u32[]{:S(2)}) collective-permute-start(bf16[576,1024]{1,0:T(8,128)(2,1)} %pad_maximum_fusion.12), channel_id=1, source_target_pairs={{0,4},{4,0},{8,12},{12,8},{16,20},{20,16},{24,28},{28,24},{1,5},{5... | collective-permute-start | bytes 3538952 | tf_op jit(solution)/shard_map/ppermute | solution.py:377
  255.4 16.1 %collective-permute-start.25 = (bf16[288,1024]{1,0:T(8,128)(2,1)}, bf16[288,1024]{1,0:T(8,128)(2,1)}, u32[]{:S(2)}, u32[]{:S(2)}) collective-permute-start(bf16[288,1024]{1,0:T(8,128)(2,1)} %add_convert_fusion.5), channel_id=1, source_target_pairs={{0,8},{4,12},{8,0},{12,4},{16,24},{20,28},{24,16},{28,20},{1,9},{5... | collective-permute-start | bytes 1769480 | tf_op jit(solution)/shard_map/ppermute | solution.py:377
  275.3 14.9 %collective-permute-start.24 = (bf16[288,1024]{1,0:T(8,128)(2,1)S(1)}, bf16[288,1024]{1,0:T(8,128)(2,1)S(1)}, u32[]{:S(2)}, u32[]{:S(2)}) collective-permute-start(bf16[288,1024]{1,0:T(8,128)(2,1)S(1)} %add_convert_fusion.4), channel_id=1, source_target_pairs={{0,8},{4,12},{8,0},{12,4},{16,24},{20,28},{24,16},{28,20},{1,9},{5... | collective-permute-start | bytes 1769480 | tf_op jit(solution)/shard_map/ppermute | solution.py:377
  294.2 23.9 %collective-permute-start.29 = (bf16[512,1024]{1,0:T(8,128)(2,1)S(1)}, bf16[512,1024]{1,0:T(8,128)(2,1)S(1)}, u32[]{:S(2)}, u32[]{:S(2)}) collective-permute-start(bf16[512,1024]{1,0:T(8,128)(2,1)S(1)} %broadcast_select_fusion.1), channel_id=1, source_target_pairs={{0,16},{4,20},{8,24},{12,28},{16,0},{20,4},{24,8},{28,12},{1,17},{... | collective-permute-start | bytes 3145736 | tf_op jit(solution)/shard_map/ppermute | solution.py:377
  307.1 32.0 %collective-permute-start.30 = (bf16[288,1024]{1,0:T(8,128)(2,1)}, bf16[288,1024]{1,0:T(8,128)(2,1)S(1)}, u32[]{:S(2)}, u32[]{:S(2)}) collective-permute-start(bf16[288,1024]{1,0:T(8,128)(2,1)} %add_convert_fusion.3), channel_id=1, source_target_pairs={{0,0},{8,1},{12,2},{4,3},{3,4},{11,5},{15,6},{7,7},{1,8},{9,9},{13... | collective-permute-start | bytes 1769480 | tf_op jit(solution)/shard_map/ppermute | solution.py:385
  341.3 25.8 %collective-permute-start.32 = (bf16[512,1024]{1,0:T(8,128)(2,1)}, bf16[512,1024]{1,0:T(8,128)(2,1)S(1)}, u32[]{:S(2)}, u32[]{:S(2)}) collective-permute-start(bf16[512,1024]{1,0:T(8,128)(2,1)} %get-tuple-element.207), channel_id=1, source_target_pairs={{0,16},{4,20},{8,24},{12,28},{16,0},{20,4},{24,8},{28,12},{1,17},{... | collective-permute-start | bytes 3145736 | tf_op jit(solution)/shard_map/ppermute | solution.py:377
  348.0 49.8 %collective-permute-start.37 = (bf16[512,256]{1,0:T(8,128)(2,1)}, bf16[512,256]{1,0:T(8,128)(2,1)}, u32[]{:S(2)}, u32[]{:S(2)}) collective-permute-start(bf16[512,256]{1,0:T(8,128)(2,1)} %get-tuple-element.219), channel_id=1, source_target_pairs={{0,1},{1,0},{2,3},{3,2},{4,5},{5,4},{6,7},{7,6},{8,9},{9,8},{10,11... | collective-permute-start | bytes 786440 | tf_op jit(solution)/shard_map/ppermute | solution.py:437
  348.5 54.9 %collective-permute-start.38 = (bf16[512,256]{1,0:T(8,128)(2,1)}, bf16[512,256]{1,0:T(8,128)(2,1)}, u32[]{:S(2)}, u32[]{:S(2)}) collective-permute-start(bf16[512,256]{1,0:T(8,128)(2,1)} %get-tuple-element.218), channel_id=1, source_target_pairs={{0,2},{1,3},{2,0},{3,1},{4,6},{5,7},{6,4},{7,5},{8,10},{9,11},{10,... | collective-permute-start | bytes 786440 | tf_op jit(solution)/shard_map/ppermute | solution.py:437
  350.0 53.5 %collective-permute-start.39 = (bf16[512,256]{1,0:T(8,128)(2,1)}, bf16[512,256]{1,0:T(8,128)(2,1)}, u32[]{:S(2)}, u32[]{:S(2)}) collective-permute-start(bf16[512,256]{1,0:T(8,128)(2,1)} %get-tuple-element.217), channel_id=1, source_target_pairs={{0,3},{1,2},{2,1},{3,0},{4,7},{5,6},{6,5},{7,4},{8,11},{9,10},{10,... | collective-permute-start | bytes 786440 | tf_op jit(solution)/shard_map/ppermute | solution.py:437
  367.1 33.2 %collective-permute-start.33 = (bf16[288,1024]{1,0:T(8,128)(2,1)}, bf16[288,1024]{1,0:T(8,128)(2,1)}, u32[]{:S(2)}, u32[]{:S(2)}) collective-permute-start(bf16[288,1024]{1,0:T(8,128)(2,1)} %add_convert_fusion.2), channel_id=1, source_target_pairs={{0,8},{4,12},{8,0},{12,4},{16,24},{20,28},{24,16},{28,20},{1,9},{5... | collective-permute-start | bytes 1769480 | tf_op jit(solution)/shard_map/ppermute | solution.py:377
  369.3 34.2 %collective-permute-start.34 = (bf16[512,256]{1,0:T(8,128)(2,1)}, bf16[512,256]{1,0:T(8,128)(2,1)}, u32[]{:S(2)}, u32[]{:S(2)}) collective-permute-start(bf16[512,256]{1,0:T(8,128)(2,1)} %get-tuple-element.223), channel_id=1, source_target_pairs={{0,1},{1,0},{2,3},{3,2},{4,5},{5,4},{6,7},{7,6},{8,9},{9,8},{10,11... | collective-permute-start | bytes 786440 | tf_op jit(solution)/shard_map/ppermute | solution.py:437
  389.7 116.5 %all-to-all-start.3 = ((bf16[32,128,256]{1,2,0:T(8,128)(2,1)}), bf16[32,128,256]{1,2,0:T(8,128)(2,1)}, u32[]{:S(2)}, u32[]{:S(2)}) async-start(bf16[32,128,256]{1,2,0:T(8,128)(2,1)} %bitcast.119), calls=%async_computation.3 | async-start | bytes 4194304 | tf_op jit(solution)/shard_map/all_to_all | solution.py:603
  397.7 61.7 %collective-permute-start.35 = (bf16[512,256]{1,0:T(8,128)(2,1)}, bf16[512,256]{1,0:T(8,128)(2,1)S(1)}, u32[]{:S(2)}, u32[]{:S(2)}) collective-permute-start(bf16[512,256]{1,0:T(8,128)(2,1)} %get-tuple-element.222), channel_id=1, source_target_pairs={{0,2},{1,3},{2,0},{3,1},{4,6},{5,7},{6,4},{7,5},{8,10},{9,11},{10,... | collective-permute-start | bytes 786440 | tf_op jit(solution)/shard_map/ppermute | solution.py:437
  400.3 59.2 %collective-permute-start.36 = (bf16[512,256]{1,0:T(8,128)(2,1)}, bf16[512,256]{1,0:T(8,128)(2,1)S(1)}, u32[]{:S(2)}, u32[]{:S(2)}) collective-permute-start(bf16[512,256]{1,0:T(8,128)(2,1)} %get-tuple-element.221), channel_id=1, source_target_pairs={{0,3},{1,2},{2,1},{3,0},{4,7},{5,6},{6,5},{7,4},{8,11},{9,10},{10,... | collective-permute-start | bytes 786440 | tf_op jit(solution)/shard_map/ppermute | solution.py:437
  464.5 40.5 %collective-permute-start.40 = (bf16[288,1024]{1,0:T(8,128)(2,1)}, bf16[288,1024]{1,0:T(8,128)(2,1)S(1)}, u32[]{:S(2)}, u32[]{:S(2)}) collective-permute-start(bf16[288,1024]{1,0:T(8,128)(2,1)} %fusion.15), channel_id=1, source_target_pairs={{0,0},{8,1},{12,2},{4,3},{3,4},{11,5},{15,6},{7,7},{1,8},{9,9},{13... | collective-permute-start | bytes 1769480 | tf_op jit(solution)/shard_map/ppermute | solution.py:385
  (85 other events, 1109.0 us)
Sparse Core Ops, SparseCore 0:
  44.8 64.6 all-gather.1

commit v4 on v3

--- a/solution.py
+++ b/solution.py
@@ -385,11 +385,9 @@
     return lax.ppermute(x, ("dp", "mp"), FROM_PLANE)
 
 
-def gather_t(x, *fill):
+def gather_t(x, near_fill=()):
     far = swap(x, 2)
-    near = swap(x, 1)
-    if fill:
-        far, *fill = tie(far, *fill)
+    near, *fill = tie(swap(x, 1), *near_fill)
     rows = jnp.concatenate([x, near, far, swap(far, 1)], axis=0)
     return (rows, *fill) if fill else rows
 
@@ -405,10 +403,6 @@
 def scatter_far(own, near, far):
     far = swap(far, 2)
     return own.astype(F32) + near.astype(F32) + far.astype(F32)
-
-
-def scatter_t(part):
-    return scatter_far(*scatter_near(part))
 
 
 def exchange_t(x):
@@ -437,12 +431,6 @@
     return lax.ppermute(x, "mp", [(i, i ^ bits) for i in range(4)])
 
 
-def gather_yz(x):
-    mine = [x] + [across(x, k) for k in (1, 2, 3)]
-    other = [swap(m, 4) for m in mine]
-    return mine, other
-
-
 def by_y(mine, other, y_index):
     mine, other = jnp.concatenate(mine, axis=1), jnp.concatenate(other, axis=1)
     first = jnp.where(y_index == 0, mine, other)
@@ -485,12 +473,6 @@
         ],
         axis=2,
     )
-    heads = lax.all_to_all(jnp.concatenate([heads, heads], axis=0), "dp", 0, 0, tiled=True)
-    heads, *vecs = tie(heads, *vecs)
-    gain_one, shift_one, qv_all, out_shift, gain_two, shift_two, up_all, down_shift = (
-        gather_vectors(vecs, n_dev)
-    )
-    hat_low, stats, segs, gain_one = tie(hat_low, stats, segs, gain_one)
     hids = jnp.concatenate(
         [
             w_up.reshape(w_up.shape[0], 4, -1).transpose(1, 0, 2),
@@ -498,47 +480,68 @@
         ],
         axis=2,
     )
-    hids, shift_one = tie(hids, shift_one)
-    hids = exchange_t(hids).reshape(sub, -1)
+    both = exchange_t(jnp.concatenate([heads, hids], axis=2)).reshape(sub, -1)
+    both, *vecs = tie(both, *vecs)
+    gain_one, shift_one, qv_all, out_shift, gain_two, shift_two, up_all, down_shift = (
+        gather_vectors(vecs, n_dev)
+    )
+    hat_low, stats, segs, gain_one = tie(hat_low, stats, segs, gain_one)
+    heads, hids = both[:, : 4 * HD], both[:, 4 * HD :]
+    heads_mine = [heads] + [across(heads, k) for k in (1, 2, 3)]
     out_low, hat_low = tie(out_grad.astype(BF), hat_low)
     grad_low = relocate(out_low)
-    hids, grad_low = tie(hids, grad_low)
-    mine, other = gather_yz(hids)
-    heads = lax.all_gather(heads.reshape(width, 4 * HD), "mp", axis=0, tiled=False)
-    heads = heads.reshape(2, 2, width, 4, HD).transpose(2, 0, 3, 1, 4)
-    heads = heads.reshape(width, 2, 4, 2 * HD)
-    w_local = heads[:, :, :3].reshape(width, -1)
-    w_out_t = heads[:, :, 3].reshape(width, -1)
+    mine = [hids] + [across(hids, k) for k in (1, 2, 3)]
+    other = [swap(hids, 4)]
+
+    qv_mine = lax.dynamic_index_in_dim(qv_all.reshape(2, 4, 4, HD), t_index, 2, False)
+    z_order = jnp.arange(4, dtype=jnp.int32) ^ lax.axis_index("mp")
+    qv_mine = qv_mine[:, z_order].reshape(2, -1)
+    b_local = pair_columns([qv_mine[0], jnp.zeros_like(qv_mine[0]), qv_mine[1]])
+    up_shift = lax.dynamic_index_in_dim(up_all.reshape(4, 4, -1), t_index, 1, False)
+    up_shift = up_shift[z_order].reshape(-1)
+    slopes = head_slopes(4 * z_order + t_index)
+    chunk = jnp.asarray(CHUNK_OF_T, jnp.int32)[t_index]
+    order = jnp.asarray(T_OF_CHUNK, jnp.int32)[jnp.arange(4, dtype=jnp.int32) ^ chunk]
+
+    hat_one = hat_low.astype(F32)
+    mean_here, inv_here = stats[0][:, None], stats[1][:, None]
+    block_here = hat_one * (1.0 / inv_here) + mean_here
+    rows_one, *heads_mine[1:] = gather_t(
+        (hat_one * gain_one + shift_one).astype(BF), near_fill=heads_mine[1:]
+    )
+    heads_other = [swap(heads, 4)]
+    heads_other = heads_other + [swap(m, 4) for m in heads_mine[1:]]
+    heads_mine = [h.reshape(sub, 4, HD) for h in heads_mine]
+    heads_other = [h.reshape(sub, 4, HD) for h in heads_other]
+    qkv_order = [(2 * p + k, which) for p in range(2) for which in range(3) for k in range(2)]
+    w_local = by_y(
+        [heads_mine[k][:, w] for k, w in qkv_order],
+        [heads_other[k][:, w] for k, w in qkv_order],
+        y_index,
+    )
+    w_out_t = by_y([h[:, 3] for h in heads_mine], [h[:, 3] for h in heads_other], y_index)
+    w_local, w_out_t = tie(w_local, w_out_t)
+    qkv = (dot(rows_one, w_local) + b_local).astype(BF)
+    grad_low, qkv = tie(grad_low, qkv)
+    grad_rows = gather_t(grad_low)
+    grad_here = grad_low.astype(F32)
+    qkv = qkv.reshape(4, -1, w_local.shape[1])
+    att, lse = attn_fwd(order, slopes, segs, qkv)
+    att_rows = att.reshape(-1, att.shape[2])
+    att_part = trans_dot(att_rows, w_out_t).astype(BF)
+    own, near, far = scatter_near(att_part)
+    att_sum = own.astype(F32) + near.astype(F32)
+    att_sum, *mine[1:] = tie(att_sum, *mine[1:])
+    att_sum = att_sum + swap(far, 2).astype(F32)
+    other = other + [swap(m, 4) for m in mine[1:]]
     units = hids.shape[1] // 2
     up_local = by_y([m[:, :units] for m in mine], [m[:, :units] for m in other], y_index)
     down_t = by_y([m[:, units:] for m in mine], [m[:, units:] for m in other], y_index)
-
-    qv_mine = lax.dynamic_index_in_dim(qv_all.reshape(2, 4, 4, HD), t_index, 2, False)
-    qv_mine = qv_mine.reshape(2, -1)
-    b_local = pair_columns([qv_mine[0], jnp.zeros_like(qv_mine[0]), qv_mine[1]])
-    up_shift = lax.dynamic_index_in_dim(up_all.reshape(4, 4, -1), t_index, 1, False)
-    z_order = jnp.arange(4, dtype=jnp.int32) ^ lax.axis_index("mp")
-    up_shift = up_shift[z_order].reshape(-1)
-    slopes = head_slopes(4 * jnp.arange(4, dtype=jnp.int32) + t_index)
-    chunk = jnp.asarray(CHUNK_OF_T, jnp.int32)[t_index]
-    order = jnp.asarray(T_OF_CHUNK, jnp.int32)[jnp.arange(4, dtype=jnp.int32) ^ chunk]
-
-    hat_one = hat_low.astype(F32)
-    mean_here, inv_here = stats[0][:, None], stats[1][:, None]
-    block_here = hat_one * (1.0 / inv_here) + mean_here
-    rows_one = gather_t((hat_one * gain_one + shift_one).astype(BF))
-    grad_low, rows_one = tie(grad_low, rows_one)
-    grad_rows = gather_t(grad_low)
-    grad_here = grad_low.astype(F32)
-
-    qkv = (dot(rows_one, w_local) + b_local).astype(BF).reshape(4, -1, w_local.shape[1])
-    att, lse = attn_fwd(order, slopes, segs, qkv)
-    att, grad_rows = tie(att, grad_rows)
-    att_rows = att.reshape(-1, att.shape[2])
-    att_part = trans_dot(att_rows, w_out_t).astype(BF)
-    resid = block_here + scatter_t(att_part) + out_shift
+    up_local, down_t = tie(up_local, down_t)
+    resid = block_here + att_sum + out_shift
     hat_two, inv_two = norm_rows(resid)
     rows_two = gather_t((hat_two * gain_two + shift_two).astype(BF))
+    rows_two, grad_rows = tie(rows_two, grad_rows)
     value, slope = gelu_both(dot(rows_two, up_local) + up_shift)
     hidden = value.astype(BF)
     down_part = trans_dot(hidden, down_t).astype(BF)
@@ -546,7 +549,7 @@
     hidden, own_d = tie(hidden, own_d)
     g_down = cross_dot(grad_rows, hidden).astype(BF)
     far_d, g_down, grad_rows = tie(far_d, g_down, grad_rows)
-    block_sum = scatter_far(own_d, near_d, far_d)
+    block_sum = swap(far_d, 2)
     pre_grad = dot(grad_rows, down_t) * slope
     pre_low = pre_grad.astype(BF)
     two_part = trans_dot(pre_low, up_local).astype(BF)
@@ -554,6 +557,8 @@
 
     far, pre_low = tie(far, pre_low)
     g_up = cross_dot(rows_two, pre_low).astype(BF)
+    g_up, block_sum = tie(g_up, block_sum)
+    block_sum = own_d.astype(F32) + near_d.astype(F32) + block_sum.astype(F32)
     block_low = (resid + block_sum + down_shift).astype(BF)
 
     def to_y(grad):
@@ -569,19 +574,20 @@
     down_keep, down_got = to_y(g_down)
     up_keep, up_got = to_y(g_up)
     two_grad, up_keep, block_low = tie(scatter_far(own, near, far), up_keep, block_low)
-    block_back = bring_back(block_low)
 
     resid_grad = grad_here + norm_back(two_grad, hat_two, inv_two, gain_two)
     resid_low = resid_grad.astype(BF)
-    resid_rows = gather_t(resid_low)
-    resid_rows, down_got = tie(resid_rows, down_got)
+    resid_rows, down_got = gather_t(resid_low, near_fill=[down_got])
+    resid_rows, block_low = tie(resid_rows, block_low)
+    block_back = bring_back(block_low)
     down_parts = to_z(down_keep, down_got)
 
     att_grad = dot(resid_rows, w_out_t).astype(BF).reshape(att.shape)
     d_qkv, sums = attn_bwd(order, slopes, segs, qkv, att, att_grad, lse)
     d_rows = d_qkv.reshape(-1, d_qkv.shape[2])
     one_part = trans_dot(d_rows, w_local).astype(BF)
-    one_part, d_rows, block_back = tie(one_part, d_rows, block_back)
+    one_part, d_rows = tie(one_part, d_rows)
+    g_qkv = cross_dot(rows_one, d_rows).astype(BF)
     own, near, far = scatter_near(one_part)
     early = (
         sums,
@@ -591,24 +597,27 @@
         jnp.sum(pre_grad, axis=0),
         jnp.sum(out_grad, axis=0),
     )
-    far, d_rows, resid_rows, up_got, *early = tie(far, d_rows, resid_rows, up_got, *early)
+    far, g_qkv, resid_rows, up_got, *early = tie(far, g_qkv, resid_rows, up_got, *early)
     sums, resid_sum, two_hat_sum, two_sum, pre_sum, out_sum = early
     up_parts = to_z(up_keep, up_got)
-    g_qkv = cross_dot(rows_one, d_rows).astype(BF)
-    g_qkv = g_qkv.reshape(2, 4, rows_d, 2, 3, 2, HD)
-    g_out = cross_dot(resid_rows, att_rows).astype(BF).reshape(2, 4, rows_d, 2, 1, 2, HD)
-    g_head = jnp.concatenate([g_qkv, g_out], axis=4).transpose(0, 1, 3, 5, 2, 4, 6)
-    g_head = g_head.reshape(n_dev, rows_d, 4 * HD)
+    qkv_keep, qkv_got = to_y(g_qkv)
+    g_out = cross_dot(resid_rows, att_rows).astype(BF)
+    out_keep, out_got = to_y(g_out)
     one_grad = scatter_far(own, near, far)
-    g_head = lax.all_to_all(g_head, ("dp", "mp"), 0, 0, tiled=True)
-    one_grad, *parts = tie(one_grad, *up_parts, *down_parts)
+    one_grad, block_back, *parts = tie(one_grad, block_back, *up_parts, *down_parts)
     in_grad = resid_grad + norm_back(one_grad, hat_one, inv_here, gain_one)
     in_back = bring_back(in_grad.astype(BF))
+    one_sum = jnp.sum(one_grad, axis=0)
+    one_sum, qkv_got, out_got = tie(one_sum, qkv_got, out_got)
+    both = (qkv_keep.astype(F32) + qkv_got.astype(F32)).astype(BF).reshape(sub, 2, 3, 2, HD)
+    both_out = (out_keep.astype(F32) + out_got.astype(F32)).astype(BF).reshape(sub, 2, 1, 2, HD)
+    both = jnp.concatenate([both, both_out], axis=2)
+    head_parts = send_z([both[:, k // 2, :, k % 2].reshape(sub, 4 * HD) for k in range(4)])
     g_hid = jnp.concatenate([total_z(parts[:4]), total_z(parts[4:])], axis=1)
     g_hid = exchange_swaps(g_hid.reshape(4, rows_d, 2 * units), t_index).astype(F32)
 
     mine = jnp.arange(4, dtype=jnp.int32) == t_index
-    qv_part = sums.transpose(1, 0, 2).reshape(2, 4, 1, HD)
+    qv_part = sums.transpose(1, 0, 2).reshape(2, 4, HD)[:, z_order][:, :, None, :]
     qv_place = jnp.where(mine[None, None, :, None], qv_part, 0.0).reshape(2, width)
     up_part = pre_sum.reshape(4, units)[z_order][:, None, :]
     up_place = jnp.where(mine[None, :, None], up_part, 0.0).reshape(-1)
@@ -624,7 +633,8 @@
     ]
     rows, shapes = cut_vectors(sums, n_dev)
     shares = share_vectors(halve_sums(rows, d_index), shapes)
-    g_head = jnp.sum(g_head.reshape(2, 4, 4, rows_d, 4, HD).astype(F32), axis=(0, 2))
+    g_head = exchange_swaps(total_z(head_parts).reshape(4, rows_d, 4 * HD), t_index)
+    g_head = g_head.astype(F32).reshape(4, rows_d, 4, HD)
     qkv_share = g_head[:, :, :3].transpose(2, 1, 0, 3).reshape(w_qkv.shape)
     out_share = g_head[:, :, 3].transpose(0, 2, 1).reshape(w_out.shape)
 

time: 527 us -> 499 us (0.947)
  waiting for transfers between devices: 217 us -> 190 us
  local copies, waits for them, and re-layouts: 54 us -> 78.3 us
  between operations: 15.6 us -> 2.64 us
  blocking collectives: 12.8 us -> 0 us
    ppermute x11 -> x17, starting transfers between devices: 18.5 us -> 51 us  [across(): return lax.ppermute(x, 'mp', [(i, i ^ bits) for i in range(4)])]
    ppermute x32 -> x41, waiting for transfers between devices: 102 us -> 73.5 us  [swap(): return lax.ppermute(x, 'dp', [(i, i ^ bits) for i in range(8)])]
    ppermute x32 -> x41, starting transfers between devices: 50.8 us -> 26.6 us  [swap(): return lax.ppermute(x, 'dp', [(i, i ^ bits) for i in range(8)])]
    unnamed x134 -> x202, local copies, waits for them, and re-layouts: 8.25 us -> 26.1 us
    all_to_all x2 -> x1, waiting for transfers between devices: 3.33 us -> 16.2 us  [exchange_t(): return lax.all_to_all(x, 'dp', 0, 0, tiled=True, axis_index_groups=GROUPS)]
    all_to_all x1 -> x0, blocking collectives: 12.8 us -> none  [exchange_t(): return lax.all_to_all(x, 'dp', 0, 0, tiled=True, axis_index_groups=GROUPS)]
    ppermute x11 -> x17, waiting for transfers between devices: 105 us -> 93.3 us  [across(): return lax.ppermute(x, 'mp', [(i, i ^ bits) for i in range(4)])]
    all_to_all x1, starting transfers between devices: 15.8 us -> 5.68 us  [gather_vectors(): got = lax.all_to_all(spread, ('dp', 'mp'), 0, 0, tiled=True)]
  transfers between devices with their start and end apart: 53 -> 66, of which waited for: 21 -> 22; matrix products, arithmetic and copies ran while one was open for 18% -> 26% of each run, Pallas kernels for 3% -> 0%
where the time goes in v4:
time: 499 us; the launch traced here: 493 us
  waiting for transfers between devices  190 us (38%)
  starting transfers between devices  102 us (20%)
  local copies, waits for them, and re-layouts  78.3 us (16%)
  other arithmetic  50.2 us (10%)
  matrix products  41.3 us (8%)
  Pallas kernels  28.2 us (6%)
    ppermute x17, waiting for transfers between devices, across(): return lax.ppermute(x, 'mp', [(i, i ^ bits) for i in range(4)])  93.3 us
    ppermute x41, waiting for transfers between devices, swap(): return lax.ppermute(x, 'dp', [(i, i ^ bits) for i in range(8)])  73.5 us
    ppermute x17, starting transfers between devices, across(): return lax.ppermute(x, 'mp', [(i, i ^ bits) for i in range(4)])  51 us
    ppermute x41, starting transfers between devices, swap(): return lax.ppermute(x, 'dp', [(i, i ^ bits) for i in range(8)])  26.6 us
    unnamed x202, local copies, waits for them, and re-layouts  26.1 us
    all_to_all x1, waiting for transfers between devices, exchange_t(): return lax.all_to_all(x, 'dp', 0, 0, tiled=True, axis_index_groups=GROUPS)  16.2 us
    dot_general x4, matrix products, dot(): return jnp.dot(left, right, preferred_element_type=F32)  15.8 us
    pallas_call x1, Pallas kernels, attn_bwd(): pl.pallas_call(lambda *refs: attn_bwd_kernel(*refs, nb=nb, rb=rb), grid=(...  15.4 us
  transfers between devices with their start and end apart: 66, of which 22 were waited for; matrix products, arithmetic and copies ran while one was open for 26% of the time, Pallas kernels for 0%

profile of v4, /device:TPU:0, one launch (start us, length us, event | category | flops | bytes accessed | tf_op | source)
XLA Modules:
  0.0 493.4 jit_solution(7734793407786921467)
XLA Ops:
  6.6 7.9 %all-to-all-start = ((bf16[4,128,768]{2,1,0:T(8,128)(2,1)}), bf16[4,128,768]{2,1,0:T(8,128)(2,1)S(1)}, u32[]{:S(2)}, u32[]{:S(2)}) async-start(bf16[4,128,768]{2,1,0:T(8,128)(2,1)} %pad_maximum_fusion.15), calls=%async_computation | async-start | bytes 1572864 | tf_op jit(solution)/shard_map/all_to_all | solution.py:409
  18.7 16.2 %all-to-all-done = bf16[4,128,768]{2,1,0:T(8,128)(2,1)S(1)} async-done(((bf16[4,128,768]{2,1,0:T(8,128)(2,1)}), bf16[4,128,768]{2,1,0:T(8,128)(2,1)S(1)}, u32[]{:S(2)}, u32[]{:S(2)}) %all-to-all-start) | async-done | bytes 786464 | tf_op jit(solution)/shard_map/all_to_all | solution.py:409
  35.8 5.7 %all-to-all-start.1 = ((f32[32,1,384]{2,1,0:T(1,128)}), f32[32,1,384]{2,1,0:T(1,128)S(1)}, u32[]{:S(2)}, u32[]{:S(2)}) async-start(f32[32,1,384]{2,1,0:T(1,128)} %broadcast_in_dim.43), calls=%async_computation.1 | async-start | bytes 98304 | tf_op jit(solution)/shard_map/all_to_all | solution.py:230
  41.5 7.4 %all-to-all-done.1 = f32[32,1,384]{2,1,0:T(1,128)S(1)} async-done(((f32[32,1,384]{2,1,0:T(1,128)}), f32[32,1,384]{2,1,0:T(1,128)S(1)}, u32[]{:S(2)}, u32[]{:S(2)}) %all-to-all-start.1) | async-done | bytes 49184 | tf_op jit(solution)/shard_map/all_to_all | solution.py:230
  61.2 5.1 %collective-permute-done.5 = bf16[512,256]{1,0:T(8,128)(2,1)} collective-permute-done((bf16[512,256]{1,0:T(8,128)(2,1)S(1)}, bf16[512,256]{1,0:T(8,128)(2,1)}, u32[]{:S(2)}, u32[]{:S(2)}) %collective-permute-start.5) | collective-permute-done | bytes 262176 | tf_op jit(solution)/shard_map/ppermute | solution.py:431
  68.5 12.9 %collective-permute-done.6 = bf16[512,256]{1,0:T(8,128)(2,1)} collective-permute-done((bf16[512,256]{1,0:T(8,128)(2,1)S(1)}, bf16[512,256]{1,0:T(8,128)(2,1)}, u32[]{:S(2)}, u32[]{:S(2)}) %collective-permute-start.6) | collective-permute-done | bytes 262176 | tf_op jit(solution)/shard_map/ppermute | solution.py:431
  120.9 4.7 fusion.5
  125.6 12.8 %attn_fwd.1 = (bf16[4,288,256]{2,1,0:T(8,128)(2,1)}, f32[2,2,1152]{2,1,0:T(2,128)}) custom-call(s32[4]{0:T(128)} %gather_fusion, f32[4]{0:T(128)} %multiply_exponential_fusion.refs_1_, s32[1,1152]{1,0:T(1,128)} %reshape.340.refs_2_, s32[1152,1]{1,0:T(8,128)} %reshape.423.refs_3_, bf16[4,288,768]{2,1,0:T(8,128)(2,1)} %bitcast.253, ...), custom_call_target="tpu_custom_call" | custom-call | flops 2717908992 | bytes 16777216 | tf_op jit(solution)/shard_map/attn_fwd/pallas_call | solution.py:184
  143.6 5.6 %collective-permute-start.15 = (bf16[512,512]{1,0:T(8,128)(2,1)}, bf16[512,512]{1,0:T(8,128)(2,1)}, u32[]{:S(2)}, u32[]{:S(2)}) collective-permute-start(bf16[512,512]{1,0:T(8,128)(2,1)} %slice.412), channel_id=1, source_target_pairs={{0,1},{1,0},{2,3},{3,2},{4,5},{5,4},{6,7},{7,6},{8,9},{9,8},{10,11... | collective-permute-start | bytes 1572872 | tf_op jit(solution)/shard_map/ppermute | solution.py:431
  157.6 6.0 %collective-permute-start.16 = (bf16[512,512]{1,0:T(8,128)(2,1)}, bf16[512,512]{1,0:T(8,128)(2,1)S(1)}, u32[]{:S(2)}, u32[]{:S(2)}) collective-permute-start(bf16[512,512]{1,0:T(8,128)(2,1)} %slice.412), channel_id=1, source_target_pairs={{0,2},{1,3},{2,0},{3,1},{4,6},{5,7},{6,4},{7,5},{8,10},{9,11},{10,... | collective-permute-start | bytes 1572872 | tf_op jit(solution)/shard_map/ppermute | solution.py:431
  167.7 30.6 %collective-permute-done.16 = bf16[512,512]{1,0:T(8,128)(2,1)S(1)} collective-permute-done((bf16[512,512]{1,0:T(8,128)(2,1)}, bf16[512,512]{1,0:T(8,128)(2,1)S(1)}, u32[]{:S(2)}, u32[]{:S(2)}) %collective-permute-start.16) | collective-permute-done | bytes 524320 | tf_op jit(solution)/shard_map/ppermute | solution.py:431
  205.1 7.1 %collective-permute-done.18 = bf16[288,1024]{1,0:T(8,128)(2,1)S(1)} collective-permute-done((bf16[288,1024]{1,0:T(8,128)(2,1)S(1)}, bf16[288,1024]{1,0:T(8,128)(2,1)S(1)}, u32[]{:S(2)}, u32[]{:S(2)}) %collective-permute-start.18) | collective-permute-done | bytes 589856 | tf_op jit(solution)/shard_map/ppermute | solution.py:377
  214.7 9.6 %collective-permute-done.27 = bf16[512,512]{1,0:T(8,128)(2,1)S(1)} collective-permute-done((bf16[512,512]{1,0:T(8,128)(2,1)S(1)}, bf16[512,512]{1,0:T(8,128)(2,1)S(1)}, u32[]{:S(2)}, u32[]{:S(2)}) %collective-permute-start.27) | collective-permute-done | bytes 524320 | tf_op jit(solution)/shard_map/ppermute | solution.py:377
  224.4 8.3 %collective-permute-done.26 = bf16[512,512]{1,0:T(8,128)(2,1)S(1)} collective-permute-done((bf16[512,512]{1,0:T(8,128)(2,1)}, bf16[512,512]{1,0:T(8,128)(2,1)S(1)}, u32[]{:S(2)}, u32[]{:S(2)}) %collective-permute-start.26) | collective-permute-done | bytes 524320 | tf_op jit(solution)/shard_map/ppermute | solution.py:377
  236.1 3.6 multiply_convert_fusion
  243.0 4.2 convolution_convert_fusion.6
  248.5 5.8 %fusion.33 = (f32[1024]{0:T(1024)}, bf16[1152,1024]{1,0:T(8,128)(2,1)S(1)}) fusion(f32[1152,1024]{1,0:T(8,128)S(1)} %get-tuple-element.335, bf16[1152,1024]{1,0:T(8,128)(2,1)S(1)} %pad_maximum_fusion.2, bf16[1024,1024]{1,0:T(8,128)(2,1)S(1)} %pad_maximum_fusion.5), kind=kOutput, calls=%fused_computation.190 | convolution fusion | flops 2439511040 | bytes 11538432 | tf_op jit(solution)/shard_map/dot_general | solution.py:48
  266.1 5.3 %convolution_convert_fusion.5 = bf16[1024,1024]{1,0:T(8,128)(2,1)S(1)} fusion(bf16[1152,1024]{1,0:T(8,128)(2,1)} %copy-done.11, bf16[1152,1024]{1,0:T(8,128)(2,1)} %copy-done.85), kind=kOutput, calls=%fused_computation.37 | convolution fusion | flops 2416967680 | bytes 6815744 | tf_op jit(solution)/shard_map/dot_general | solution.py:52
  271.4 6.6 %collective-permute-done.32 = bf16[288,1024]{1,0:T(8,128)(2,1)S(1)} collective-permute-done((bf16[288,1024]{1,0:T(8,128)(2,1)}, bf16[288,1024]{1,0:T(8,128)(2,1)S(1)}, u32[]{:S(2)}, u32[]{:S(2)}) %collective-permute-start.32) | collective-permute-done | bytes 589856 | tf_op jit(solution)/shard_map/ppermute | solution.py:377
  280.7 9.0 %collective-permute-done.31 = bf16[288,1024]{1,0:T(8,128)(2,1)S(1)} collective-permute-done((bf16[288,1024]{1,0:T(8,128)(2,1)S(1)}, bf16[288,1024]{1,0:T(8,128)(2,1)S(1)}, u32[]{:S(2)}, u32[]{:S(2)}) %collective-permute-start.31) | collective-permute-done | bytes 589856 | tf_op jit(solution)/shard_map/ppermute | solution.py:377
  295.9 12.2 %collective-permute-done.35 = bf16[288,1024]{1,0:T(8,128)(2,1)S(1)} collective-permute-done((bf16[288,1024]{1,0:T(8,128)(2,1)S(1)}, bf16[288,1024]{1,0:T(8,128)(2,1)S(1)}, u32[]{:S(2)}, u32[]{:S(2)}) %collective-permute-start.35) | collective-permute-done | bytes 589856 | tf_op jit(solution)/shard_map/ppermute | solution.py:377
  308.8 10.6 %collective-permute-done.34 = bf16[512,1024]{1,0:T(8,128)(2,1)S(1)} collective-permute-done((bf16[512,1024]{1,0:T(8,128)(2,1)S(1)}, bf16[512,1024]{1,0:T(8,128)(2,1)S(1)}, u32[]{:S(2)}, u32[]{:S(2)}) %collective-permute-start.34) | collective-permute-done | bytes 1048608 | tf_op jit(solution)/shard_map/ppermute | solution.py:377
  322.2 15.4 %attn_bwd.1 = (bf16[4,288,768]{2,1,0:T(8,128)(2,1)}, f32[2,2,128]{2,1,0:T(2,128)}) custom-call(s32[4]{0:T(128)} %gather_fusion, f32[4]{0:T(128)} %multiply_exponential_fusion.refs_1_, s32[1,1152]{1,0:T(1,128)} %reshape.340.refs_2_, s32[1152,1]{1,0:T(8,128)} %reshape.423.refs_3_, bf16[4,288,768]{2,1,0:T(8,128)(2,1)} %bitcast.256, ...), custom_call_target="tpu_custom_call" | custom-call | flops 5435817984 | bytes 33554432 | tf_op jit(solution)/shard_map/attn_bwd/pallas_call | solution.py:206
  347.1 11.8 %collective-permute-start.44 = (bf16[512,256]{1,0:T(8,128)(2,1)}, bf16[512,256]{1,0:T(8,128)(2,1)}, u32[]{:S(2)}, u32[]{:S(2)}) collective-permute-start(bf16[512,256]{1,0:T(8,128)(2,1)} %get-tuple-element.255), channel_id=1, source_target_pairs={{0,1},{1,0},{2,3},{3,2},{4,5},{5,4},{6,7},{7,6},{8,9},{9,8},{10,11... | collective-permute-start | bytes 786440 | tf_op jit(solution)/shard_map/ppermute | solution.py:431
  361.3 3.7 convolution_convert_fusion.7
  365.0 6.3 %collective-permute-start.40 = (bf16[288,1024]{1,0:T(8,128)(2,1)}, bf16[288,1024]{1,0:T(8,128)(2,1)}, u32[]{:S(2)}, u32[]{:S(2)}) collective-permute-start(bf16[288,1024]{1,0:T(8,128)(2,1)} %add_convert_fusion.4), channel_id=1, source_target_pairs={{0,0},{8,1},{12,2},{4,3},{3,4},{11,5},{15,6},{7,7},{1,8},{9,9},{13... | collective-permute-start | bytes 1769480 | tf_op jit(solution)/shard_map/ppermute | solution.py:385
  384.3 7.1 %collective-permute-start.41 = (bf16[512,256]{1,0:T(8,128)(2,1)S(1)}, bf16[512,256]{1,0:T(8,128)(2,1)S(1)}, u32[]{:S(2)}, u32[]{:S(2)}) collective-permute-start(bf16[512,256]{1,0:T(8,128)(2,1)S(1)} %copy-done.55), channel_id=1, source_target_pairs={{0,1},{1,0},{2,3},{3,2},{4,5},{5,4},{6,7},{7,6},{8,9},{9,8},{10,11... | collective-permute-start | bytes 786440 | tf_op jit(solution)/shard_map/ppermute | solution.py:431
  397.8 6.9 %collective-permute-done.41 = bf16[512,256]{1,0:T(8,128)(2,1)S(1)} collective-permute-done((bf16[512,256]{1,0:T(8,128)(2,1)S(1)}, bf16[512,256]{1,0:T(8,128)(2,1)S(1)}, u32[]{:S(2)}, u32[]{:S(2)}) %collective-permute-start.41) | collective-permute-done | bytes 262176 | tf_op jit(solution)/shard_map/ppermute | solution.py:431
  404.7 12.7 %collective-permute-done.42 = bf16[512,256]{1,0:T(8,128)(2,1)S(1)} collective-permute-done((bf16[512,256]{1,0:T(8,128)(2,1)S(1)}, bf16[512,256]{1,0:T(8,128)(2,1)S(1)}, u32[]{:S(2)}, u32[]{:S(2)}) %collective-permute-start.42) | collective-permute-done | bytes 262176 | tf_op jit(solution)/shard_map/ppermute | solution.py:431
  454.9 3.7 collective-permute-done.52
  458.6 19.9 %collective-permute-done.51 = bf16[512,256]{0,1:T(8,128)(2,1)} collective-permute-done((bf16[512,256]{0,1:T(8,128)(2,1)}, bf16[512,256]{0,1:T(8,128)(2,1)}, u32[]{:S(2)}, u32[]{:S(2)}) %collective-permute-start.51) | collective-permute-done | bytes 262176 | tf_op jit(solution)/shard_map/ppermute | solution.py:431
  483.7 4.5 collective-permute-done.55
  (506 shorter events, 201.6 us)
Async XLA Ops:
  4.1 45.6 %collective-permute-start = (bf16[288,1024]{1,0:T(8,128)(2,1)S(1)}, bf16[288,1024]{1,0:T(8,128)(2,1)S(1)}, u32[]{:S(2)}, u32[]{:S(2)}) collective-permute-start(bf16[288,1024]{1,0:T(8,128)(2,1)S(1)} %multiply_convert_fusion.1), channel_id=1, source_target_pairs={{0,0},{1,8},{2,12},{3,4},{4,3},{5,11},{6,15},{7,7},{8,1},{9,9},{10... | collective-permute-start | bytes 1769480 | tf_op jit(solution)/shard_map/ppermute | solution.py:381
  6.6 28.3 %all-to-all-start = ((bf16[4,128,768]{2,1,0:T(8,128)(2,1)}), bf16[4,128,768]{2,1,0:T(8,128)(2,1)S(1)}, u32[]{:S(2)}, u32[]{:S(2)}) async-start(bf16[4,128,768]{2,1,0:T(8,128)(2,1)} %pad_maximum_fusion.15), calls=%async_computation | async-start | bytes 1572864 | tf_op jit(solution)/shard_map/all_to_all | solution.py:409
  14.5 35.1 %collective-permute-start.1 = (f32[2,288]{1,0:T(2,128)S(1)}, f32[2,288]{1,0:T(2,128)S(1)}, u32[]{:S(2)}, u32[]{:S(2)}) collective-permute-start(f32[2,288]{1,0:T(2,128)S(1)} %pad_maximum_fusion.26), channel_id=1, source_target_pairs={{0,0},{1,8},{2,12},{3,4},{4,3},{5,11},{6,15},{7,7},{8,1},{9,9},{10... | collective-permute-start | bytes 6920 | tf_op jit(solution)/shard_map/ppermute | solution.py:381
  15.2 34.4 %collective-permute-start.2 = (s32[1152]{0:T(1024)S(1)}, s32[1152]{0:T(1024)S(1)}, u32[]{:S(2)}, u32[]{:S(2)}) collective-permute-start(s32[1152]{0:T(1024)S(1)} %copy-done.81), channel_id=1, source_target_pairs={{0,0},{1,8},{2,12},{3,4},{4,3},{5,11},{6,15},{7,7},{8,1},{9,9},{10... | collective-permute-start | bytes 13832 | tf_op jit(solution)/shard_map/ppermute | solution.py:381
  49.9 31.6 %collective-permute-start.4 = (bf16[288,1024]{1,0:T(8,128)(2,1)S(1)}, bf16[288,1024]{1,0:T(8,128)(2,1)}, u32[]{:S(2)}, u32[]{:S(2)}) collective-permute-start(bf16[288,1024]{1,0:T(8,128)(2,1)S(1)} %fusion.7), channel_id=1, source_target_pairs={{0,4},{4,0},{8,12},{12,8},{16,20},{20,16},{24,28},{28,24},{1,5},{5... | collective-permute-start | bytes 1769480 | tf_op jit(solution)/shard_map/ppermute | solution.py:377
  53.7 27.8 %collective-permute-start.6 = (bf16[512,256]{1,0:T(8,128)(2,1)S(1)}, bf16[512,256]{1,0:T(8,128)(2,1)}, u32[]{:S(2)}, u32[]{:S(2)}) collective-permute-start(bf16[512,256]{1,0:T(8,128)(2,1)S(1)} %get-tuple-element.263), channel_id=1, source_target_pairs={{0,2},{1,3},{2,0},{3,1},{4,6},{5,7},{6,4},{7,5},{8,10},{9,11},{10,... | collective-permute-start | bytes 786440 | tf_op jit(solution)/shard_map/ppermute | solution.py:431
  54.4 27.0 %collective-permute-start.7 = (bf16[512,256]{1,0:T(8,128)(2,1)S(1)}, bf16[512,256]{1,0:T(8,128)(2,1)}, u32[]{:S(2)}, u32[]{:S(2)}) collective-permute-start(bf16[512,256]{1,0:T(8,128)(2,1)S(1)} %get-tuple-element.263), channel_id=1, source_target_pairs={{0,3},{1,2},{2,1},{3,0},{4,7},{5,6},{6,5},{7,4},{8,11},{9,10},{10,... | collective-permute-start | bytes 786440 | tf_op jit(solution)/shard_map/ppermute | solution.py:431
  60.5 41.6 %collective-permute-start.8 = (bf16[288,1024]{1,0:T(8,128)(2,1)S(1)}, bf16[288,1024]{1,0:T(8,128)(2,1)}, u32[]{:S(2)}, u32[]{:S(2)}) collective-permute-start(bf16[288,1024]{1,0:T(8,128)(2,1)S(1)} %fusion.7), channel_id=1, source_target_pairs={{0,8},{4,12},{8,0},{12,4},{16,24},{20,28},{24,16},{28,20},{1,9},{5... | collective-permute-start | bytes 1769480 | tf_op jit(solution)/shard_map/ppermute | solution.py:377
  66.3 59.3 %collective-permute-start.3 = (bf16[288,1024]{1,0:T(8,128)(2,1)}, bf16[288,1024]{1,0:T(8,128)(2,1)S(1)}, u32[]{:S(2)}, u32[]{:S(2)}) collective-permute-start(bf16[288,1024]{1,0:T(8,128)(2,1)} %get-tuple-element.99), channel_id=1, source_target_pairs={{0,0},{1,8},{2,12},{3,4},{4,3},{5,11},{6,15},{7,7},{8,1},{9,9},{10... | collective-permute-start | bytes 1769480 | tf_op jit(solution)/shard_map/ppermute | solution.py:381
  141.6 24.4 %collective-permute-start.14 = (bf16[576,1024]{1,0:T(8,128)(2,1)}, bf16[576,1024]{1,0:T(8,128)(2,1)}, u32[]{:S(2)}, u32[]{:S(2)}) collective-permute-start(bf16[576,1024]{1,0:T(8,128)(2,1)} %pad_maximum_fusion.7), channel_id=1, source_target_pairs={{0,4},{4,0},{8,12},{12,8},{16,20},{20,16},{24,28},{28,24},{1,5},{5... | collective-permute-start | bytes 3538952 | tf_op jit(solution)/shard_map/ppermute | solution.py:377
  143.6 24.1 %collective-permute-start.15 = (bf16[512,512]{1,0:T(8,128)(2,1)}, bf16[512,512]{1,0:T(8,128)(2,1)}, u32[]{:S(2)}, u32[]{:S(2)}) collective-permute-start(bf16[512,512]{1,0:T(8,128)(2,1)} %slice.412), channel_id=1, source_target_pairs={{0,1},{1,0},{2,3},{3,2},{4,5},{5,4},{6,7},{7,6},{8,9},{9,8},{10,11... | collective-permute-start | bytes 1572872 | tf_op jit(solution)/shard_map/ppermute | solution.py:431
  157.6 40.7 %collective-permute-start.16 = (bf16[512,512]{1,0:T(8,128)(2,1)}, bf16[512,512]{1,0:T(8,128)(2,1)S(1)}, u32[]{:S(2)}, u32[]{:S(2)}) collective-permute-start(bf16[512,512]{1,0:T(8,128)(2,1)} %slice.412), channel_id=1, source_target_pairs={{0,2},{1,3},{2,0},{3,1},{4,6},{5,7},{6,4},{7,5},{8,10},{9,11},{10,... | collective-permute-start | bytes 1572872 | tf_op jit(solution)/shard_map/ppermute | solution.py:431
  163.6 34.6 %collective-permute-start.17 = (bf16[512,512]{1,0:T(8,128)(2,1)}, bf16[512,512]{1,0:T(8,128)(2,1)S(1)}, u32[]{:S(2)}, u32[]{:S(2)}) collective-permute-start(bf16[512,512]{1,0:T(8,128)(2,1)} %slice.412), channel_id=1, source_target_pairs={{0,3},{1,2},{2,1},{3,0},{4,7},{5,6},{6,5},{7,4},{8,11},{9,10},{10,... | collective-permute-start | bytes 1572872 | tf_op jit(solution)/shard_map/ppermute | solution.py:431
  165.9 37.7 %collective-permute-start.24 = (bf16[288,1024]{1,0:T(8,128)(2,1)}, bf16[288,1024]{1,0:T(8,128)(2,1)S(1)}, u32[]{:S(2)}, u32[]{:S(2)}) collective-permute-start(bf16[288,1024]{1,0:T(8,128)(2,1)} %collective-permute-done.23), channel_id=1, source_target_pairs={{0,4},{4,0},{8,12},{12,8},{16,20},{20,16},{24,28},{28,24},{1,5},{5... | collective-permute-start | bytes 1769480 | tf_op jit(solution)/shard_map/ppermute | solution.py:377
  200.5 23.8 %collective-permute-start.27 = (bf16[512,512]{1,0:T(8,128)(2,1)S(1)}, bf16[512,512]{1,0:T(8,128)(2,1)S(1)}, u32[]{:S(2)}, u32[]{:S(2)}) collective-permute-start(bf16[512,512]{1,0:T(8,128)(2,1)S(1)} %collective-permute-done.16), channel_id=1, source_target_pairs={{0,16},{4,20},{8,24},{12,28},{16,0},{20,4},{24,8},{28,12},{1,17},{... | collective-permute-start | bytes 1572872 | tf_op jit(solution)/shard_map/ppermute | solution.py:377
  201.8 30.8 %collective-permute-start.26 = (bf16[512,512]{1,0:T(8,128)(2,1)}, bf16[512,512]{1,0:T(8,128)(2,1)S(1)}, u32[]{:S(2)}, u32[]{:S(2)}) collective-permute-start(bf16[512,512]{1,0:T(8,128)(2,1)} %collective-permute-done.15), channel_id=1, source_target_pairs={{0,16},{4,20},{8,24},{12,28},{16,0},{20,4},{24,8},{28,12},{1,17},{... | collective-permute-start | bytes 1572872 | tf_op jit(solution)/shard_map/ppermute | solution.py:377
  264.6 25.2 %collective-permute-start.31 = (bf16[288,1024]{1,0:T(8,128)(2,1)S(1)}, bf16[288,1024]{1,0:T(8,128)(2,1)S(1)}, u32[]{:S(2)}, u32[]{:S(2)}) collective-permute-start(bf16[288,1024]{1,0:T(8,128)(2,1)S(1)} %add_convert_fusion.5), channel_id=1, source_target_pairs={{0,8},{4,12},{8,0},{12,4},{16,24},{20,28},{24,16},{28,20},{1,9},{5... | collective-permute-start | bytes 1769480 | tf_op jit(solution)/shard_map/ppermute | solution.py:377
  295.3 24.1 %collective-permute-start.34 = (bf16[512,1024]{1,0:T(8,128)(2,1)S(1)}, bf16[512,1024]{1,0:T(8,128)(2,1)S(1)}, u32[]{:S(2)}, u32[]{:S(2)}) collective-permute-start(bf16[512,1024]{1,0:T(8,128)(2,1)S(1)} %broadcast_select_fusion.1), channel_id=1, source_target_pairs={{0,16},{4,20},{8,24},{12,28},{16,0},{20,4},{24,8},{28,12},{1,17},{... | collective-permute-start | bytes 3145736 | tf_op jit(solution)/shard_map/ppermute | solution.py:377
  295.9 23.4 %collective-permute-start.33 = (bf16[288,1024]{1,0:T(8,128)(2,1)S(1)}, bf16[288,1024]{1,0:T(8,128)(2,1)S(1)}, u32[]{:S(2)}, u32[]{:S(2)}) collective-permute-start(bf16[288,1024]{1,0:T(8,128)(2,1)S(1)} %convert_element_type.272), channel_id=1, source_target_pairs={{0,4},{4,0},{8,12},{12,8},{16,20},{20,16},{24,28},{28,24},{1,5},{5... | collective-permute-start | bytes 1769480 | tf_op jit(solution)/shard_map/ppermute | solution.py:377
  342.9 22.1 %collective-permute-start.37 = (bf16[576,1024]{1,0:T(8,128)(2,1)}, bf16[576,1024]{1,0:T(8,128)(2,1)}, u32[]{:S(2)}, u32[]{:S(2)}) collective-permute-start(bf16[576,1024]{1,0:T(8,128)(2,1)} %pad_maximum_fusion.10), channel_id=1, source_target_pairs={{0,4},{4,0},{8,12},{12,8},{16,20},{20,16},{24,28},{28,24},{1,5},{5... | collective-permute-start | bytes 3538952 | tf_op jit(solution)/shard_map/ppermute | solution.py:377
  343.1 30.5 %collective-permute-start.38 = (bf16[512,1024]{1,0:T(8,128)(2,1)}, bf16[512,1024]{1,0:T(8,128)(2,1)S(1)}, u32[]{:S(2)}, u32[]{:S(2)}) collective-permute-start(bf16[512,1024]{1,0:T(8,128)(2,1)} %get-tuple-element.237), channel_id=1, source_target_pairs={{0,16},{4,20},{8,24},{12,28},{16,0},{20,4},{24,8},{28,12},{1,17},{... | collective-permute-start | bytes 3145736 | tf_op jit(solution)/shard_map/ppermute | solution.py:377
  347.1 37.3 %collective-permute-start.44 = (bf16[512,256]{1,0:T(8,128)(2,1)}, bf16[512,256]{1,0:T(8,128)(2,1)}, u32[]{:S(2)}, u32[]{:S(2)}) collective-permute-start(bf16[512,256]{1,0:T(8,128)(2,1)} %get-tuple-element.255), channel_id=1, source_target_pairs={{0,1},{1,0},{2,3},{3,2},{4,5},{5,4},{6,7},{7,6},{8,9},{9,8},{10,11... | collective-permute-start | bytes 786440 | tf_op jit(solution)/shard_map/ppermute | solution.py:431
  358.9 32.5 %collective-permute-start.45 = (bf16[512,256]{1,0:T(8,128)(2,1)}, bf16[512,256]{1,0:T(8,128)(2,1)}, u32[]{:S(2)}, u32[]{:S(2)}) collective-permute-start(bf16[512,256]{1,0:T(8,128)(2,1)} %get-tuple-element.254), channel_id=1, source_target_pairs={{0,2},{1,3},{2,0},{3,1},{4,6},{5,7},{6,4},{7,5},{8,10},{9,11},{10,... | collective-permute-start | bytes 786440 | tf_op jit(solution)/shard_map/ppermute | solution.py:431
  358.9 36.8 %collective-permute-start.46 = (bf16[512,256]{1,0:T(8,128)(2,1)}, bf16[512,256]{1,0:T(8,128)(2,1)}, u32[]{:S(2)}, u32[]{:S(2)}) collective-permute-start(bf16[512,256]{1,0:T(8,128)(2,1)} %get-tuple-element.253), channel_id=1, source_target_pairs={{0,3},{1,2},{2,1},{3,0},{4,7},{5,6},{6,5},{7,4},{8,11},{9,10},{10,... | collective-permute-start | bytes 786440 | tf_op jit(solution)/shard_map/ppermute | solution.py:431
  365.0 31.5 %collective-permute-start.40 = (bf16[288,1024]{1,0:T(8,128)(2,1)}, bf16[288,1024]{1,0:T(8,128)(2,1)}, u32[]{:S(2)}, u32[]{:S(2)}) collective-permute-start(bf16[288,1024]{1,0:T(8,128)(2,1)} %add_convert_fusion.4), channel_id=1, source_target_pairs={{0,0},{8,1},{12,2},{4,3},{3,4},{11,5},{15,6},{7,7},{1,8},{9,9},{13... | collective-permute-start | bytes 1769480 | tf_op jit(solution)/shard_map/ppermute | solution.py:385
  391.4 26.0 %collective-permute-start.42 = (bf16[512,256]{1,0:T(8,128)(2,1)S(1)}, bf16[512,256]{1,0:T(8,128)(2,1)S(1)}, u32[]{:S(2)}, u32[]{:S(2)}) collective-permute-start(bf16[512,256]{1,0:T(8,128)(2,1)S(1)} %copy-done.54), channel_id=1, source_target_pairs={{0,2},{1,3},{2,0},{3,1},{4,6},{5,7},{6,4},{7,5},{8,10},{9,11},{10,... | collective-permute-start | bytes 786440 | tf_op jit(solution)/shard_map/ppermute | solution.py:431
  391.4 26.0 %collective-permute-start.43 = (bf16[512,256]{1,0:T(8,128)(2,1)S(1)}, bf16[512,256]{1,0:T(8,128)(2,1)S(1)}, u32[]{:S(2)}, u32[]{:S(2)}) collective-permute-start(bf16[512,256]{1,0:T(8,128)(2,1)S(1)} %copy-done.53), channel_id=1, source_target_pairs={{0,3},{1,2},{2,1},{3,0},{4,7},{5,6},{6,5},{7,4},{8,11},{9,10},{10,... | collective-permute-start | bytes 786440 | tf_op jit(solution)/shard_map/ppermute | solution.py:431
  395.7 47.7 %collective-permute-start.48 = (bf16[512,768]{1,0:T(8,128)(2,1)}, bf16[512,768]{1,0:T(8,128)(2,1)}, u32[]{:S(2)}, u32[]{:S(2)}) collective-permute-start(bf16[512,768]{1,0:T(8,128)(2,1)} %broadcast_select_fusion.7), channel_id=1, source_target_pairs={{0,16},{4,20},{8,24},{12,28},{16,0},{20,4},{24,8},{28,12},{1,17},{... | collective-permute-start | bytes 2359304 | tf_op jit(solution)/shard_map/ppermute | solution.py:377
  396.5 47.0 %collective-permute-start.49 = (bf16[512,256]{0,1:T(8,128)(2,1)}, bf16[512,256]{0,1:T(8,128)(2,1)}, u32[]{:S(2)}, u32[]{:S(2)}) collective-permute-start(bf16[512,256]{0,1:T(8,128)(2,1)} %broadcast_select_fusion.10), channel_id=1, source_target_pairs={{0,16},{4,20},{8,24},{12,28},{16,0},{20,4},{24,8},{28,12},{1,17},{... | collective-permute-start | bytes 786440 | tf_op jit(solution)/shard_map/ppermute | solution.py:377
  448.9 29.6 %collective-permute-start.51 = (bf16[512,256]{0,1:T(8,128)(2,1)}, bf16[512,256]{0,1:T(8,128)(2,1)}, u32[]{:S(2)}, u32[]{:S(2)}) collective-permute-start(bf16[512,256]{0,1:T(8,128)(2,1)} %bitcast.66), channel_id=1, source_target_pairs={{0,2},{1,3},{2,0},{3,1},{4,6},{5,7},{6,4},{7,5},{8,10},{9,11},{10,... | collective-permute-start | bytes 786440 | tf_op jit(solution)/shard_map/ppermute | solution.py:431
  448.9 29.6 %collective-permute-start.50 = (bf16[512,256]{0,1:T(8,128)(2,1)}, bf16[512,256]{0,1:T(8,128)(2,1)}, u32[]{:S(2)}, u32[]{:S(2)}) collective-permute-start(bf16[512,256]{0,1:T(8,128)(2,1)} %bitcast.65), channel_id=1, source_target_pairs={{0,1},{1,0},{2,3},{3,2},{4,5},{5,4},{6,7},{7,6},{8,9},{9,8},{10,11... | collective-permute-start | bytes 786440 | tf_op jit(solution)/shard_map/ppermute | solution.py:431
  452.2 39.8 %collective-permute-start.47 = (bf16[288,1024]{1,0:T(8,128)(2,1)S(1)}, bf16[288,1024]{1,0:T(8,128)(2,1)S(1)}, u32[]{:S(2)}, u32[]{:S(2)}) collective-permute-start(bf16[288,1024]{1,0:T(8,128)(2,1)S(1)} %copy-done.32), channel_id=1, source_target_pairs={{0,0},{8,1},{12,2},{4,3},{3,4},{11,5},{15,6},{7,7},{1,8},{9,9},{13... | collective-permute-start | bytes 1769480 | tf_op jit(solution)/shard_map/ppermute | solution.py:385
  (120 other events, 1288.3 us)

commit v5 on v4

--- a/solution.py
+++ b/solution.py
@@ -438,6 +438,43 @@
     return jnp.concatenate([first, second], axis=0)
 
 
+def head_weights_kernel(y_ref, *refs, n):
+    qkv_ref, out_ref = refs[8:]
+
+    def write(half, rows):
+        for p in range(2):
+            low, high = refs[4 * half + 2 * p][...], refs[4 * half + 2 * p + 1][...]
+            for w in range(4):
+                cols = slice(w * HD, (w + 1) * HD)
+                both = jnp.concatenate([low[:, cols], high[:, cols]], axis=1)
+                if w < 3:
+                    qkv_ref[rows, (3 * p + w) * 2 * HD : (3 * p + w + 1) * 2 * HD] = both
+                else:
+                    out_ref[rows, p * 2 * HD : (p + 1) * 2 * HD] = both
+
+    for y in range(2):
+
+        @pl.when(y_ref[0] == y)
+        def _():
+            for half in range(2):
+                write(half, slice((y ^ half) * n, ((y ^ half) + 1) * n))
+
+
+def head_weights(y_index, mine, other):
+    n = mine[0].shape[0]
+    vmem = pl.BlockSpec(memory_space=pltpu.VMEM)
+    return pl.pallas_call(
+        lambda *refs: head_weights_kernel(*refs, n=n),
+        in_specs=[pl.BlockSpec(memory_space=pltpu.SMEM)] + [vmem] * 8,
+        out_specs=[vmem, vmem],
+        out_shape=[
+            jax.ShapeDtypeStruct((2 * n, 12 * HD), BF),
+            jax.ShapeDtypeStruct((2 * n, 4 * HD), BF),
+        ],
+        name="head_weights",
+    )(y_index.reshape(1), *mine, *other)
+
+
 def send_z(parts):
     return [parts[0]] + [across(parts[k], k) for k in (1, 2, 3)]
 
@@ -466,6 +503,10 @@
     stats = relocate(jnp.concatenate([mean_one.reshape(1, -1), inv_one.reshape(1, -1)], axis=0))
     segs = relocate(segment_ids)
 
+    gain_one, shift_one, qv_all, out_shift, gain_two, shift_two, up_all, down_shift = (
+        gather_vectors(vecs, n_dev)
+    )
+
     heads = jnp.concatenate(
         [
             w_qkv.reshape(3, -1, 4, HD).transpose(2, 1, 0, 3).reshape(4, -1, 3 * HD),
@@ -480,11 +521,8 @@
         ],
         axis=2,
     )
-    both = exchange_t(jnp.concatenate([heads, hids], axis=2)).reshape(sub, -1)
-    both, *vecs = tie(both, *vecs)
-    gain_one, shift_one, qv_all, out_shift, gain_two, shift_two, up_all, down_shift = (
-        gather_vectors(vecs, n_dev)
-    )
+    both, shift_one = tie(jnp.concatenate([heads, hids], axis=2), shift_one)
+    both = exchange_t(both).reshape(sub, -1)
     hat_low, stats, segs, gain_one = tie(hat_low, stats, segs, gain_one)
     heads, hids = both[:, : 4 * HD], both[:, 4 * HD :]
     heads_mine = [heads] + [across(heads, k) for k in (1, 2, 3)]
@@ -511,18 +549,8 @@
     )
     heads_other = [swap(heads, 4)]
     heads_other = heads_other + [swap(m, 4) for m in heads_mine[1:]]
-    heads_mine = [h.reshape(sub, 4, HD) for h in heads_mine]
-    heads_other = [h.reshape(sub, 4, HD) for h in heads_other]
-    qkv_order = [(2 * p + k, which) for p in range(2) for which in range(3) for k in range(2)]
-    w_local = by_y(
-        [heads_mine[k][:, w] for k, w in qkv_order],
-        [heads_other[k][:, w] for k, w in qkv_order],
-        y_index,
-    )
-    w_out_t = by_y([h[:, 3] for h in heads_mine], [h[:, 3] for h in heads_other], y_index)
-    w_local, w_out_t = tie(w_local, w_out_t)
+    w_local, w_out_t = head_weights(y_index, heads_mine, heads_other)
     qkv = (dot(rows_one, w_local) + b_local).astype(BF)
-    grad_low, qkv = tie(grad_low, qkv)
     grad_rows = gather_t(grad_low)
     grad_here = grad_low.astype(F32)
     qkv = qkv.reshape(4, -1, w_local.shape[1])
@@ -541,9 +569,9 @@
     resid = block_here + att_sum + out_shift
     hat_two, inv_two = norm_rows(resid)
     rows_two = gather_t((hat_two * gain_two + shift_two).astype(BF))
-    rows_two, grad_rows = tie(rows_two, grad_rows)
     value, slope = gelu_both(dot(rows_two, up_local) + up_shift)
     hidden = value.astype(BF)
+    hidden, grad_rows = tie(hidden, grad_rows)
     down_part = trans_dot(hidden, down_t).astype(BF)
     own_d, near_d, far_d = scatter_near(down_part)
     hidden, own_d = tie(hidden, own_d)
@@ -604,11 +632,11 @@
     g_out = cross_dot(resid_rows, att_rows).astype(BF)
     out_keep, out_got = to_y(g_out)
     one_grad = scatter_far(own, near, far)
-    one_grad, block_back, *parts = tie(one_grad, block_back, *up_parts, *down_parts)
+    one_grad, block_back = tie(one_grad, block_back)
     in_grad = resid_grad + norm_back(one_grad, hat_one, inv_here, gain_one)
     in_back = bring_back(in_grad.astype(BF))
     one_sum = jnp.sum(one_grad, axis=0)
-    one_sum, qkv_got, out_got = tie(one_sum, qkv_got, out_got)
+    one_sum, qkv_got, out_got, *parts = tie(one_sum, qkv_got, out_got, *up_parts, *down_parts)
     both = (qkv_keep.astype(F32) + qkv_got.astype(F32)).astype(BF).reshape(sub, 2, 3, 2, HD)
     both_out = (out_keep.astype(F32) + out_got.astype(F32)).astype(BF).reshape(sub, 2, 1, 2, HD)
     both = jnp.concatenate([both, both_out], axis=2)

time: 499 us -> 500 us (level)
  local copies, waits for them, and re-layouts: 78.3 us -> 35.5 us
  waiting for transfers between devices: 190 us -> 208 us
  starting transfers between devices: 102 us -> 118 us
    ppermute x41, waiting for transfers between devices: 73.5 us -> 107 us  [swap(): return lax.ppermute(x, 'dp', [(i, i ^ bits) for i in range(8)])]
    unnamed x202 -> x122, local copies, waits for them, and re-layouts: 26.1 us -> 5.73 us
    ppermute x17, starting transfers between devices: 51 us -> 61.5 us  [across(): return lax.ppermute(x, 'mp', [(i, i ^ bits) for i in range(4)])]
    ppermute x17, waiting for transfers between devices: 93.3 us -> 84.2 us  [across(): return lax.ppermute(x, 'mp', [(i, i ^ bits) for i in range(4)])]
    all_to_all x1, waiting for transfers between devices: 16.2 us -> 7.58 us  [exchange_t(): return lax.all_to_all(x, 'dp', 0, 0, tiled=True, axis_index_groups=GROUPS)]
    all_to_all x1, starting transfers between devices: 5.68 us -> 14.2 us  [gather_vectors(): got = lax.all_to_all(spread, ('dp', 'mp'), 0, 0, tiled=True)]
    concatenate x2 -> x0, local copies, waits for them, and re-layouts: 5.81 us -> none  [the longest x1 3.06 us: by_y(): jnp.concatenate(mine, axis=1)]
  transfers between devices with their start and end apart: 66 -> 66, of which waited for: 22 -> 29; matrix products, arithmetic and copies ran while one was open for 26% -> 18% of each run, Pallas kernels for 0% -> 3%
where the time goes in v5:
time: 500 us; the launch traced here: 490 us
  waiting for transfers between devices  208 us (42%)
  starting transfers between devices  118 us (24%)
  other arithmetic  50.3 us (10%)
  matrix products  44.4 us (9%)
  local copies, waits for them, and re-layouts  35.5 us (7%)
  Pallas kernels  31.5 us (6%)
    ppermute x41, waiting for transfers between devices, swap(): return lax.ppermute(x, 'dp', [(i, i ^ bits) for i in range(8)])  107 us
    ppermute x17, waiting for transfers between devices, across(): return lax.ppermute(x, 'mp', [(i, i ^ bits) for i in range(4)])  84.2 us
    ppermute x17, starting transfers between devices, across(): return lax.ppermute(x, 'mp', [(i, i ^ bits) for i in range(4)])  61.5 us
    ppermute x41, starting transfers between devices, swap(): return lax.ppermute(x, 'dp', [(i, i ^ bits) for i in range(8)])  29 us
    dot_general x4, matrix products, dot(): return jnp.dot(left, right, preferred_element_type=F32)  16.5 us
    dot_general x4, matrix products, cross_dot(): lax.dot_general(left, right, (((0,), (0,)), ((), ())), preferred_element_...  16.1 us
    pallas_call x1, Pallas kernels, attn_bwd(): pl.pallas_call(lambda *refs: attn_bwd_kernel(*refs, nb=nb, rb=rb), grid=(...  15.3 us
    all_to_all x1, starting transfers between devices, gather_vectors(): got = lax.all_to_all(spread, ('dp', 'mp'), 0, 0, tiled=True)  14.2 us
  transfers between devices with their start and end apart: 66, of which 29 were waited for; matrix products, arithmetic and copies ran while one was open for 18% of the time, Pallas kernels for 3%

profile of v5, /device:TPU:0, one launch (start us, length us, event | category | flops | bytes accessed | tf_op | source)
XLA Modules:
  0.0 490.0 jit_solution(17767024344878641269)
XLA Ops:
  7.8 14.2 %all-to-all-start = ((f32[32,1,384]{2,1,0:T(1,128)}), f32[32,1,384]{2,1,0:T(1,128)S(1)}, u32[]{:S(2)}, u32[]{:S(2)}) async-start(f32[32,1,384]{2,1,0:T(1,128)} %broadcast_in_dim.43), calls=%async_computation | async-start | bytes 98304 | tf_op jit(solution)/shard_map/all_to_all | solution.py:230
  23.7 9.3 %all-to-all-done = f32[32,1,384]{2,1,0:T(1,128)S(1)} async-done(((f32[32,1,384]{2,1,0:T(1,128)}), f32[32,1,384]{2,1,0:T(1,128)S(1)}, u32[]{:S(2)}, u32[]{:S(2)}) %all-to-all-start) | async-done | bytes 49184 | tf_op jit(solution)/shard_map/all_to_all | solution.py:230
  41.9 7.6 %all-to-all-done.1 = bf16[4,128,768]{2,1,0:T(8,128)(2,1)S(1)} async-done(((bf16[4,128,768]{2,1,0:T(8,128)(2,1)}), bf16[4,128,768]{2,1,0:T(8,128)(2,1)S(1)}, u32[]{:S(2)}, u32[]{:S(2)}) %all-to-all-start.1) | async-done | bytes 786464 | tf_op jit(solution)/shard_map/all_to_all | solution.py:409
  55.4 7.5 %collective-permute-done.4.refs_2_ = bf16[512,256]{1,0:T(8,128)(2,1)S(1)} collective-permute-done((bf16[512,256]{1,0:T(8,128)(2,1)S(1)}, bf16[512,256]{1,0:T(8,128)(2,1)S(1)}, u32[]{:S(2)}, u32[]{:S(2)}) %collective-permute-start.4) | collective-permute-done | bytes 262176 | tf_op jit(solution)/shard_map/ppermute | solution.py:431
  62.9 4.2 collective-permute-start.6
  67.1 9.3 %collective-permute-done.5.refs_3_ = bf16[512,256]{1,0:T(8,128)(2,1)S(1)} collective-permute-done((bf16[512,256]{1,0:T(8,128)(2,1)S(1)}, bf16[512,256]{1,0:T(8,128)(2,1)S(1)}, u32[]{:S(2)}, u32[]{:S(2)}) %collective-permute-start.5) | collective-permute-done | bytes 262176 | tf_op jit(solution)/shard_map/ppermute | solution.py:431
  89.2 5.4 %collective-permute-done.11.refs_7_ = bf16[512,256]{1,0:T(8,128)(2,1)} collective-permute-done((bf16[512,256]{1,0:T(8,128)(2,1)S(1)}, bf16[512,256]{1,0:T(8,128)(2,1)}, u32[]{:S(2)}, u32[]{:S(2)}) %collective-permute-start.11) | collective-permute-done | bytes 262176 | tf_op jit(solution)/shard_map/ppermute | solution.py:377
  94.6 5.2 %collective-permute-done.12.refs_8_ = bf16[512,256]{1,0:T(8,128)(2,1)} collective-permute-done((bf16[512,256]{1,0:T(8,128)(2,1)}, bf16[512,256]{1,0:T(8,128)(2,1)}, u32[]{:S(2)}, u32[]{:S(2)}) %collective-permute-start.12) | collective-permute-done | bytes 262176 | tf_op jit(solution)/shard_map/ppermute | solution.py:377
  103.2 5.4 %fusion.5 = bf16[1152,768]{1,0:T(8,128)(2,1)} fusion(bf16[1024,768]{1,0:T(8,128)(2,1)} %get-tuple-element.90, f32[768]{0:T(1024)S(1)} %add.333, bf16[288,1024]{1,0:T(8,128)(2,1)} %collective-permute-done.8, bf16[288,1024]{1,0:T(8,128)(2,1)} %collective-permute-done.7, bf16[288,1024]{1,0:T(8,128)(2,1)} %collective-permute-done.3, bf16[288,1024]{1,0:T(8,128)(2,1)} %fusion.7), kind=kOutput, calls=%fused_computation.22 | convolution fusion | flops 1823145984 | bytes 5704704 | tf_op jit(solution)/shard_map/dot_general | solution.py:48
  108.7 12.7 %attn_fwd.1 = (bf16[4,288,256]{2,1,0:T(8,128)(2,1)}, f32[2,2,1152]{2,1,0:T(2,128)}) custom-call(s32[4]{0:T(128)} %gather_fusion, f32[4]{0:T(128)} %multiply_exponential_fusion.refs_1_, s32[1,1152]{1,0:T(1,128)} %reshape.316.refs_2_, s32[1152,1]{1,0:T(8,128)} %reshape.399.refs_3_, bf16[4,288,768]{2,1,0:T(8,128)(2,1)} %bitcast.175, ...), custom_call_target="tpu_custom_call" | custom-call | flops 2717908992 | bytes 16777216 | tf_op jit(solution)/shard_map/attn_fwd/pallas_call | solution.py:184
  135.2 6.7 %collective-permute-start.15 = (bf16[512,512]{1,0:T(8,128)(2,1)}, bf16[512,512]{1,0:T(8,128)(2,1)S(1)}, u32[]{:S(2)}, u32[]{:S(2)}) collective-permute-start(bf16[512,512]{1,0:T(8,128)(2,1)} %slice.383), channel_id=1, source_target_pairs={{0,1},{1,0},{2,3},{3,2},{4,5},{5,4},{6,7},{7,6},{8,9},{9,8},{10,11... | collective-permute-start | bytes 1572872 | tf_op jit(solution)/shard_map/ppermute | solution.py:431
  142.0 6.3 %collective-permute-start.16 = (bf16[512,512]{1,0:T(8,128)(2,1)}, bf16[512,512]{1,0:T(8,128)(2,1)S(1)}, u32[]{:S(2)}, u32[]{:S(2)}) collective-permute-start(bf16[512,512]{1,0:T(8,128)(2,1)} %slice.383), channel_id=1, source_target_pairs={{0,2},{1,3},{2,0},{3,1},{4,6},{5,7},{6,4},{7,5},{8,10},{9,11},{10,... | collective-permute-start | bytes 1572872 | tf_op jit(solution)/shard_map/ppermute | solution.py:431
  154.6 8.0 %collective-permute-done.15 = bf16[512,512]{1,0:T(8,128)(2,1)S(1)} collective-permute-done((bf16[512,512]{1,0:T(8,128)(2,1)}, bf16[512,512]{1,0:T(8,128)(2,1)S(1)}, u32[]{:S(2)}, u32[]{:S(2)}) %collective-permute-start.15) | collective-permute-done | bytes 524320 | tf_op jit(solution)/shard_map/ppermute | solution.py:431
  162.5 21.2 %collective-permute-done.16 = bf16[512,512]{1,0:T(8,128)(2,1)S(1)} collective-permute-done((bf16[512,512]{1,0:T(8,128)(2,1)}, bf16[512,512]{1,0:T(8,128)(2,1)S(1)}, u32[]{:S(2)}, u32[]{:S(2)}) %collective-permute-start.16) | collective-permute-done | bytes 524320 | tf_op jit(solution)/shard_map/ppermute | solution.py:431
  187.1 9.4 %collective-permute-done.18 = bf16[288,1024]{1,0:T(8,128)(2,1)S(1)} collective-permute-done((bf16[288,1024]{1,0:T(8,128)(2,1)S(1)}, bf16[288,1024]{1,0:T(8,128)(2,1)S(1)}, u32[]{:S(2)}, u32[]{:S(2)}) %collective-permute-start.18) | collective-permute-done | bytes 589856 | tf_op jit(solution)/shard_map/ppermute | solution.py:377
  198.5 11.2 %collective-permute-done.24 = bf16[512,512]{1,0:T(8,128)(2,1)S(1)} collective-permute-done((bf16[512,512]{1,0:T(8,128)(2,1)S(1)}, bf16[512,512]{1,0:T(8,128)(2,1)S(1)}, u32[]{:S(2)}, u32[]{:S(2)}) %collective-permute-start.24) | collective-permute-done | bytes 524320 | tf_op jit(solution)/shard_map/ppermute | solution.py:377
  209.7 7.3 %collective-permute-done.23 = bf16[512,512]{1,0:T(8,128)(2,1)S(1)} collective-permute-done((bf16[512,512]{1,0:T(8,128)(2,1)S(1)}, bf16[512,512]{1,0:T(8,128)(2,1)S(1)}, u32[]{:S(2)}, u32[]{:S(2)}) %collective-permute-start.23) | collective-permute-done | bytes 524320 | tf_op jit(solution)/shard_map/ppermute | solution.py:377
  227.3 4.2 convolution_convert_fusion.6
  232.7 5.9 %fusion.35 = (f32[1024]{0:T(1024)}, bf16[1152,1024]{1,0:T(8,128)(2,1)S(1)}) fusion(f32[1152,1024]{1,0:T(8,128)S(1)} %get-tuple-element.281, bf16[1152,1024]{1,0:T(8,128)(2,1)S(1)} %pad_maximum_fusion.2, bf16[1024,1024]{1,0:T(8,128)(2,1)S(1)} %pad_maximum_fusion.5), kind=kOutput, calls=%fused_computation.176 | convolution fusion | flops 2439511040 | bytes 11538432 | tf_op jit(solution)/shard_map/dot_general | solution.py:48
  249.5 5.3 %convolution_convert_fusion.5 = bf16[1024,1024]{1,0:T(8,128)(2,1)S(1)} fusion(bf16[1152,1024]{1,0:T(8,128)(2,1)} %copy-done.57, bf16[288,1024]{1,0:T(8,128)(2,1)} %copy-done.53, bf16[288,1024]{1,0:T(8,128)(2,1)} %copy-done.51, bf16[288,1024]{1,0:T(8,128)(2,1)} %copy-done.52, bf16[288,1024]{1,0:T(8,128)(2,1)} %copy-done.21), kind=kOutput, calls=%fused_computation.37 | convolution fusion | flops 2426404864 | bytes 6815744 | tf_op jit(solution)/shard_map/dot_general | solution.py:52
  254.8 7.4 %collective-permute-done.32 = bf16[288,1024]{1,0:T(8,128)(2,1)S(1)} collective-permute-done((bf16[288,1024]{1,0:T(8,128)(2,1)}, bf16[288,1024]{1,0:T(8,128)(2,1)S(1)}, u32[]{:S(2)}, u32[]{:S(2)}) %collective-permute-start.32) | collective-permute-done | bytes 589856 | tf_op jit(solution)/shard_map/ppermute | solution.py:377
  264.9 9.1 %collective-permute-done.31 = bf16[288,1024]{1,0:T(8,128)(2,1)S(1)} collective-permute-done((bf16[288,1024]{1,0:T(8,128)(2,1)S(1)}, bf16[288,1024]{1,0:T(8,128)(2,1)S(1)}, u32[]{:S(2)}, u32[]{:S(2)}) %collective-permute-start.31) | collective-permute-done | bytes 589856 | tf_op jit(solution)/shard_map/ppermute | solution.py:377
  279.3 13.1 %collective-permute-done.35 = bf16[288,1024]{1,0:T(8,128)(2,1)S(1)} collective-permute-done((bf16[288,1024]{1,0:T(8,128)(2,1)S(1)}, bf16[288,1024]{1,0:T(8,128)(2,1)S(1)}, u32[]{:S(2)}, u32[]{:S(2)}) %collective-permute-start.35) | collective-permute-done | bytes 589856 | tf_op jit(solution)/shard_map/ppermute | solution.py:377
  293.0 9.8 %collective-permute-done.34 = bf16[512,1024]{1,0:T(8,128)(2,1)S(1)} collective-permute-done((bf16[512,1024]{1,0:T(8,128)(2,1)S(1)}, bf16[512,1024]{1,0:T(8,128)(2,1)S(1)}, u32[]{:S(2)}, u32[]{:S(2)}) %collective-permute-start.34) | collective-permute-done | bytes 1048608 | tf_op jit(solution)/shard_map/ppermute | solution.py:377
  304.6 15.3 %attn_bwd.1 = (bf16[4,288,768]{2,1,0:T(8,128)(2,1)}, f32[2,2,128]{2,1,0:T(2,128)}) custom-call(s32[4]{0:T(128)} %gather_fusion, f32[4]{0:T(128)} %multiply_exponential_fusion.refs_1_, s32[1,1152]{1,0:T(1,128)} %reshape.316.refs_2_, s32[1152,1]{1,0:T(8,128)} %reshape.399.refs_3_, bf16[4,288,768]{2,1,0:T(8,128)(2,1)} %bitcast.178, ...), custom_call_target="tpu_custom_call" | custom-call | flops 5435817984 | bytes 33554432 | tf_op jit(solution)/shard_map/attn_bwd/pallas_call | solution.py:206
  320.0 4.0 convolution_convert_fusion
  329.6 11.8 %collective-permute-start.47 = (bf16[512,256]{1,0:T(8,128)(2,1)}, bf16[512,256]{1,0:T(8,128)(2,1)}, u32[]{:S(2)}, u32[]{:S(2)}) collective-permute-start(bf16[512,256]{1,0:T(8,128)(2,1)} %get-tuple-element.235), channel_id=1, source_target_pairs={{0,1},{1,0},{2,3},{3,2},{4,5},{5,4},{6,7},{7,6},{8,9},{9,8},{10,11... | collective-permute-start | bytes 786440 | tf_op jit(solution)/shard_map/ppermute | solution.py:431
  348.3 6.3 %collective-permute-start.40 = (bf16[288,1024]{1,0:T(8,128)(2,1)}, bf16[288,1024]{1,0:T(8,128)(2,1)}, u32[]{:S(2)}, u32[]{:S(2)}) collective-permute-start(bf16[288,1024]{1,0:T(8,128)(2,1)} %add_convert_fusion.4), channel_id=1, source_target_pairs={{0,0},{8,1},{12,2},{4,3},{3,4},{11,5},{15,6},{7,7},{1,8},{9,9},{13... | collective-permute-start | bytes 1769480 | tf_op jit(solution)/shard_map/ppermute | solution.py:385
  363.8 16.5 %collective-permute-done.39 = bf16[288,1024]{1,0:T(8,128)(2,1)} collective-permute-done((bf16[288,1024]{1,0:T(8,128)(2,1)}, bf16[288,1024]{1,0:T(8,128)(2,1)}, u32[]{:S(2)}, u32[]{:S(2)}) %collective-permute-start.39) | collective-permute-done | bytes 589856 | tf_op jit(solution)/shard_map/ppermute | solution.py:377
  394.6 14.2 %collective-permute-start.62 = (f32[2,384]{1,0:T(2,128)S(1)}, f32[2,384]{1,0:T(2,128)S(1)}, u32[]{:S(2)}, u32[]{:S(2)}) collective-permute-start(f32[2,384]{1,0:T(2,128)S(1)} %bitcast.173), channel_id=1, source_target_pairs={{0,1},{1,0},{2,3},{3,2},{4,5},{5,4},{6,7},{7,6},{8,9},{9,8},{10,11... | collective-permute-start | bytes 9224 | tf_op jit(solution)/shard_map/ppermute | solution.py:431
  425.1 12.2 %collective-permute-done.45 = bf16[512,256]{1,0:T(8,128)(2,1)} collective-permute-done((bf16[512,256]{1,0:T(8,128)(2,1)}, bf16[512,256]{1,0:T(8,128)(2,1)}, u32[]{:S(2)}, u32[]{:S(2)}) %collective-permute-start.45) | collective-permute-done | bytes 262176 | tf_op jit(solution)/shard_map/ppermute | solution.py:431
  456.0 21.4 %collective-permute-done.51 = bf16[512,256]{0,1:T(8,128)(2,1)} collective-permute-done((bf16[512,256]{0,1:T(8,128)(2,1)}, bf16[512,256]{0,1:T(8,128)(2,1)}, u32[]{:S(2)}, u32[]{:S(2)}) %collective-permute-start.51) | collective-permute-done | bytes 262176 | tf_op jit(solution)/shard_map/ppermute | solution.py:431
  (408 shorter events, 180.5 us)
Async XLA Ops:
  4.1 34.8 %collective-permute-start = (bf16[288,1024]{1,0:T(8,128)(2,1)S(1)}, bf16[288,1024]{1,0:T(8,128)(2,1)S(1)}, u32[]{:S(2)}, u32[]{:S(2)}) collective-permute-start(bf16[288,1024]{1,0:T(8,128)(2,1)S(1)} %multiply_convert_fusion.1), channel_id=1, source_target_pairs={{0,0},{1,8},{2,12},{3,4},{4,3},{5,11},{6,15},{7,7},{8,1},{9,9},{10... | collective-permute-start | bytes 1769480 | tf_op jit(solution)/shard_map/ppermute | solution.py:381
  4.9 34.0 %collective-permute-start.1 = (f32[2,288]{1,0:T(2,128)S(1)}, f32[2,288]{1,0:T(2,128)S(1)}, u32[]{:S(2)}, u32[]{:S(2)}) collective-permute-start(f32[2,288]{1,0:T(2,128)S(1)} %pad_maximum_fusion.24), channel_id=1, source_target_pairs={{0,0},{1,8},{2,12},{3,4},{4,3},{5,11},{6,15},{7,7},{8,1},{9,9},{10... | collective-permute-start | bytes 6920 | tf_op jit(solution)/shard_map/ppermute | solution.py:381
  5.5 33.4 %collective-permute-start.2 = (s32[1152]{0:T(1024)}, s32[1152]{0:T(1024)S(1)}, u32[]{:S(2)}, u32[]{:S(2)}) collective-permute-start(s32[1152]{0:T(1024)} %param.19), channel_id=1, source_target_pairs={{0,0},{1,8},{2,12},{3,4},{4,3},{5,11},{6,15},{7,7},{8,1},{9,9},{10... | collective-permute-start | bytes 13832 | tf_op jit(solution)/shard_map/ppermute | solution.py:381
  7.8 25.2 %all-to-all-start = ((f32[32,1,384]{2,1,0:T(1,128)}), f32[32,1,384]{2,1,0:T(1,128)S(1)}, u32[]{:S(2)}, u32[]{:S(2)}) async-start(f32[32,1,384]{2,1,0:T(1,128)} %broadcast_in_dim.43), calls=%async_computation | async-start | bytes 98304 | tf_op jit(solution)/shard_map/all_to_all | solution.py:230
  39.9 37.1 %collective-permute-start.7 = (bf16[288,1024]{1,0:T(8,128)(2,1)}, bf16[288,1024]{1,0:T(8,128)(2,1)}, u32[]{:S(2)}, u32[]{:S(2)}) collective-permute-start(bf16[288,1024]{1,0:T(8,128)(2,1)} %fusion.7), channel_id=1, source_target_pairs={{0,8},{4,12},{8,0},{12,4},{16,24},{20,28},{24,16},{28,20},{1,9},{5... | collective-permute-start | bytes 1769480 | tf_op jit(solution)/shard_map/ppermute | solution.py:377
  50.4 26.1 %collective-permute-start.5 = (bf16[512,256]{1,0:T(8,128)(2,1)S(1)}, bf16[512,256]{1,0:T(8,128)(2,1)S(1)}, u32[]{:S(2)}, u32[]{:S(2)}) collective-permute-start(bf16[512,256]{1,0:T(8,128)(2,1)S(1)} %get-tuple-element.243.refs_1_), channel_id=1, source_target_pairs={{0,2},{1,3},{2,0},{3,1},{4,6},{5,7},{6,4},{7,5},{8,10},{9,11},{10,... | collective-permute-start | bytes 786440 | tf_op jit(solution)/shard_map/ppermute | solution.py:431
  53.4 26.2 %collective-permute-start.3 = (bf16[288,1024]{1,0:T(8,128)(2,1)}, bf16[288,1024]{1,0:T(8,128)(2,1)}, u32[]{:S(2)}, u32[]{:S(2)}) collective-permute-start(bf16[288,1024]{1,0:T(8,128)(2,1)} %fusion.7), channel_id=1, source_target_pairs={{0,4},{4,0},{8,12},{12,8},{16,20},{20,16},{24,28},{28,24},{1,5},{5... | collective-permute-start | bytes 1769480 | tf_op jit(solution)/shard_map/ppermute | solution.py:377
  54.7 30.7 %collective-permute-start.13 = (bf16[288,1024]{1,0:T(8,128)(2,1)S(1)}, bf16[288,1024]{1,0:T(8,128)(2,1)S(1)}, u32[]{:S(2)}, u32[]{:S(2)}) collective-permute-start(bf16[288,1024]{1,0:T(8,128)(2,1)S(1)} %copy-done.20), channel_id=1, source_target_pairs={{0,0},{1,8},{2,12},{3,4},{4,3},{5,11},{6,15},{7,7},{8,1},{9,9},{10... | collective-permute-start | bytes 1769480 | tf_op jit(solution)/shard_map/ppermute | solution.py:381
  77.0 26.3 %collective-permute-start.8 = (bf16[288,1024]{1,0:T(8,128)(2,1)}, bf16[288,1024]{1,0:T(8,128)(2,1)}, u32[]{:S(2)}, u32[]{:S(2)}) collective-permute-start(bf16[288,1024]{1,0:T(8,128)(2,1)} %collective-permute-done.7), channel_id=1, source_target_pairs={{0,4},{4,0},{8,12},{12,8},{16,20},{20,16},{24,28},{28,24},{1,5},{5... | collective-permute-start | bytes 1769480 | tf_op jit(solution)/shard_map/ppermute | solution.py:377
  85.4 44.6 %collective-permute-start.27 = (bf16[288,1024]{1,0:T(8,128)(2,1)S(1)}, bf16[288,1024]{1,0:T(8,128)(2,1)}, u32[]{:S(2)}, u32[]{:S(2)}) collective-permute-start(bf16[288,1024]{1,0:T(8,128)(2,1)S(1)} %collective-permute-done.13), channel_id=1, source_target_pairs={{0,8},{4,12},{8,0},{12,4},{16,24},{20,28},{24,16},{28,20},{1,9},{5... | collective-permute-start | bytes 1769480 | tf_op jit(solution)/shard_map/ppermute | solution.py:377
  124.7 28.2 %collective-permute-start.14 = (bf16[576,1024]{1,0:T(8,128)(2,1)}, bf16[576,1024]{1,0:T(8,128)(2,1)}, u32[]{:S(2)}, u32[]{:S(2)}) collective-permute-start(bf16[576,1024]{1,0:T(8,128)(2,1)} %pad_maximum_fusion.6), channel_id=1, source_target_pairs={{0,4},{4,0},{8,12},{12,8},{16,20},{20,16},{24,28},{28,24},{1,5},{5... | collective-permute-start | bytes 3538952 | tf_op jit(solution)/shard_map/ppermute | solution.py:377
  129.9 21.3 %collective-permute-start.28 = (bf16[288,1024]{1,0:T(8,128)(2,1)}, bf16[288,1024]{1,0:T(8,128)(2,1)}, u32[]{:S(2)}, u32[]{:S(2)}) collective-permute-start(bf16[288,1024]{1,0:T(8,128)(2,1)} %collective-permute-done.27), channel_id=1, source_target_pairs={{0,4},{4,0},{8,12},{12,8},{16,20},{20,16},{24,28},{28,24},{1,5},{5... | collective-permute-start | bytes 1769480 | tf_op jit(solution)/shard_map/ppermute | solution.py:377
  135.2 27.3 %collective-permute-start.15 = (bf16[512,512]{1,0:T(8,128)(2,1)}, bf16[512,512]{1,0:T(8,128)(2,1)S(1)}, u32[]{:S(2)}, u32[]{:S(2)}) collective-permute-start(bf16[512,512]{1,0:T(8,128)(2,1)} %slice.383), channel_id=1, source_target_pairs={{0,1},{1,0},{2,3},{3,2},{4,5},{5,4},{6,7},{7,6},{8,9},{9,8},{10,11... | collective-permute-start | bytes 1572872 | tf_op jit(solution)/shard_map/ppermute | solution.py:431
  142.0 41.7 %collective-permute-start.16 = (bf16[512,512]{1,0:T(8,128)(2,1)}, bf16[512,512]{1,0:T(8,128)(2,1)S(1)}, u32[]{:S(2)}, u32[]{:S(2)}) collective-permute-start(bf16[512,512]{1,0:T(8,128)(2,1)} %slice.383), channel_id=1, source_target_pairs={{0,2},{1,3},{2,0},{3,1},{4,6},{5,7},{6,4},{7,5},{8,10},{9,11},{10,... | collective-permute-start | bytes 1572872 | tf_op jit(solution)/shard_map/ppermute | solution.py:431
  149.3 34.4 %collective-permute-start.17 = (bf16[512,512]{1,0:T(8,128)(2,1)}, bf16[512,512]{1,0:T(8,128)(2,1)S(1)}, u32[]{:S(2)}, u32[]{:S(2)}) collective-permute-start(bf16[512,512]{1,0:T(8,128)(2,1)} %slice.383), channel_id=1, source_target_pairs={{0,3},{1,2},{2,1},{3,0},{4,7},{5,6},{6,5},{7,4},{8,11},{9,10},{10,... | collective-permute-start | bytes 1572872 | tf_op jit(solution)/shard_map/ppermute | solution.py:431
  184.9 24.8 %collective-permute-start.24 = (bf16[512,512]{1,0:T(8,128)(2,1)S(1)}, bf16[512,512]{1,0:T(8,128)(2,1)S(1)}, u32[]{:S(2)}, u32[]{:S(2)}) collective-permute-start(bf16[512,512]{1,0:T(8,128)(2,1)S(1)} %collective-permute-done.16), channel_id=1, source_target_pairs={{0,16},{4,20},{8,24},{12,28},{16,0},{20,4},{24,8},{28,12},{1,17},{... | collective-permute-start | bytes 1572872 | tf_op jit(solution)/shard_map/ppermute | solution.py:377
  186.5 30.6 %collective-permute-start.23 = (bf16[512,512]{1,0:T(8,128)(2,1)S(1)}, bf16[512,512]{1,0:T(8,128)(2,1)S(1)}, u32[]{:S(2)}, u32[]{:S(2)}) collective-permute-start(bf16[512,512]{1,0:T(8,128)(2,1)S(1)} %collective-permute-done.15), channel_id=1, source_target_pairs={{0,16},{4,20},{8,24},{12,28},{16,0},{20,4},{24,8},{28,12},{1,17},{... | collective-permute-start | bytes 1572872 | tf_op jit(solution)/shard_map/ppermute | solution.py:377
  248.7 25.3 %collective-permute-start.31 = (bf16[288,1024]{1,0:T(8,128)(2,1)S(1)}, bf16[288,1024]{1,0:T(8,128)(2,1)S(1)}, u32[]{:S(2)}, u32[]{:S(2)}) collective-permute-start(bf16[288,1024]{1,0:T(8,128)(2,1)S(1)} %add_convert_fusion.5), channel_id=1, source_target_pairs={{0,8},{4,12},{8,0},{12,4},{16,24},{20,28},{24,16},{28,20},{1,9},{5... | collective-permute-start | bytes 1769480 | tf_op jit(solution)/shard_map/ppermute | solution.py:377
  278.7 24.1 %collective-permute-start.34 = (bf16[512,1024]{1,0:T(8,128)(2,1)S(1)}, bf16[512,1024]{1,0:T(8,128)(2,1)S(1)}, u32[]{:S(2)}, u32[]{:S(2)}) collective-permute-start(bf16[512,1024]{1,0:T(8,128)(2,1)S(1)} %broadcast_select_fusion.1), channel_id=1, source_target_pairs={{0,16},{4,20},{8,24},{12,28},{16,0},{20,4},{24,8},{28,12},{1,17},{... | collective-permute-start | bytes 3145736 | tf_op jit(solution)/shard_map/ppermute | solution.py:377
  279.3 23.5 %collective-permute-start.33 = (bf16[288,1024]{1,0:T(8,128)(2,1)S(1)}, bf16[288,1024]{1,0:T(8,128)(2,1)S(1)}, u32[]{:S(2)}, u32[]{:S(2)}) collective-permute-start(bf16[288,1024]{1,0:T(8,128)(2,1)S(1)} %convert_element_type.272), channel_id=1, source_target_pairs={{0,4},{4,0},{8,12},{12,8},{16,20},{20,16},{24,28},{28,24},{1,5},{5... | collective-permute-start | bytes 1769480 | tf_op jit(solution)/shard_map/ppermute | solution.py:377
  325.7 22.6 %collective-permute-start.37 = (bf16[576,1024]{1,0:T(8,128)(2,1)}, bf16[576,1024]{1,0:T(8,128)(2,1)}, u32[]{:S(2)}, u32[]{:S(2)}) collective-permute-start(bf16[576,1024]{1,0:T(8,128)(2,1)} %pad_maximum_fusion.9), channel_id=1, source_target_pairs={{0,4},{4,0},{8,12},{12,8},{16,20},{20,16},{24,28},{28,24},{1,5},{5... | collective-permute-start | bytes 3538952 | tf_op jit(solution)/shard_map/ppermute | solution.py:377
  325.9 31.0 %collective-permute-start.38 = (bf16[512,1024]{1,0:T(8,128)(2,1)}, bf16[512,1024]{1,0:T(8,128)(2,1)}, u32[]{:S(2)}, u32[]{:S(2)}) collective-permute-start(bf16[512,1024]{1,0:T(8,128)(2,1)} %get-tuple-element.219), channel_id=1, source_target_pairs={{0,16},{4,20},{8,24},{12,28},{16,0},{20,4},{24,8},{28,12},{1,17},{... | collective-permute-start | bytes 3145736 | tf_op jit(solution)/shard_map/ppermute | solution.py:377
  329.6 84.1 %collective-permute-start.47 = (bf16[512,256]{1,0:T(8,128)(2,1)}, bf16[512,256]{1,0:T(8,128)(2,1)}, u32[]{:S(2)}, u32[]{:S(2)}) collective-permute-start(bf16[512,256]{1,0:T(8,128)(2,1)} %get-tuple-element.235), channel_id=1, source_target_pairs={{0,1},{1,0},{2,3},{3,2},{4,5},{5,4},{6,7},{7,6},{8,9},{9,8},{10,11... | collective-permute-start | bytes 786440 | tf_op jit(solution)/shard_map/ppermute | solution.py:431
  341.4 73.8 %collective-permute-start.48 = (bf16[512,256]{1,0:T(8,128)(2,1)}, bf16[512,256]{1,0:T(8,128)(2,1)}, u32[]{:S(2)}, u32[]{:S(2)}) collective-permute-start(bf16[512,256]{1,0:T(8,128)(2,1)} %get-tuple-element.234), channel_id=1, source_target_pairs={{0,2},{1,3},{2,0},{3,1},{4,6},{5,7},{6,4},{7,5},{8,10},{9,11},{10,... | collective-permute-start | bytes 786440 | tf_op jit(solution)/shard_map/ppermute | solution.py:431
  342.9 73.5 %collective-permute-start.49 = (bf16[512,256]{1,0:T(8,128)(2,1)}, bf16[512,256]{1,0:T(8,128)(2,1)}, u32[]{:S(2)}, u32[]{:S(2)}) collective-permute-start(bf16[512,256]{1,0:T(8,128)(2,1)} %get-tuple-element.233), channel_id=1, source_target_pairs={{0,3},{1,2},{2,1},{3,0},{4,7},{5,6},{6,5},{7,4},{8,11},{9,10},{10,... | collective-permute-start | bytes 786440 | tf_op jit(solution)/shard_map/ppermute | solution.py:431
  348.3 35.2 %collective-permute-start.40 = (bf16[288,1024]{1,0:T(8,128)(2,1)}, bf16[288,1024]{1,0:T(8,128)(2,1)}, u32[]{:S(2)}, u32[]{:S(2)}) collective-permute-start(bf16[288,1024]{1,0:T(8,128)(2,1)} %add_convert_fusion.4), channel_id=1, source_target_pairs={{0,0},{8,1},{12,2},{4,3},{3,4},{11,5},{15,6},{7,7},{1,8},{9,9},{13... | collective-permute-start | bytes 1769480 | tf_op jit(solution)/shard_map/ppermute | solution.py:385
  356.9 23.4 %collective-permute-start.39 = (bf16[288,1024]{1,0:T(8,128)(2,1)}, bf16[288,1024]{1,0:T(8,128)(2,1)}, u32[]{:S(2)}, u32[]{:S(2)}) collective-permute-start(bf16[288,1024]{1,0:T(8,128)(2,1)} %add_convert_fusion.3), channel_id=1, source_target_pairs={{0,8},{4,12},{8,0},{12,4},{16,24},{20,28},{24,16},{28,20},{1,9},{5... | collective-permute-start | bytes 1769480 | tf_op jit(solution)/shard_map/ppermute | solution.py:377
  380.3 57.0 %collective-permute-start.42 = (bf16[512,768]{1,0:T(8,128)(2,1)}, bf16[512,768]{1,0:T(8,128)(2,1)}, u32[]{:S(2)}, u32[]{:S(2)}) collective-permute-start(bf16[512,768]{1,0:T(8,128)(2,1)} %broadcast_select_fusion.7), channel_id=1, source_target_pairs={{0,16},{4,20},{8,24},{12,28},{16,0},{20,4},{24,8},{28,12},{1,17},{... | collective-permute-start | bytes 2359304 | tf_op jit(solution)/shard_map/ppermute | solution.py:377
  416.3 21.0 %collective-permute-start.45 = (bf16[512,256]{1,0:T(8,128)(2,1)}, bf16[512,256]{1,0:T(8,128)(2,1)}, u32[]{:S(2)}, u32[]{:S(2)}) collective-permute-start(bf16[512,256]{1,0:T(8,128)(2,1)} %get-tuple-element.238), channel_id=1, source_target_pairs={{0,2},{1,3},{2,0},{3,1},{4,6},{5,7},{6,4},{7,5},{8,10},{9,11},{10,... | collective-permute-start | bytes 786440 | tf_op jit(solution)/shard_map/ppermute | solution.py:431
  446.1 31.3 %collective-permute-start.51 = (bf16[512,256]{0,1:T(8,128)(2,1)}, bf16[512,256]{0,1:T(8,128)(2,1)}, u32[]{:S(2)}, u32[]{:S(2)}) collective-permute-start(bf16[512,256]{0,1:T(8,128)(2,1)} %bitcast.27), channel_id=1, source_target_pairs={{0,2},{1,3},{2,0},{3,1},{4,6},{5,7},{6,4},{7,5},{8,10},{9,11},{10,... | collective-permute-start | bytes 786440 | tf_op jit(solution)/shard_map/ppermute | solution.py:431
  449.1 28.4 %collective-permute-start.50 = (bf16[512,256]{0,1:T(8,128)(2,1)}, bf16[512,256]{0,1:T(8,128)(2,1)}, u32[]{:S(2)}, u32[]{:S(2)}) collective-permute-start(bf16[512,256]{0,1:T(8,128)(2,1)} %bitcast.26), channel_id=1, source_target_pairs={{0,1},{1,0},{2,3},{3,2},{4,5},{5,4},{6,7},{7,6},{8,9},{9,8},{10,11... | collective-permute-start | bytes 786440 | tf_op jit(solution)/shard_map/ppermute | solution.py:431
  454.3 34.4 %collective-permute-start.41 = (bf16[288,1024]{1,0:T(8,128)(2,1)S(1)}, bf16[288,1024]{1,0:T(8,128)(2,1)S(1)}, u32[]{:S(2)}, u32[]{:S(2)}) collective-permute-start(bf16[288,1024]{1,0:T(8,128)(2,1)S(1)} %copy-done.22), channel_id=1, source_target_pairs={{0,0},{8,1},{12,2},{4,3},{3,4},{11,5},{15,6},{7,7},{1,8},{9,9},{13... | collective-permute-start | bytes 1769480 | tf_op jit(solution)/shard_map/ppermute | solution.py:385
  (92 other events, 1099.4 us)

commit v6 on v5

--- a/solution.py
+++ b/solution.py
@@ -551,8 +551,6 @@
     heads_other = heads_other + [swap(m, 4) for m in heads_mine[1:]]
     w_local, w_out_t = head_weights(y_index, heads_mine, heads_other)
     qkv = (dot(rows_one, w_local) + b_local).astype(BF)
-    grad_rows = gather_t(grad_low)
-    grad_here = grad_low.astype(F32)
     qkv = qkv.reshape(4, -1, w_local.shape[1])
     att, lse = attn_fwd(order, slopes, segs, qkv)
     att_rows = att.reshape(-1, att.shape[2])
@@ -568,8 +566,15 @@
     up_local, down_t = tie(up_local, down_t)
     resid = block_here + att_sum + out_shift
     hat_two, inv_two = norm_rows(resid)
-    rows_two = gather_t((hat_two * gain_two + shift_two).astype(BF))
-    value, slope = gelu_both(dot(rows_two, up_local) + up_shift)
+    normed = (hat_two * gain_two + shift_two).astype(BF)
+    far = swap(normed, 2)
+    near = swap(normed, 1)
+    far, grad_low = tie(far, grad_low)
+    rows_two = jnp.concatenate([normed, near, far, swap(far, 1)], axis=0)
+    grad_rows = gather_t(grad_low)
+    grad_here = grad_low.astype(F32)
+    pre_act = dot(rows_two, up_local)
+    value, slope = gelu_both(pre_act + up_shift)
     hidden = value.astype(BF)
     hidden, grad_rows = tie(hidden, grad_rows)
     down_part = trans_dot(hidden, down_t).astype(BF)

time: 500 us -> 502 us (level)
  waiting for transfers between devices: 208 us -> 217 us
    ppermute x41, starting transfers between devices: 29 us -> 38 us  [swap(): return lax.ppermute(x, 'dp', [(i, i ^ bits) for i in range(8)])]
    ppermute x41, waiting for transfers between devices: 107 us -> 115 us  [swap(): return lax.ppermute(x, 'dp', [(i, i ^ bits) for i in range(8)])]
    ppermute x17, starting transfers between devices: 61.5 us -> 53.3 us  [across(): return lax.ppermute(x, 'mp', [(i, i ^ bits) for i in range(4)])]
  transfers between devices with their start and end apart: 66 -> 66, of which waited for: 29 -> 27; matrix products, arithmetic and copies ran while one was open for 18% -> 15% of each run, Pallas kernels for 3% -> 1%
where the time goes in v6:
time: 502 us; the launch traced here: 496 us
  waiting for transfers between devices  217 us (43%)
  starting transfers between devices  120 us (24%)
  other arithmetic  48.9 us (10%)
  matrix products  44.2 us (9%)
  local copies, waits for them, and re-layouts  31.8 us (6%)
  Pallas kernels  31.3 us (6%)
    ppermute x41, waiting for transfers between devices, swap(): return lax.ppermute(x, 'dp', [(i, i ^ bits) for i in range(8)])  115 us
    ppermute x17, waiting for transfers between devices, across(): return lax.ppermute(x, 'mp', [(i, i ^ bits) for i in range(4)])  88 us
    ppermute x17, starting transfers between devices, across(): return lax.ppermute(x, 'mp', [(i, i ^ bits) for i in range(4)])  53.3 us
    ppermute x41, starting transfers between devices, swap(): return lax.ppermute(x, 'dp', [(i, i ^ bits) for i in range(8)])  38 us
    dot_general x4, matrix products, dot(): return jnp.dot(left, right, preferred_element_type=F32)  16.1 us
    dot_general x4, matrix products, cross_dot(): lax.dot_general(left, right, (((0,), (0,)), ((), ())), preferred_element_...  16 us
    pallas_call x1, Pallas kernels, attn_bwd(): pl.pallas_call(lambda *refs: attn_bwd_kernel(*refs, nb=nb, rb=rb), grid=(...  15.1 us
    pallas_call x1, Pallas kernels, attn_fwd(): pl.pallas_call(lambda *refs: attn_fwd_kernel(*refs, nb=nb, rb=rb), grid=(...  12.6 us
  transfers between devices with their start and end apart: 66, of which 27 were waited for; matrix products, arithmetic and copies ran while one was open for 15% of the time, Pallas kernels for 1%

profile of v6, /device:TPU:0, one launch (start us, length us, event | category | flops | bytes accessed | tf_op | source)
XLA Modules:
  0.0 496.1 jit_solution(12911866004246646298)
XLA Ops:
  10.8 12.5 %all-to-all-start = ((f32[32,1,384]{2,1,0:T(1,128)}), f32[32,1,384]{2,1,0:T(1,128)S(1)}, u32[]{:S(2)}, u32[]{:S(2)}) async-start(f32[32,1,384]{2,1,0:T(1,128)} %broadcast_in_dim.43), calls=%async_computation | async-start | bytes 98304 | tf_op jit(solution)/shard_map/all_to_all | solution.py:230
  28.3 5.7 %all-to-all-done = f32[32,1,384]{2,1,0:T(1,128)S(1)} async-done(((f32[32,1,384]{2,1,0:T(1,128)}), f32[32,1,384]{2,1,0:T(1,128)S(1)}, u32[]{:S(2)}, u32[]{:S(2)}) %all-to-all-start) | async-done | bytes 49184 | tf_op jit(solution)/shard_map/all_to_all | solution.py:230
  42.1 8.6 %all-to-all-done.1 = bf16[4,128,768]{2,1,0:T(8,128)(2,1)S(1)} async-done(((bf16[4,128,768]{2,1,0:T(8,128)(2,1)}), bf16[4,128,768]{2,1,0:T(8,128)(2,1)S(1)}, u32[]{:S(2)}, u32[]{:S(2)}) %all-to-all-start.1) | async-done | bytes 786464 | tf_op jit(solution)/shard_map/all_to_all | solution.py:409
  56.0 6.9 %collective-permute-done.7 = bf16[288,1024]{1,0:T(8,128)(2,1)} collective-permute-done((bf16[288,1024]{1,0:T(8,128)(2,1)S(1)}, bf16[288,1024]{1,0:T(8,128)(2,1)}, u32[]{:S(2)}, u32[]{:S(2)}) %collective-permute-start.7) | collective-permute-done | bytes 589856 | tf_op jit(solution)/shard_map/ppermute | solution.py:377
  66.1 6.9 %collective-permute-done.5.refs_3_ = bf16[512,256]{1,0:T(8,128)(2,1)S(1)} collective-permute-done((bf16[512,256]{1,0:T(8,128)(2,1)S(1)}, bf16[512,256]{1,0:T(8,128)(2,1)S(1)}, u32[]{:S(2)}, u32[]{:S(2)}) %collective-permute-start.5) | collective-permute-done | bytes 262176 | tf_op jit(solution)/shard_map/ppermute | solution.py:431
  77.5 4.8 collective-permute-done.10.refs_6_
  82.4 5.6 %collective-permute-done.11.refs_7_ = bf16[512,256]{1,0:T(8,128)(2,1)} collective-permute-done((bf16[512,256]{1,0:T(8,128)(2,1)S(1)}, bf16[512,256]{1,0:T(8,128)(2,1)}, u32[]{:S(2)}, u32[]{:S(2)}) %collective-permute-start.11) | collective-permute-done | bytes 262176 | tf_op jit(solution)/shard_map/ppermute | solution.py:377
  94.8 5.3 %fusion.5 = bf16[1152,768]{1,0:T(8,128)(2,1)} fusion(bf16[1024,768]{1,0:T(8,128)(2,1)} %get-tuple-element.92, f32[768]{0:T(1024)S(1)} %add.333, bf16[288,1024]{1,0:T(8,128)(2,1)} %collective-permute-done.8, bf16[288,1024]{1,0:T(8,128)(2,1)} %collective-permute-done.7, bf16[288,1024]{1,0:T(8,128)(2,1)} %collective-permute-done.3, ...), kind=kOutput, calls=%fused_computation.22 | convolution fusion | flops 1823145984 | bytes 5704704 | tf_op jit(solution)/shard_map/dot_general | solution.py:48
  100.1 12.6 %attn_fwd.1 = (bf16[4,288,256]{2,1,0:T(8,128)(2,1)}, f32[2,2,1152]{2,1,0:T(2,128)}) custom-call(s32[4]{0:T(128)} %gather_fusion, f32[4]{0:T(128)} %multiply_exponential_fusion.refs_1_, s32[1,1152]{1,0:T(1,128)} %reshape.316.refs_2_, s32[1152,1]{1,0:T(8,128)} %reshape.399.refs_3_, bf16[4,288,768]{2,1,0:T(8,128)(2,1)} %bitcast.175, ...), custom_call_target="tpu_custom_call" | custom-call | flops 2717908992 | bytes 16777216 | tf_op jit(solution)/shard_map/attn_fwd/pallas_call | solution.py:184
  127.0 4.3 collective-permute-done.22
  136.6 42.7 %collective-permute-done.14 = bf16[512,512]{1,0:T(8,128)(2,1)S(1)} collective-permute-done((bf16[512,512]{1,0:T(8,128)(2,1)}, bf16[512,512]{1,0:T(8,128)(2,1)S(1)}, u32[]{:S(2)}, u32[]{:S(2)}) %collective-permute-start.14) | collective-permute-done | bytes 524320 | tf_op jit(solution)/shard_map/ppermute | solution.py:431
  184.0 8.8 %collective-permute-done.17 = bf16[288,1024]{1,0:T(8,128)(2,1)S(1)} collective-permute-done((bf16[288,1024]{1,0:T(8,128)(2,1)S(1)}, bf16[288,1024]{1,0:T(8,128)(2,1)S(1)}, u32[]{:S(2)}, u32[]{:S(2)}) %collective-permute-start.17) | collective-permute-done | bytes 589856 | tf_op jit(solution)/shard_map/ppermute | solution.py:377
  195.3 6.5 %collective-permute-done.24 = bf16[512,512]{1,0:T(8,128)(2,1)S(1)} collective-permute-done((bf16[512,512]{1,0:T(8,128)(2,1)S(1)}, bf16[512,512]{1,0:T(8,128)(2,1)S(1)}, u32[]{:S(2)}, u32[]{:S(2)}) %collective-permute-start.24) | collective-permute-done | bytes 524320 | tf_op jit(solution)/shard_map/ppermute | solution.py:377
  201.9 5.6 %collective-permute-done.23 = bf16[512,512]{1,0:T(8,128)(2,1)S(1)} collective-permute-done((bf16[512,512]{1,0:T(8,128)(2,1)S(1)}, bf16[512,512]{1,0:T(8,128)(2,1)S(1)}, u32[]{:S(2)}, u32[]{:S(2)}) %collective-permute-start.23) | collective-permute-done | bytes 524320 | tf_op jit(solution)/shard_map/ppermute | solution.py:377
  207.6 4.6 collective-permute-start.27
  214.8 11.4 %collective-permute-done.27 = bf16[288,1024]{1,0:T(8,128)(2,1)S(1)} collective-permute-done((bf16[288,1024]{1,0:T(8,128)(2,1)S(1)}, bf16[288,1024]{1,0:T(8,128)(2,1)S(1)}, u32[]{:S(2)}, u32[]{:S(2)}) %collective-permute-start.27) | collective-permute-done | bytes 589856 | tf_op jit(solution)/shard_map/ppermute | solution.py:377
  233.8 4.2 convolution_convert_fusion.6
  239.2 5.6 %fusion.35 = (f32[1024]{0:T(1024)}, bf16[1152,1024]{1,0:T(8,128)(2,1)S(1)}) fusion(f32[1152,1024]{1,0:T(8,128)S(1)} %get-tuple-element.285, bf16[1152,1024]{1,0:T(8,128)(2,1)S(1)} %pad_maximum_fusion.2, bf16[1024,1024]{1,0:T(8,128)(2,1)S(1)} %pad_maximum_fusion.5), kind=kOutput, calls=%fused_computation.176 | convolution fusion | flops 2439511040 | bytes 11538432 | tf_op jit(solution)/shard_map/dot_general | solution.py:48
  257.3 5.3 %convolution_convert_fusion.5 = bf16[1024,1024]{1,0:T(8,128)(2,1)S(1)} fusion(bf16[1152,1024]{1,0:T(8,128)(2,1)} %copy-done.59, bf16[288,1024]{1,0:T(8,128)(2,1)} %copy-done.55, bf16[288,1024]{1,0:T(8,128)(2,1)} %copy-done.53, bf16[288,1024]{1,0:T(8,128)(2,1)} %copy-done.54, bf16[288,1024]{1,0:T(8,128)(2,1)} %copy-done.19), kind=kOutput, calls=%fused_computation.37 | convolution fusion | flops 2426404864 | bytes 6815744 | tf_op jit(solution)/shard_map/dot_general | solution.py:52
  262.6 6.0 %collective-permute-done.32 = bf16[288,1024]{1,0:T(8,128)(2,1)S(1)} collective-permute-done((bf16[288,1024]{1,0:T(8,128)(2,1)}, bf16[288,1024]{1,0:T(8,128)(2,1)S(1)}, u32[]{:S(2)}, u32[]{:S(2)}) %collective-permute-start.32) | collective-permute-done | bytes 589856 | tf_op jit(solution)/shard_map/ppermute | solution.py:377
  271.3 9.5 %collective-permute-done.31 = bf16[288,1024]{1,0:T(8,128)(2,1)S(1)} collective-permute-done((bf16[288,1024]{1,0:T(8,128)(2,1)S(1)}, bf16[288,1024]{1,0:T(8,128)(2,1)S(1)}, u32[]{:S(2)}, u32[]{:S(2)}) %collective-permute-start.31) | collective-permute-done | bytes 589856 | tf_op jit(solution)/shard_map/ppermute | solution.py:377
  288.1 11.4 %collective-permute-done.35 = bf16[288,1024]{1,0:T(8,128)(2,1)S(1)} collective-permute-done((bf16[288,1024]{1,0:T(8,128)(2,1)S(1)}, bf16[288,1024]{1,0:T(8,128)(2,1)S(1)}, u32[]{:S(2)}, u32[]{:S(2)}) %collective-permute-start.35) | collective-permute-done | bytes 589856 | tf_op jit(solution)/shard_map/ppermute | solution.py:377
  299.6 11.4 %collective-permute-done.34 = bf16[512,1024]{1,0:T(8,128)(2,1)S(1)} collective-permute-done((bf16[512,1024]{1,0:T(8,128)(2,1)S(1)}, bf16[512,1024]{1,0:T(8,128)(2,1)S(1)}, u32[]{:S(2)}, u32[]{:S(2)}) %collective-permute-start.34) | collective-permute-done | bytes 1048608 | tf_op jit(solution)/shard_map/ppermute | solution.py:377
  312.8 15.1 %attn_bwd.1 = (bf16[4,288,768]{2,1,0:T(8,128)(2,1)}, f32[2,2,128]{2,1,0:T(2,128)}) custom-call(s32[4]{0:T(128)} %gather_fusion, f32[4]{0:T(128)} %multiply_exponential_fusion.refs_1_, s32[1,1152]{1,0:T(1,128)} %reshape.316.refs_2_, s32[1152,1]{1,0:T(8,128)} %reshape.399.refs_3_, bf16[4,288,768]{2,1,0:T(8,128)(2,1)} %bitcast.178, ...), custom_call_target="tpu_custom_call" | custom-call | flops 5435817984 | bytes 33554432 | tf_op jit(solution)/shard_map/attn_bwd/pallas_call | solution.py:206
  327.9 4.0 convolution_convert_fusion
  338.7 10.7 %collective-permute-start.47 = (bf16[512,256]{1,0:T(8,128)(2,1)}, bf16[512,256]{1,0:T(8,128)(2,1)}, u32[]{:S(2)}, u32[]{:S(2)}) collective-permute-start(bf16[512,256]{1,0:T(8,128)(2,1)} %get-tuple-element.239), channel_id=1, source_target_pairs={{0,1},{1,0},{2,3},{3,2},{4,5},{5,4},{6,7},{7,6},{8,9},{9,8},{10,11... | collective-permute-start | bytes 786440 | tf_op jit(solution)/shard_map/ppermute | solution.py:431
  355.8 6.1 %collective-permute-start.40 = (bf16[288,1024]{1,0:T(8,128)(2,1)}, bf16[288,1024]{1,0:T(8,128)(2,1)}, u32[]{:S(2)}, u32[]{:S(2)}) collective-permute-start(bf16[288,1024]{1,0:T(8,128)(2,1)} %add_convert_fusion.4), channel_id=1, source_target_pairs={{0,0},{8,1},{12,2},{4,3},{3,4},{11,5},{15,6},{7,7},{1,8},{9,9},{13... | collective-permute-start | bytes 1769480 | tf_op jit(solution)/shard_map/ppermute | solution.py:385
  371.1 9.4 %collective-permute-done.39 = bf16[288,1024]{1,0:T(8,128)(2,1)} collective-permute-done((bf16[288,1024]{1,0:T(8,128)(2,1)}, bf16[288,1024]{1,0:T(8,128)(2,1)}, u32[]{:S(2)}, u32[]{:S(2)}) %collective-permute-start.39) | collective-permute-done | bytes 589856 | tf_op jit(solution)/shard_map/ppermute | solution.py:377
  385.9 6.9 %collective-permute-start.60 = (f32[2,2,2,384]{3,2,1,0:T(2,128)S(1)}, f32[2,2,2,384]{3,2,1,0:T(2,128)S(1)}, u32[]{:S(2)}, u32[]{:S(2)}) collective-permute-start(f32[2,2,2,384]{3,2,1,0:T(2,128)S(1)} %dynamic-slice_bitcast_fusion.7), channel_id=1, source_target_pairs={{0,8},{4,12},{8,0},{12,4},{16,24},{20,28},{24,16},{28,20},{1,9},{5... | collective-permute-start | bytes 36872 | tf_op jit(solution)/shard_map/ppermute | solution.py:377
  398.2 17.8 %collective-permute-start.62 = (f32[2,384]{1,0:T(2,128)S(1)}, f32[2,384]{1,0:T(2,128)S(1)}, u32[]{:S(2)}, u32[]{:S(2)}) collective-permute-start(f32[2,384]{1,0:T(2,128)S(1)} %bitcast.173), channel_id=1, source_target_pairs={{0,1},{1,0},{2,3},{3,2},{4,5},{5,4},{6,7},{7,6},{8,9},{9,8},{10,11... | collective-permute-start | bytes 9224 | tf_op jit(solution)/shard_map/ppermute | solution.py:431
  431.3 12.2 %collective-permute-done.45 = bf16[512,256]{1,0:T(8,128)(2,1)} collective-permute-done((bf16[512,256]{1,0:T(8,128)(2,1)}, bf16[512,256]{1,0:T(8,128)(2,1)}, u32[]{:S(2)}, u32[]{:S(2)}) %collective-permute-start.45) | collective-permute-done | bytes 262176 | tf_op jit(solution)/shard_map/ppermute | solution.py:431
  462.0 21.6 %collective-permute-done.51 = bf16[512,256]{0,1:T(8,128)(2,1)} collective-permute-done((bf16[512,256]{0,1:T(8,128)(2,1)}, bf16[512,256]{0,1:T(8,128)(2,1)}, u32[]{:S(2)}, u32[]{:S(2)}) %collective-permute-start.51) | collective-permute-done | bytes 262176 | tf_op jit(solution)/shard_map/ppermute | solution.py:431
  (412 shorter events, 183.7 us)
Async XLA Ops:
  4.9 33.6 %collective-permute-start = (bf16[288,1024]{1,0:T(8,128)(2,1)}, bf16[288,1024]{1,0:T(8,128)(2,1)S(1)}, u32[]{:S(2)}, u32[]{:S(2)}) collective-permute-start(bf16[288,1024]{1,0:T(8,128)(2,1)} %multiply_convert_fusion.1), channel_id=1, source_target_pairs={{0,0},{1,8},{2,12},{3,4},{4,3},{5,11},{6,15},{7,7},{8,1},{9,9},{10... | collective-permute-start | bytes 1769480 | tf_op jit(solution)/shard_map/ppermute | solution.py:381
  7.2 31.3 %collective-permute-start.1 = (f32[2,288]{1,0:T(2,128)}, f32[2,288]{1,0:T(2,128)S(1)}, u32[]{:S(2)}, u32[]{:S(2)}) collective-permute-start(f32[2,288]{1,0:T(2,128)} %pad_maximum_fusion.24), channel_id=1, source_target_pairs={{0,0},{1,8},{2,12},{3,4},{4,3},{5,11},{6,15},{7,7},{8,1},{9,9},{10... | collective-permute-start | bytes 6920 | tf_op jit(solution)/shard_map/ppermute | solution.py:381
  8.6 30.0 %collective-permute-start.2 = (s32[1152]{0:T(1024)}, s32[1152]{0:T(1024)S(1)}, u32[]{:S(2)}, u32[]{:S(2)}) collective-permute-start(s32[1152]{0:T(1024)} %param.19), channel_id=1, source_target_pairs={{0,0},{1,8},{2,12},{3,4},{4,3},{5,11},{6,15},{7,7},{8,1},{9,9},{10... | collective-permute-start | bytes 13832 | tf_op jit(solution)/shard_map/ppermute | solution.py:381
  10.8 23.2 %all-to-all-start = ((f32[32,1,384]{2,1,0:T(1,128)}), f32[32,1,384]{2,1,0:T(1,128)S(1)}, u32[]{:S(2)}, u32[]{:S(2)}) async-start(f32[32,1,384]{2,1,0:T(1,128)} %broadcast_in_dim.43), calls=%async_computation | async-start | bytes 98304 | tf_op jit(solution)/shard_map/all_to_all | solution.py:230
  38.7 24.1 %collective-permute-start.7 = (bf16[288,1024]{1,0:T(8,128)(2,1)S(1)}, bf16[288,1024]{1,0:T(8,128)(2,1)}, u32[]{:S(2)}, u32[]{:S(2)}) collective-permute-start(bf16[288,1024]{1,0:T(8,128)(2,1)S(1)} %fusion.7), channel_id=1, source_target_pairs={{0,8},{4,12},{8,0},{12,4},{16,24},{20,28},{24,16},{28,20},{1,9},{5... | collective-permute-start | bytes 1769480 | tf_op jit(solution)/shard_map/ppermute | solution.py:377
  42.0 31.1 %collective-permute-start.3 = (bf16[288,1024]{1,0:T(8,128)(2,1)S(1)}, bf16[288,1024]{1,0:T(8,128)(2,1)}, u32[]{:S(2)}, u32[]{:S(2)}) collective-permute-start(bf16[288,1024]{1,0:T(8,128)(2,1)S(1)} %fusion.7), channel_id=1, source_target_pairs={{0,4},{4,0},{8,12},{12,8},{16,20},{20,16},{24,28},{28,24},{1,5},{5... | collective-permute-start | bytes 1769480 | tf_op jit(solution)/shard_map/ppermute | solution.py:377
  51.6 21.4 %collective-permute-start.5 = (bf16[512,256]{1,0:T(8,128)(2,1)S(1)}, bf16[512,256]{1,0:T(8,128)(2,1)S(1)}, u32[]{:S(2)}, u32[]{:S(2)}) collective-permute-start(bf16[512,256]{1,0:T(8,128)(2,1)S(1)} %get-tuple-element.247.refs_1_), channel_id=1, source_target_pairs={{0,2},{1,3},{2,0},{3,1},{4,6},{5,7},{6,4},{7,5},{8,10},{9,11},{10,... | collective-permute-start | bytes 786440 | tf_op jit(solution)/shard_map/ppermute | solution.py:431
  62.8 32.0 %collective-permute-start.8 = (bf16[288,1024]{1,0:T(8,128)(2,1)}, bf16[288,1024]{1,0:T(8,128)(2,1)}, u32[]{:S(2)}, u32[]{:S(2)}) collective-permute-start(bf16[288,1024]{1,0:T(8,128)(2,1)} %collective-permute-done.7), channel_id=1, source_target_pairs={{0,4},{4,0},{8,12},{12,8},{16,20},{20,16},{24,28},{28,24},{1,5},{5... | collective-permute-start | bytes 1769480 | tf_op jit(solution)/shard_map/ppermute | solution.py:377
  115.8 19.1 %collective-permute-start.13 = (bf16[576,1024]{1,0:T(8,128)(2,1)}, bf16[576,1024]{1,0:T(8,128)(2,1)}, u32[]{:S(2)}, u32[]{:S(2)}) collective-permute-start(bf16[576,1024]{1,0:T(8,128)(2,1)} %pad_maximum_fusion.6), channel_id=1, source_target_pairs={{0,4},{4,0},{8,12},{12,8},{16,20},{20,16},{24,28},{28,24},{1,5},{5... | collective-permute-start | bytes 3538952 | tf_op jit(solution)/shard_map/ppermute | solution.py:377
  119.4 88.2 %collective-permute-start.19 = (bf16[288,1024]{1,0:T(8,128)(2,1)}, bf16[288,1024]{1,0:T(8,128)(2,1)S(1)}, u32[]{:S(2)}, u32[]{:S(2)}) collective-permute-start(bf16[288,1024]{1,0:T(8,128)(2,1)} %get-tuple-element.97), channel_id=1, source_target_pairs={{0,0},{1,8},{2,12},{3,4},{4,3},{5,11},{6,15},{7,7},{8,1},{9,9},{10... | collective-permute-start | bytes 1769480 | tf_op jit(solution)/shard_map/ppermute | solution.py:381
  122.1 57.3 %collective-permute-start.14 = (bf16[512,512]{1,0:T(8,128)(2,1)}, bf16[512,512]{1,0:T(8,128)(2,1)S(1)}, u32[]{:S(2)}, u32[]{:S(2)}) collective-permute-start(bf16[512,512]{1,0:T(8,128)(2,1)} %slice.383), channel_id=1, source_target_pairs={{0,1},{1,0},{2,3},{3,2},{4,5},{5,4},{6,7},{7,6},{8,9},{9,8},{10,11... | collective-permute-start | bytes 1572872 | tf_op jit(solution)/shard_map/ppermute | solution.py:431
  126.0 53.3 %collective-permute-start.15 = (bf16[512,512]{1,0:T(8,128)(2,1)}, bf16[512,512]{1,0:T(8,128)(2,1)S(1)}, u32[]{:S(2)}, u32[]{:S(2)}) collective-permute-start(bf16[512,512]{1,0:T(8,128)(2,1)} %slice.383), channel_id=1, source_target_pairs={{0,2},{1,3},{2,0},{3,1},{4,6},{5,7},{6,4},{7,5},{8,10},{9,11},{10,... | collective-permute-start | bytes 1572872 | tf_op jit(solution)/shard_map/ppermute | solution.py:431
  131.3 48.0 %collective-permute-start.16 = (bf16[512,512]{1,0:T(8,128)(2,1)}, bf16[512,512]{1,0:T(8,128)(2,1)S(1)}, u32[]{:S(2)}, u32[]{:S(2)}) collective-permute-start(bf16[512,512]{1,0:T(8,128)(2,1)} %slice.383), channel_id=1, source_target_pairs={{0,3},{1,2},{2,1},{3,0},{4,7},{5,6},{6,5},{7,4},{8,11},{9,10},{10,... | collective-permute-start | bytes 1572872 | tf_op jit(solution)/shard_map/ppermute | solution.py:431
  181.8 20.1 %collective-permute-start.24 = (bf16[512,512]{1,0:T(8,128)(2,1)S(1)}, bf16[512,512]{1,0:T(8,128)(2,1)S(1)}, u32[]{:S(2)}, u32[]{:S(2)}) collective-permute-start(bf16[512,512]{1,0:T(8,128)(2,1)S(1)} %collective-permute-done.15), channel_id=1, source_target_pairs={{0,16},{4,20},{8,24},{12,28},{16,0},{20,4},{24,8},{28,12},{1,17},{... | collective-permute-start | bytes 1572872 | tf_op jit(solution)/shard_map/ppermute | solution.py:377
  182.4 25.1 %collective-permute-start.23 = (bf16[512,512]{1,0:T(8,128)(2,1)S(1)}, bf16[512,512]{1,0:T(8,128)(2,1)S(1)}, u32[]{:S(2)}, u32[]{:S(2)}) collective-permute-start(bf16[512,512]{1,0:T(8,128)(2,1)S(1)} %collective-permute-done.14), channel_id=1, source_target_pairs={{0,16},{4,20},{8,24},{12,28},{16,0},{20,4},{24,8},{28,12},{1,17},{... | collective-permute-start | bytes 1572872 | tf_op jit(solution)/shard_map/ppermute | solution.py:377
  207.5 18.7 %collective-permute-start.20 = (bf16[288,1024]{1,0:T(8,128)(2,1)S(1)}, bf16[288,1024]{1,0:T(8,128)(2,1)S(1)}, u32[]{:S(2)}, u32[]{:S(2)}) collective-permute-start(bf16[288,1024]{1,0:T(8,128)(2,1)S(1)} %add_convert_fusion.7), channel_id=1, source_target_pairs={{0,4},{4,0},{8,12},{12,8},{16,20},{20,16},{24,28},{28,24},{1,5},{5... | collective-permute-start | bytes 1769480 | tf_op jit(solution)/shard_map/ppermute | solution.py:377
  207.6 18.6 %collective-permute-start.27 = (bf16[288,1024]{1,0:T(8,128)(2,1)S(1)}, bf16[288,1024]{1,0:T(8,128)(2,1)S(1)}, u32[]{:S(2)}, u32[]{:S(2)}) collective-permute-start(bf16[288,1024]{1,0:T(8,128)(2,1)S(1)} %collective-permute-done.19), channel_id=1, source_target_pairs={{0,8},{4,12},{8,0},{12,4},{16,24},{20,28},{24,16},{28,20},{1,9},{5... | collective-permute-start | bytes 1769480 | tf_op jit(solution)/shard_map/ppermute | solution.py:377
  255.5 25.3 %collective-permute-start.31 = (bf16[288,1024]{1,0:T(8,128)(2,1)S(1)}, bf16[288,1024]{1,0:T(8,128)(2,1)S(1)}, u32[]{:S(2)}, u32[]{:S(2)}) collective-permute-start(bf16[288,1024]{1,0:T(8,128)(2,1)S(1)} %add_convert_fusion.5), channel_id=1, source_target_pairs={{0,8},{4,12},{8,0},{12,4},{16,24},{20,28},{24,16},{28,20},{1,9},{5... | collective-permute-start | bytes 1769480 | tf_op jit(solution)/shard_map/ppermute | solution.py:377
  286.5 24.5 %collective-permute-start.34 = (bf16[512,1024]{1,0:T(8,128)(2,1)S(1)}, bf16[512,1024]{1,0:T(8,128)(2,1)S(1)}, u32[]{:S(2)}, u32[]{:S(2)}) collective-permute-start(bf16[512,1024]{1,0:T(8,128)(2,1)S(1)} %broadcast_select_fusion.1), channel_id=1, source_target_pairs={{0,16},{4,20},{8,24},{12,28},{16,0},{20,4},{24,8},{28,12},{1,17},{... | collective-permute-start | bytes 3145736 | tf_op jit(solution)/shard_map/ppermute | solution.py:377
  288.1 22.9 %collective-permute-start.33 = (bf16[288,1024]{1,0:T(8,128)(2,1)S(1)}, bf16[288,1024]{1,0:T(8,128)(2,1)S(1)}, u32[]{:S(2)}, u32[]{:S(2)}) collective-permute-start(bf16[288,1024]{1,0:T(8,128)(2,1)S(1)} %convert_element_type.272), channel_id=1, source_target_pairs={{0,4},{4,0},{8,12},{12,8},{16,20},{20,16},{24,28},{28,24},{1,5},{5... | collective-permute-start | bytes 1769480 | tf_op jit(solution)/shard_map/ppermute | solution.py:377
  333.7 22.1 %collective-permute-start.37 = (bf16[576,1024]{1,0:T(8,128)(2,1)}, bf16[576,1024]{1,0:T(8,128)(2,1)}, u32[]{:S(2)}, u32[]{:S(2)}) collective-permute-start(bf16[576,1024]{1,0:T(8,128)(2,1)} %pad_maximum_fusion.9), channel_id=1, source_target_pairs={{0,4},{4,0},{8,12},{12,8},{16,20},{20,16},{24,28},{28,24},{1,5},{5... | collective-permute-start | bytes 3538952 | tf_op jit(solution)/shard_map/ppermute | solution.py:377
  333.9 30.3 %collective-permute-start.38 = (bf16[512,1024]{1,0:T(8,128)(2,1)}, bf16[512,1024]{1,0:T(8,128)(2,1)}, u32[]{:S(2)}, u32[]{:S(2)}) collective-permute-start(bf16[512,1024]{1,0:T(8,128)(2,1)} %get-tuple-element.223), channel_id=1, source_target_pairs={{0,16},{4,20},{8,24},{12,28},{16,0},{20,4},{24,8},{28,12},{1,17},{... | collective-permute-start | bytes 3145736 | tf_op jit(solution)/shard_map/ppermute | solution.py:377
  338.7 82.2 %collective-permute-start.47 = (bf16[512,256]{1,0:T(8,128)(2,1)}, bf16[512,256]{1,0:T(8,128)(2,1)}, u32[]{:S(2)}, u32[]{:S(2)}) collective-permute-start(bf16[512,256]{1,0:T(8,128)(2,1)} %get-tuple-element.239), channel_id=1, source_target_pairs={{0,1},{1,0},{2,3},{3,2},{4,5},{5,4},{6,7},{7,6},{8,9},{9,8},{10,11... | collective-permute-start | bytes 786440 | tf_op jit(solution)/shard_map/ppermute | solution.py:431
  349.5 72.0 %collective-permute-start.48 = (bf16[512,256]{1,0:T(8,128)(2,1)}, bf16[512,256]{1,0:T(8,128)(2,1)}, u32[]{:S(2)}, u32[]{:S(2)}) collective-permute-start(bf16[512,256]{1,0:T(8,128)(2,1)} %get-tuple-element.238), channel_id=1, source_target_pairs={{0,2},{1,3},{2,0},{3,1},{4,6},{5,7},{6,4},{7,5},{8,10},{9,11},{10,... | collective-permute-start | bytes 786440 | tf_op jit(solution)/shard_map/ppermute | solution.py:431
  350.5 72.0 %collective-permute-start.49 = (bf16[512,256]{1,0:T(8,128)(2,1)}, bf16[512,256]{1,0:T(8,128)(2,1)}, u32[]{:S(2)}, u32[]{:S(2)}) collective-permute-start(bf16[512,256]{1,0:T(8,128)(2,1)} %get-tuple-element.237), channel_id=1, source_target_pairs={{0,3},{1,2},{2,1},{3,0},{4,7},{5,6},{6,5},{7,4},{8,11},{9,10},{10,... | collective-permute-start | bytes 786440 | tf_op jit(solution)/shard_map/ppermute | solution.py:431
  355.8 26.9 %collective-permute-start.40 = (bf16[288,1024]{1,0:T(8,128)(2,1)}, bf16[288,1024]{1,0:T(8,128)(2,1)}, u32[]{:S(2)}, u32[]{:S(2)}) collective-permute-start(bf16[288,1024]{1,0:T(8,128)(2,1)} %add_convert_fusion.4), channel_id=1, source_target_pairs={{0,0},{8,1},{12,2},{4,3},{3,4},{11,5},{15,6},{7,7},{1,8},{9,9},{13... | collective-permute-start | bytes 1769480 | tf_op jit(solution)/shard_map/ppermute | solution.py:385
  380.5 63.0 %collective-permute-start.42 = (bf16[512,768]{1,0:T(8,128)(2,1)}, bf16[512,768]{1,0:T(8,128)(2,1)}, u32[]{:S(2)}, u32[]{:S(2)}) collective-permute-start(bf16[512,768]{1,0:T(8,128)(2,1)} %broadcast_select_fusion.7), channel_id=1, source_target_pairs={{0,16},{4,20},{8,24},{12,28},{16,0},{20,4},{24,8},{28,12},{1,17},{... | collective-permute-start | bytes 2359304 | tf_op jit(solution)/shard_map/ppermute | solution.py:377
  398.2 19.4 %collective-permute-start.62 = (f32[2,384]{1,0:T(2,128)S(1)}, f32[2,384]{1,0:T(2,128)S(1)}, u32[]{:S(2)}, u32[]{:S(2)}) collective-permute-start(f32[2,384]{1,0:T(2,128)S(1)} %bitcast.173), channel_id=1, source_target_pairs={{0,1},{1,0},{2,3},{3,2},{4,5},{5,4},{6,7},{7,6},{8,9},{9,8},{10,11... | collective-permute-start | bytes 9224 | tf_op jit(solution)/shard_map/ppermute | solution.py:431
  422.5 21.0 %collective-permute-start.45 = (bf16[512,256]{1,0:T(8,128)(2,1)}, bf16[512,256]{1,0:T(8,128)(2,1)}, u32[]{:S(2)}, u32[]{:S(2)}) collective-permute-start(bf16[512,256]{1,0:T(8,128)(2,1)} %get-tuple-element.242), channel_id=1, source_target_pairs={{0,2},{1,3},{2,0},{3,1},{4,6},{5,7},{6,4},{7,5},{8,10},{9,11},{10,... | collective-permute-start | bytes 786440 | tf_op jit(solution)/shard_map/ppermute | solution.py:431
  452.3 31.3 %collective-permute-start.51 = (bf16[512,256]{0,1:T(8,128)(2,1)}, bf16[512,256]{0,1:T(8,128)(2,1)}, u32[]{:S(2)}, u32[]{:S(2)}) collective-permute-start(bf16[512,256]{0,1:T(8,128)(2,1)} %bitcast.27), channel_id=1, source_target_pairs={{0,2},{1,3},{2,0},{3,1},{4,6},{5,7},{6,4},{7,5},{8,10},{9,11},{10,... | collective-permute-start | bytes 786440 | tf_op jit(solution)/shard_map/ppermute | solution.py:431
  455.2 28.4 %collective-permute-start.50 = (bf16[512,256]{0,1:T(8,128)(2,1)}, bf16[512,256]{0,1:T(8,128)(2,1)}, u32[]{:S(2)}, u32[]{:S(2)}) collective-permute-start(bf16[512,256]{0,1:T(8,128)(2,1)} %bitcast.26), channel_id=1, source_target_pairs={{0,1},{1,0},{2,3},{3,2},{4,5},{5,4},{6,7},{7,6},{8,9},{9,8},{10,11... | collective-permute-start | bytes 786440 | tf_op jit(solution)/shard_map/ppermute | solution.py:431
  460.5 34.2 %collective-permute-start.41 = (bf16[288,1024]{1,0:T(8,128)(2,1)S(1)}, bf16[288,1024]{1,0:T(8,128)(2,1)S(1)}, u32[]{:S(2)}, u32[]{:S(2)}) collective-permute-start(bf16[288,1024]{1,0:T(8,128)(2,1)S(1)} %copy-done.22), channel_id=1, source_target_pairs={{0,0},{8,1},{12,2},{4,3},{3,4},{11,5},{15,6},{7,7},{1,8},{9,9},{13... | collective-permute-start | bytes 1769480 | tf_op jit(solution)/shard_map/ppermute | solution.py:385
  (94 other events, 1186.4 us)
